TPU v7x, 256 devices: a whole 4x4x8 slice. The times are simulated.
256 devices in a mesh: ctx: 64 (over z, y, core), tp: 4 (over x).
Axes of the slice: x: 4, y: 4, z: 8, core: 2. Of those that a mesh axis runs over, the one named last changes fastest.
Arguments:
- projected: bfloat16 [8192, 4, 4640], P('ctx', 'tp'), may hold values from -6 to 6
- conv_weight: float32 [4, 4, 2560], P('tp'), may hold values from -3 to 3
- conv_bias: float32 [4, 2560], P('tp'), may hold values from -1.5 to 1.5
- step_bias: float32 [4, 32], P('tp'), may hold values from -1 to 0.5
- log_rates: float32 [4, 32], P('tp'), as said below
- norm_gain: float32 [4, 2048], P('tp'), may hold values from 0.1 to 1.9
- out_weight: bfloat16 [4, 2048, 4096], P('tp', 'ctx'), may hold values from -0.0625 to 0.0625
Outputs:
- mixed: bfloat16 [8192, 4096], P('ctx', 'tp')
Inputs may be any that keep to these rules, and one draw needn't show every extreme that they name: log_rates lies between log(0.3 / 8192) and log(1 / 25).
All inputs are finite; a program needn't handle non-finite values.
Results may differ from a plain program's by a relative error of at most 0.0058.
Values may be sent and summed in bfloat16 or wider, within the bound.
No kernel may reach another device: no remote copies, remote signals or barrier semaphores. Data moves between devices by JAX's collectives and lax.ppermute only.
A program may use at most 320 MiB of HBM per device.

v0:
```python
import jax
import jax.numpy as jnp
import numpy as np
from jax import lax
from jax.sharding import PartitionSpec as P

P_SIZE = 64
N = 256
KCONV = 4
SPAN = 128
GCH = 2048
GCONV = 2560


highest_precision = lax.Precision.HIGHEST


def from_behind(shard, axis, by):
    peers = lax.axis_size(axis)
    pairs = [(i, i + by) for i in range(peers) if 0 <= i + by < peers]
    return lax.ppermute(shard, axis, pairs)


def ssd_blocks(inputs_x, step_sizes, decay_rate, b_keys, c_keys, block_rows):
    row_count = inputs_x.shape[0]
    block_count = row_count // block_rows
    head_count = inputs_x.shape[1]
    head_width = inputs_x.shape[2]
    state_count = b_keys.shape[1]
    x_blocks = inputs_x.reshape(block_count, block_rows, head_count, head_width)
    step_blocks = step_sizes.reshape(block_count, block_rows, head_count)
    b_blocks = b_keys.reshape(block_count, block_rows, state_count)
    c_blocks = c_keys.reshape(block_count, block_rows, state_count)
    causal_mask = (jnp.arange(block_rows)[:, None] >= jnp.arange(block_rows)[None, :])[None]

    def advance(carried, pieces):
        x_block, step_block, b_block, c_block = pieces
        log_steps = step_block * decay_rate[None, :]
        running = jnp.cumsum(log_steps, axis=0)
        intersection = jnp.dot(c_block, b_block.T, preferred_element_type=jnp.float32)
        b_float = b_block.astype(jnp.float32)
        c_float = c_block.astype(jnp.float32)
        log_gaps = running.T[:, :, None] - running.T[:, None, :]
        factors = jnp.where(causal_mask, jnp.exp(jnp.where(causal_mask, log_gaps, 0.0)), 0.0)
        factors = factors * intersection[None] * step_block.T[:, None, :]
        within = jnp.einsum("hts,shp->thp", factors, x_block, precision=highest_precision)
        carried_part = (
            jnp.einsum("tn,hpn->thp", c_float, carried, precision=highest_precision)
            * jnp.exp(running)[:, :, None]
        )
        tail_weight = jnp.exp(running[-1][None, :] - running) * step_block
        weighted = x_block * tail_weight[:, :, None]
        updated = carried * jnp.exp(running[-1])[:, None, None] + jnp.einsum(
            "shp,sn->hpn", weighted, b_float, precision=highest_precision
        )
        return (updated, within + carried_part)

    initial = jnp.zeros((head_count, head_width, state_count), jnp.float32)
    final_state, outputs = lax.scan(advance, initial, (x_blocks, step_blocks, b_blocks, c_blocks))
    total_log = jnp.sum(step_sizes * decay_rate[None, :], axis=0)
    return (outputs.reshape(row_count, head_count, head_width), final_state, total_log)


def on_device(projected, conv_weight, conv_bias, step_bias, log_rates, norm_gain, out_weight):
    row_count = projected.shape[0]
    conv_input = projected[:, :, GCH : GCH + GCONV]
    rim_rows = from_behind(conv_input[row_count - (KCONV - 1) :], "ctx", 1)
    padded = jnp.concatenate([rim_rows, conv_input], axis=0).astype(jnp.float32)
    mixed_conv = conv_bias[None]
    for offset in range(KCONV):
        mixed_conv = mixed_conv + conv_weight[:, offset][None] * padded[offset : offset + row_count]
    activated = jax.nn.silu(mixed_conv).astype(jnp.bfloat16)
    values = activated[:, :, :GCH]
    key_rows = activated[:, :, GCH:]
    raw_steps = projected[:, :, GCH + GCONV :]
    decay_rate = -jnp.exp(log_rates)
    devices = lax.axis_size("ctx")
    shard_width = GCH // devices
    shard_heads = max(1, shard_width // P_SIZE)
    piece_width = shard_width // shard_heads
    head_table = (
        np.arange(devices)[:, None] * shard_width // P_SIZE + np.arange(shard_heads)[None, :]
    ).reshape(-1)
    spread_steps = jnp.take(raw_steps, jnp.asarray(head_table, jnp.int32), axis=2)
    local_values, local_steps = (
        lax.all_to_all(values, "ctx", split_axis=2, concat_axis=0, tiled=True),
        lax.all_to_all(spread_steps, "ctx", split_axis=2, concat_axis=0, tiled=True),
    )
    all_keys = lax.all_gather(key_rows, "ctx", axis=0, tiled=True)
    sequence = local_values.shape[0]
    first_head = lax.axis_index("ctx") * shard_width // P_SIZE
    bias_slice = lax.dynamic_slice_in_dim(step_bias[0], first_head, shard_heads)
    rate_slice = lax.dynamic_slice_in_dim(decay_rate[0], first_head, shard_heads)
    step_sizes = jax.nn.softplus(local_steps[:, 0].astype(jnp.float32) + bias_slice[None, :])
    outputs, final_state, total_log = ssd_blocks(
        local_values[:, 0].astype(jnp.float32).reshape(sequence, shard_heads, piece_width),
        step_sizes,
        rate_slice,
        all_keys[:, 0, :N],
        all_keys[:, 0, N:],
        4 * SPAN,
    )
    pieces_out = [outputs.reshape(sequence, shard_width).astype(jnp.bfloat16)]
    scanned = lax.all_to_all(
        jnp.stack(pieces_out, axis=1), "ctx", split_axis=0, concat_axis=2, tiled=True
    )
    gated = scanned.astype(jnp.float32) * jax.nn.silu(projected[:, :, :GCH].astype(jnp.float32))
    normed = (
        gated * lax.rsqrt(jnp.mean(gated * gated, axis=2, keepdims=True) + 1e-05) * norm_gain[None]
    ).astype(jnp.bfloat16)
    summed = jnp.einsum(
        "tgr,grd->td",
        normed,
        lax.all_gather(out_weight, "ctx", axis=1, tiled=True),
        preferred_element_type=jnp.float32,
    )
    shares = lax.psum_scatter(summed, "tp", scatter_dimension=1, tiled=True)
    return shares.astype(jnp.bfloat16)


def solution(mesh):
    return jax.shard_map(
        on_device,
        mesh=mesh,
        in_specs=(
            P("ctx", "tp", None),
            P("tp", None, None),
            P("tp", None),
            P("tp", None),
            P("tp", None),
            P("tp", None),
            P("tp", "ctx", None),
        ),
        out_specs=P("ctx", "tp"),
        check_vma=False,
    )
```

profile of v0, /device:TPU:1, one launch (start us, length us, event | category | flops | bytes accessed | tf_op | source)
XLA Modules:
  0.0 387.9 jit_solution(16653090227472884516)
XLA Ops:
  8.2 4.7 %collective-permute-start = (bf16[3,1,2560]{2,0,1:T(4,128)(2,1)S(1)}, bf16[3,1,2560]{2,0,1:T(4,128)(2,1)S(1)}, u32[]{:S(2)}, u32[]{:S(2)}) collective-permute-start(bf16[3,1,2560]{2,0,1:T(4,128)(2,1)S(1)} %copy.77), channel_id=1, source_target_pairs={{0,4},{4,8},{8,12},{12,16},{16,20},{20,24},{24,28},{28,32},{32,36}... | collective-permute-start | bytes 46088 | tf_op jit(solution)/shard_map/ppermute | solution.py:21
  16.9 13.5 %all-to-all-start = ((bf16[128,1,64]{0,1,2:T(2,128)(2,1)}), bf16[128,1,64]{0,1,2:T(2,128)(2,1)S(1)}, u32[]{:S(2)}, u32[]{:S(2)}) async-start(bf16[128,1,64]{0,1,2:T(2,128)(2,1)} %copy.66), calls=%async_computation | async-start | bytes 65536 | tf_op jit(solution)/shard_map/all_to_all | solution.py:87
  31.7 11.5 %reduce.12 = bf16[2048,128]{1,0:T(8,128)(2,1)S(1)} reduce(bf16[2048,1,128]{2,1,0:T(2,128)(2,1)S(1)} %bitcast.163, bf16[]{:T(256)} %broadcast.159), dimensions={1}, to_apply=%bitcast.98.reduce_sub_computation | reduce | bytes 1048578
  44.2 10.3 %all-to-all-start.1 = ((bf16[64,2,2048]{2,1,0:T(2,128)(2,1)}), bf16[64,2,2048]{2,1,0:T(2,128)(2,1)S(1)}, u32[]{:S(2)}, u32[]{:S(2)}) async-start(bf16[64,2,2048]{2,1,0:T(2,128)(2,1)} %reshape.445), calls=%async_computation.1 | async-start | bytes 1048576 | tf_op jit(solution)/shard_map/all_to_all | solution.py:86
  57.5 14.9 %all-to-all-done.1 = bf16[64,2,2048]{2,1,0:T(2,128)(2,1)S(1)} async-done(((bf16[64,2,2048]{2,1,0:T(2,128)(2,1)}), bf16[64,2,2048]{2,1,0:T(2,128)(2,1)S(1)}, u32[]{:S(2)}, u32[]{:S(2)}) %all-to-all-start.1) | async-done | bytes 524320 | tf_op jit(solution)/shard_map/all_to_all | solution.py:86
  74.1 2.7 copy.70
  76.8 26.9 %all-gather.3.cloned.1.call-done = bf16[8192,1,512]{2,0,1:T(8,128)(2,1)} async-done(((bf16[128,1,512]{2,0,1:T(8,128)(2,1)}), bf16[8192,1,512]{2,0,1:T(8,128)(2,1)}) %all-gather.3.cloned.1.call-update) | async-done | bytes 8388624 | tf_op jit(solution)/shard_map/all_gather | solution.py:89
  103.7 5.9 %fusion.41 = (bf16[8192,1,256]{2,0,1:T(8,128)(2,1)}, bf16[8192,1,256]{2,0,1:T(8,128)(2,1)}) fusion(bf16[8192,1,512]{2,0,1:T(8,128)(2,1)} %all-gather.3.cloned.1.call-done), kind=kLoop, calls=%fused_computation.76 | loop fusion | bytes 16777216 | tf_op jit(solution)/shard_map/slice | solution.py:100
  109.6 184.8 %while.14 = (s32[]{:T(128)}, f32[1,32,256]{2,1,0:T(8,128)S(1)}, bf16[16,512,1,32]{1,3,2,0:T(8,128)(2,1)S(1)}, f32[16,512,1]{1,0,2:T(8,128)S(1)}, f32[1]{0:T(128)...) while((s32[]{:T(128)}, f32[1,32,256]{2,1,0:T(8,128)S(1)}, ...), condition=%wide.region_3.4_spmd.clone.clone, body=%wide.region_0.0_spmd.clone.clone.sunk | while | flops 337266176 | bytes 4002620 | solution.py:59
  113.5 2.4 broadcast_multiply_fusion.2
  125.0 2.4 broadcast_multiply_fusion.2
  136.5 2.4 broadcast_multiply_fusion.2
  148.1 2.4 broadcast_multiply_fusion.2
  159.7 2.5 broadcast_multiply_fusion.2
  171.3 2.4 broadcast_multiply_fusion.2
  182.8 2.4 broadcast_multiply_fusion.2
  194.4 2.4 broadcast_multiply_fusion.2
  206.0 2.4 broadcast_multiply_fusion.2
  217.5 2.4 broadcast_multiply_fusion.2
  229.1 2.4 broadcast_multiply_fusion.2
  240.6 2.4 broadcast_multiply_fusion.2
  252.1 2.4 broadcast_multiply_fusion.2
  263.7 2.4 broadcast_multiply_fusion.2
  275.2 2.4 broadcast_multiply_fusion.2
  286.7 2.4 broadcast_multiply_fusion.2
  296.0 1.9 copy.81
  298.0 2.8 reshape.447
  300.8 23.8 %all_to_all.12 = bf16[64,2,2048]{2,1,0:T(2,128)(2,1)S(1)} all-to-all(bf16[64,2,2048]{2,1,0:T(2,128)(2,1)} %reshape.447), channel_id=1, replica_groups=mesh['ctx'=64,'tp'=4] {'ctx'}, dimensions={0} | all-to-all | bytes 1048576 | tf_op jit(solution)/shard_map/all_to_all | solution.py:104
  324.6 7.1 %reshape.448 = bf16[8192,1,32]{2,1,0:T(2,128)(2,1)} reshape(bf16[64,2,2048]{2,1,0:T(2,128)(2,1)S(1)} %all_to_all.12) | data formatting | bytes 1048576
  331.8 8.0 %copy.74 = bf16[8192,1,32]{0,2,1:T(8,128)(2,1)S(1)} copy(bf16[8192,1,32]{2,1,0:T(2,128)(2,1)} %reshape.448) | data formatting | bytes 1048576 | tf_op jit(solution)/shard_map/all_to_all | solution.py:104
  341.3 9.6 %fusion.25 = f32[128,4096]{1,0:T(8,128)} fusion(bf16[1,2048,4096]{2,1,0:T(8,128)(2,1)} %all-gather.5.cloned.1.call-done, f32[128,1,2048]{0,2,1:T(8,128)S(1)} %get-tuple-element.150, f32[2048]{0:T(1024)S(1)} %bitcast.173, f32[128]{0:T(128)S(1)} %add_rsqrt_fusion), kind=kOutput, calls=%fused_computation.38 | convolution fusion | flops 2148270080 | bytes 19931648 | tf_op jit(solution)/shard_map/tgr,grd->td/dot_general | solution.py:111
  350.9 28.7 %reduce-scatter.2.cloned.1.call-done = f32[128,1024]{1,0:T(8,128)} async-done(((f32[128,4096]{1,0:T(8,128)}), f32[128,1024]{1,0:T(8,128)}) %reduce-scatter.2.cloned.1.call-update) | async-done | bytes 524304 | tf_op jit(solution)/shard_map/reduce_scatter | solution.py:117
  (287 shorter events, 141.2 us)
Async XLA Ops:
  6.5 49.0 %copy-start = (f32[1,32]{1,0:T(1,128)S(1)}, f32[1,32]{1,0:T(1,128)}, u32[]{:S(2)}) copy-start(f32[1,32]{1,0:T(1,128)} %param.13) | copy-start | bytes 388
  6.5 6.4 %copy-start.5 = (f32[1,4,2560]{2,1,0:T(4,128)S(1)}, f32[1,4,2560]{2,1,0:T(4,128)}, u32[]{:S(2)}) copy-start(f32[1,4,2560]{2,1,0:T(4,128)} %param.11) | copy-start | bytes 122884
  6.5 6.5 %slice-start = ((bf16[128,1,4640]{0,2,1:T(8,128)(2,1)}), bf16[128,1,2560]{0,2,1:T(8,128)(2,1)S(1)}, s32[]{:S(2)}) async-start(bf16[128,1,4640]{0,2,1:T(8,128)(2,1)} %param.10), calls=%async_computation.7 | async-start | bytes 1310720 | tf_op jit(solution)/shard_map/slice | solution.py:66
  6.5 97.2 %all-gather.3.cloned.1.call-start = ((), (), s32[]{:S(2)}) async-start(), calls=%async_computation.4 | async-start | bytes 8519680 | tf_op jit(solution)/shard_map/all_gather | solution.py:89
  8.2 5.1 %copy-start.6 = (f32[1,2560]{1,0:T(1,128)S(1)}, f32[1,2560]{1,0:T(1,128)}, u32[]{:S(2)}) copy-start(f32[1,2560]{1,0:T(1,128)} %param.12) | copy-start | bytes 30724
  8.2 5.6 %collective-permute-start = (bf16[3,1,2560]{2,0,1:T(4,128)(2,1)S(1)}, bf16[3,1,2560]{2,0,1:T(4,128)(2,1)S(1)}, u32[]{:S(2)}, u32[]{:S(2)}) collective-permute-start(bf16[3,1,2560]{2,0,1:T(4,128)(2,1)S(1)} %copy.77), channel_id=1, source_target_pairs={{0,4},{4,8},{8,12},{12,16},{16,20},{20,24},{24,28},{28,32},{32,36}... | collective-permute-start | bytes 46088 | tf_op jit(solution)/shard_map/ppermute | solution.py:21
  14.0 1.6 copy-start.7
  14.0 1.6 copy-start.2
  16.9 27.3 %all-to-all-start = ((bf16[128,1,64]{0,1,2:T(2,128)(2,1)}), bf16[128,1,64]{0,1,2:T(2,128)(2,1)S(1)}, u32[]{:S(2)}, u32[]{:S(2)}) async-start(bf16[128,1,64]{0,1,2:T(2,128)(2,1)} %copy.66), calls=%async_computation | async-start | bytes 65536 | tf_op jit(solution)/shard_map/all_to_all | solution.py:87
  43.2 13.0 %copy-start.8 = (f32[1,32]{1,0:T(1,128)S(1)}, f32[1,32]{1,0:T(1,128)}, u32[]{:S(2)}) copy-start(f32[1,32]{1,0:T(1,128)} %param.14) | copy-start | bytes 388
  44.2 28.2 %all-to-all-start.1 = ((bf16[64,2,2048]{2,1,0:T(2,128)(2,1)}), bf16[64,2,2048]{2,1,0:T(2,128)(2,1)S(1)}, u32[]{:S(2)}, u32[]{:S(2)}) async-start(bf16[64,2,2048]{2,1,0:T(2,128)(2,1)} %reshape.445), calls=%async_computation.1 | async-start | bytes 1048576 | tf_op jit(solution)/shard_map/all_to_all | solution.py:86
  54.5 286.5 %all-gather.5.cloned.1.call-start = ((), (), s32[]{:S(2)}) async-start(), calls=%async_computation.5 | async-start | bytes 17039360 | tf_op jit(solution)/shard_map/all_gather | solution.py:114
  55.3 324.3 %reduce-scatter.2.cloned.1.call-start = ((), (), s32[]{:S(2)}) async-start(), calls=%async_computation.6 | async-start | bytes 2621440 | tf_op jit(solution)/shard_map/reduce_scatter | solution.py:117
  76.8 32.8 %copy-start.3 = (bf16[16,512,1,32]{1,3,2,0:T(8,128)(2,1)S(1)}, bf16[16,512,1,32]{1,3,2,0:T(8,128)(2,1)}, u32[]{:S(2)}) copy-start(bf16[16,512,1,32]{1,3,2,0:T(8,128)(2,1)} %custom-call.3) | copy-start | bytes 1572868
  340.6 0.7 copy-start.4
  350.9 30.5 %copy-start.1 = (f32[1,32]{1,0:T(1,128)S(1)}, f32[1,32]{1,0:T(1,128)}, u32[]{:S(2)}) copy-start(f32[1,32]{1,0:T(1,128)} %param.13) | copy-start | bytes 388
Sparse Core Ops, SparseCore 0:
  15.7 87.9 all-gather.2
  106.5 97.1 all-gather.4
  351.1 28.4 reduce-scatter.1
where the time goes:
time: 391 us; the launch traced here: 388 us
  matrix products  91.8 us (23%)
  other arithmetic  75.4 us (19%)
  waiting for transfers between devices  71.7 us (18%)
  local copies, waits for them, and re-layouts  60.7 us (16%)
  starting transfers between devices  28.7 us (7%)
  blocking collectives  23.8 us (6%)
  loops' own time  22.3 us (6%)
  between operations  13.4 us (3%)
    mul x16, other arithmetic, advance(): weighted = x_block * tail_weight[:, :, None]  38.7 us
    reduce_scatter x1, waiting for transfers between devices, on_device(): shares = lax.psum_scatter(summed, 'tp', scatter_dimension=1, tiled=True)  28.7 us
    all_gather x1, waiting for transfers between devices, on_device(): all_keys = lax.all_gather(key_rows, 'ctx', axis=0, tiled=True)  26.9 us
    all_to_all x1, blocking collectives, on_device(): lax.all_to_all(jnp.stack(pieces_out, axis=1), 'ctx', split_axis=0, concat...  23.8 us
    another operation x1, loops' own time, ssd_blocks(): lax.scan(advance, initial, (x_blocks, step_blocks, b_blocks, c_blocks))  22.3 us
    dot_general x16, matrix products, advance(): jnp.dot(c_block, b_block.T, preferred_element_type=jnp.float32)  22 us
    dot_general x16, matrix products, advance(): jnp.einsum('shp,sn->hpn', weighted, b_float, precision=highest_precision)  21.3 us
    dot_general x16, matrix products, advance(): jnp.einsum('tn,hpn->thp', c_float, carried, precision=highest_precision)  20.8 us
  transfers between devices with their start and end apart: 6, of which 4 were waited for; matrix products, arithmetic and copies ran while one was open for 55% of the time, Pallas kernels for 0%

commit v1 on v0

v1 whole, which is shorter than its diff:
```python
import jax
import jax.numpy as jnp
from jax import lax
from jax.experimental import pallas as pl
from jax.experimental.pallas import tpu as pltpu
from jax.sharding import Mesh
from jax.sharding import PartitionSpec as P

P_SIZE = 64
N = 256
KCONV = 4
ROWS = 128
PAIR = 256
GCH = 2048
GCONV = 2560
GCOLS = 4640
HALF = 1024
HEADS = 16
BLOCK = 512
Z, Y, C, T = 8, 4, 2, 4
CHIPS = Z * Y
f32, bf16 = jnp.float32, jnp.bfloat16
MIB = 1 << 20


def params(mib):
    return pltpu.CompilerParams(vmem_limit_bytes=mib * MIB)


def vmem():
    return pl.BlockSpec(memory_space=pltpu.VMEM)


def smem():
    return pl.BlockSpec(memory_space=pltpu.SMEM)


def dot(a, b, ca=1, cb=0, precision=None):
    return lax.dot_general(
        a, b, (((ca,), (cb,)), ((), ())), precision=precision, preferred_element_type=f32
    )


def lanes(shape):
    return lax.broadcasted_iota(jnp.int32, shape, 1)


def split_three(v):
    v = jnp.where(lanes(v.shape) < HEADS, v, 0.0)
    high = v.astype(bf16).astype(f32)
    rest = v - high
    middle = rest.astype(bf16).astype(f32)
    low = (rest - middle).astype(bf16).astype(f32)
    packed = high + pltpu.roll(middle, HEADS, 1) + pltpu.roll(low, 2 * HEADS, 1)
    return packed.astype(bf16)


def head_table(first, width):
    row = lax.broadcasted_iota(jnp.int32, (128, width), 0)
    column = lax.broadcasted_iota(jnp.int32, (128, width), 1) + first
    hit = (row < 3 * HEADS) & ((row % HEADS) == column // P_SIZE)
    return jnp.where(hit, 1.0, 0.0).astype(bf16)


def scan_kernel(
    at, mine, other, rim, taps, bias, step_bias, log_rates,
    within, keys, growth, send,
    padded, tap_rows, values, queries, raw, small,
):
    core = at[0]
    x_at = pl.multiple_of(core * HALF, 128)
    mine_at = pl.multiple_of(core * ROWS, 128)
    other_at = pl.multiple_of((1 - core) * ROWS, 128)
    padded[0:8, 0:HALF] = rim[:, pl.ds(x_at, HALF)].astype(f32)
    padded[0:8, HALF:] = rim[:, GCH:GCONV].astype(f32)
    z_end = pl.multiple_of(GCH + x_at, 128)
    for rows, ref in ((mine_at, mine), (other_at, other)):
        target = pl.ds(pl.multiple_of(8 + rows, 8), ROWS)
        padded[target, 0:HALF] = ref[:, pl.ds(z_end, HALF)].astype(f32)
        padded[target, HALF:] = ref[:, 2 * GCH : GCH + GCONV].astype(f32)
        raw[pl.ds(rows, ROWS), :] = jnp.zeros((ROWS, 128), f32)
        raw[pl.ds(rows, ROWS), 0:32] = ref[:, GCH + GCONV : GCOLS].astype(f32)
    tap_rows[0:KCONV, 0:HALF] = taps[:, pl.ds(x_at, HALF)]
    tap_rows[0:KCONV, HALF:] = taps[:, GCH:GCONV]
    tap_rows[4:5, 0:HALF] = bias[:, pl.ds(x_at, HALF)]
    tap_rows[4:5, HALF:] = bias[:, GCH:GCONV]
    small[...] = jnp.zeros((8, 128), f32)
    small[0:1, 0:32] = step_bias[...]
    small[1:2, 0:32] = log_rates[...]

    for c0 in range(0, HALF + 2 * N, 256):
        for r0 in range(0, PAIR, 64):
            total = jnp.broadcast_to(tap_rows[4:5, c0 : c0 + 256], (64, 256))
            for k in range(KCONV):
                total = total + tap_rows[k : k + 1, c0 : c0 + 256] * padded[
                    5 + k + r0 : 5 + k + r0 + 64, c0 : c0 + 256
                ]
            active = (total * jax.nn.sigmoid(total)).astype(bf16)
            if c0 < HALF:
                values[r0 : r0 + 64, c0 : c0 + 256] = active
            elif c0 == HALF:
                keys[r0 : r0 + 64, :] = active
            else:
                queries[r0 : r0 + 64, :] = active

    first = core == 0

    def own(v):
        return jnp.where(first, v, pltpu.roll(v, 128 - HEADS, 1))

    head_lane = lanes((PAIR, 128)) < HEADS
    steps = own(raw[...] + small[0:1, :])
    steps = jnp.where(head_lane, jax.nn.softplus(steps), 0.0)
    rate = -jnp.exp(own(jnp.broadcast_to(small[1:2, :], (8, 128))))[0:1]
    logs = steps * rate
    row = lax.broadcasted_iota(jnp.int32, (PAIR, PAIR), 0)
    column = lax.broadcasted_iota(jnp.int32, (PAIR, PAIR), 1)
    running = dot(jnp.where(row >= column, 1.0, 0.0), logs, precision=lax.Precision.HIGHEST)
    running_t = running.T
    steps_t = steps.T
    growth[...] = split_three(jnp.exp(running))

    causal = row[:ROWS, :ROWS] >= column[:ROWS, :ROWS]
    products = []
    for a in (0, ROWS):
        own_product = dot(queries[a : a + ROWS, :], keys[a : a + ROWS, :], 1, 1)
        products.append(jnp.where(causal, own_product, 0.0))
    across = dot(queries[ROWS:, :], keys[:ROWS, :], 1, 1).astype(bf16)
    low_lane = lanes((ROWS, 128)) < P_SIZE
    for pair in range(HEADS // 2):
        c0 = pair * 128
        for i, a in enumerate((0, ROWS)):
            x = values[a : a + ROWS, c0 : c0 + 128]
            parts = []
            for h in (2 * pair, 2 * pair + 1):
                gap = running[a : a + ROWS, h : h + 1] - running_t[h : h + 1, a : a + ROWS]
                factor = products[i] * jnp.exp(jnp.minimum(gap, 0.0)) * steps_t[h : h + 1, a : a + ROWS]
                parts.append(dot(factor.astype(bf16), x))
            within[a : a + ROWS, c0 : c0 + 128] = jnp.where(low_lane, parts[0], parts[1])

    middle = running[ROWS - 1 : ROWS, :]
    end = running[PAIR - 1 : PAIR, :]
    to_end = split_three(jnp.exp(end - running) * steps)
    to_middle = split_three(jnp.exp(middle - running[:ROWS]) * steps[:ROWS])
    from_middle = split_three(jnp.exp(running[ROWS:] - middle))
    all_logs = split_three(jnp.broadcast_to(end, (PAIR, 128)))
    keys_t = keys[...].astype(f32).T.astype(bf16)
    for c0 in range(0, HALF, 256):
        table = head_table(c0, 256)
        x = values[:, c0 : c0 + 256].astype(f32)
        entering = dot(across, (x[:ROWS] * dot(to_middle, table)).astype(bf16))
        within[ROWS:, c0 : c0 + 256] += entering * dot(from_middle, table)
        weighted = (x * dot(to_end, table)).astype(bf16)
        send[:, c0 : c0 + 256] = dot(keys_t, weighted).astype(bf16)
    send[:, HALF:] = all_logs
    keys[...] = queries[...]


def prefix_kernel(got, back, decays):
    for c0 in range(0, HALF, 256):
        decays[:, c0 : c0 + 256] = jnp.exp(dot(got[:, HALF:], head_table(c0, 256)))
    state = jnp.zeros((8, HALF), f32)
    for pair in range(CHIPS // 2):
        rows = slice(16 * pair, 16 * pair + 16)
        local = got[rows, 0:HALF].astype(f32)
        decay = decays[rows, :]
        second = state * decay[:8] + local[:8]
        back[rows, :] = jnp.concatenate([state, second], axis=0).astype(bf16)
        state = second * decay[8:] + local[8:]


def carried_kernel(within, queries, growth, state, scanned):
    for c0 in range(0, HALF, 256):
        carried = dot(queries[...], state[:, c0 : c0 + 256])
        carried = carried * dot(growth[...], head_table(c0, 256))
        scanned[:, c0 : c0 + 256] = (within[:, c0 : c0 + 256] + carried).astype(bf16)


def norm_kernel(at, scanned, scanned_other, gate, gate_other, gain, normed, whole, gates):
    core = at[0]
    own_at = pl.multiple_of(core * HALF, 128)
    other_at = pl.multiple_of((1 - core) * HALF, 128)
    whole[:, pl.ds(own_at, HALF)] = scanned[...]
    whole[:, pl.ds(other_at, HALF)] = scanned_other[...]
    gates[pl.ds(pl.multiple_of(core * ROWS, 128), ROWS), :] = gate[...]
    gates[pl.ds(pl.multiple_of((1 - core) * ROWS, 128), ROWS), :] = gate_other[...]

    def body(i, carry):
        rows = pl.ds(pl.multiple_of(i * 16, 16), 16)
        g = gates[rows, :].astype(f32)
        gated = whole[rows, :].astype(f32) * (g * jax.nn.sigmoid(g))
        scale = lax.rsqrt(jnp.mean(gated * gated, axis=1, keepdims=True) + 1e-05)
        normed[rows, :] = (gated * scale * gain[...]).astype(bf16)
        return carry

    lax.fori_loop(0, PAIR // 16, body, 0)


def project_kernel(at, normed, weight, out, total):
    step = pl.program_id(0)

    @pl.when(step == 0)
    def _():
        total[...] = jnp.zeros_like(total)

    total[...] += dot(normed[...], weight[...])

    @pl.when(step == pl.num_programs(0) - 1)
    def _():
        out[...] = total[...].astype(out.dtype)


def project(block, normed, weight, dtype):
    depth = 512
    return pl.pallas_call(
        project_kernel,
        out_shape=jax.ShapeDtypeStruct((PAIR, BLOCK), dtype),
        grid_spec=pltpu.PrefetchScalarGridSpec(
            num_scalar_prefetch=1,
            grid=(GCH // depth,),
            in_specs=[
                pl.BlockSpec((PAIR, depth), lambda k, at: (0, k)),
                pl.BlockSpec((depth, BLOCK), lambda k, at: (k, at[0])),
            ],
            out_specs=pl.BlockSpec((PAIR, BLOCK), lambda k, at: (0, 0)),
            scratch_shapes=[pltpu.VMEM((PAIR, BLOCK), f32)],
        ),
        cost_estimate=pl.CostEstimate(
            flops=2 * PAIR * GCH * BLOCK, bytes_accessed=2 * GCH * BLOCK, transcendentals=0
        ),
        compiler_params=params(24),
        name="project",
    )(block, normed, weight)


def add_kernel(at, own, a, b, c, keep, away):
    core = at[0]
    for ref, which in ((keep, core), (away, 1 - core)):
        rows = pl.ds(pl.multiple_of(which * ROWS, 128), ROWS)
        total = own[rows, :] + a[rows, :].astype(f32) + b[rows, :].astype(f32)
        ref[...] = (total + c[rows, :].astype(f32)).astype(bf16)


def join_kernel(at, keep, got, out):
    core = at[0]
    out[:, pl.ds(pl.multiple_of(core * BLOCK, 128), BLOCK)] = keep[...]
    out[:, pl.ds(pl.multiple_of((1 - core) * BLOCK, 128), BLOCK)] = got[...]


def shape(*dims, dtype=bf16):
    return jax.ShapeDtypeStruct(dims, dtype)


def on_device(projected, conv_weight, conv_bias, step_bias, log_rates, norm_gain, out_weight):
    weight = lax.all_gather(out_weight[0], ("z", "y", "c"), axis=0, tiled=True)
    mine = projected.reshape(ROWS, GCOLS)
    swap = [(0, 1), (1, 0)]
    other = lax.ppermute(mine, "c", swap)
    tail = mine[ROWS - 8 :, GCH : GCH + GCONV]
    all_axes = ("z", "y", "c")
    rim_0 = lax.ppermute(tail, all_axes, [(2 * i + 1, 2 * i + 2) for i in range(CHIPS - 1)])
    rim_1 = lax.ppermute(tail, all_axes, [(2 * i + 1, 2 * i + 3) for i in range(CHIPS - 1)])
    core, tp = lax.axis_index("c"), lax.axis_index("tp")
    rim = jnp.where(core == 0, rim_0, rim_1)
    at = core.astype(jnp.int32).reshape(1)

    within, queries, growth, send = pl.pallas_call(
        scan_kernel,
        out_shape=(
            shape(PAIR, HALF, dtype=f32), shape(PAIR, N), shape(PAIR, 128), shape(N, HALF + 128),
        ),
        in_specs=[smem()] + [vmem()] * 7,
        out_specs=(vmem(),) * 4,
        scratch_shapes=[
            pltpu.VMEM((PAIR + 8, HALF + 2 * N), f32),
            pltpu.VMEM((8, HALF + 2 * N), f32),
            pltpu.VMEM((PAIR, HALF), bf16),
            pltpu.VMEM((PAIR, N), bf16),
            pltpu.VMEM((PAIR, 128), f32),
            pltpu.VMEM((8, 128), f32),
        ],
        cost_estimate=pl.CostEstimate(
            flops=1 << 29, bytes_accessed=5 * MIB, transcendentals=1 << 20
        ),
        compiler_params=params(32),
        name="scan",
    )(at, mine, other, rim, conv_weight[0], conv_bias, step_bias, log_rates)

    got = lax.all_to_all(send, ("z", "y"), 0, 0, tiled=True)
    back = pl.pallas_call(
        prefix_kernel,
        out_shape=shape(N, HALF),
        in_specs=[vmem()],
        out_specs=vmem(),
        scratch_shapes=[pltpu.VMEM((N, HALF), f32)],
        cost_estimate=pl.CostEstimate(flops=1 << 26, bytes_accessed=MIB, transcendentals=1 << 18),
        compiler_params=params(16),
        name="prefix",
    )(got)
    state = lax.all_to_all(back, ("z", "y"), 0, 0, tiled=True)
    scanned = pl.pallas_call(
        carried_kernel,
        out_shape=shape(PAIR, HALF),
        in_specs=[vmem()] * 4,
        out_specs=vmem(),
        cost_estimate=pl.CostEstimate(flops=1 << 28, bytes_accessed=2 * MIB, transcendentals=0),
        compiler_params=params(16),
        name="carried",
    )(within, queries, growth, state)
    scanned_other = lax.ppermute(scanned, "c", swap)

    gate = pl.BlockSpec((ROWS, GCH), lambda i: (0, 0))
    whole = pl.BlockSpec((PAIR, HALF), lambda i: (0, 0))
    normed = pl.pallas_call(
        norm_kernel,
        grid=(1,),
        out_shape=shape(PAIR, GCH),
        in_specs=[smem(), whole, whole, gate, gate, pl.BlockSpec((1, GCH), lambda i: (0, 0))],
        out_specs=pl.BlockSpec((PAIR, GCH), lambda i: (0, 0)),
        scratch_shapes=[pltpu.VMEM((PAIR, GCH), bf16), pltpu.VMEM((PAIR, GCH), bf16)],
        cost_estimate=pl.CostEstimate(flops=1 << 23, bytes_accessed=4 * MIB, transcendentals=1 << 19),
        compiler_params=params(24),
        name="norm",
    )(at, scanned, scanned_other, mine, other, norm_gain)

    shares = []
    for k in (2, 1, 3):
        block = (((tp + k) % T) * C + core).astype(jnp.int32).reshape(1)
        part = project(block, normed, weight, bf16)
        shares.append(lax.ppermute(part, "tp", [(i, (i + k) % T) for i in range(T)]))
    own = project((tp * C + core).astype(jnp.int32).reshape(1), normed, weight, f32)
    keep, away = pl.pallas_call(
        add_kernel,
        out_shape=(shape(ROWS, BLOCK), shape(ROWS, BLOCK)),
        in_specs=[smem()] + [vmem()] * 4,
        out_specs=(vmem(), vmem()),
        compiler_params=params(16),
        name="add",
    )(at, own, *shares)
    got_half = lax.ppermute(away, "c", swap)
    return pl.pallas_call(
        join_kernel,
        out_shape=shape(ROWS, C * BLOCK),
        in_specs=[smem(), vmem(), vmem()],
        out_specs=vmem(),
        compiler_params=params(16),
        name="join",
    )(at, keep, got_half)


def solution(mesh):
    chips = Mesh(mesh.devices.reshape(Z, Y, C, T), ("z", "y", "c", "tp"))
    ctx = ("z", "y", "c")
    return jax.shard_map(
        on_device,
        mesh=chips,
        in_specs=(
            P(ctx, "tp", None),
            P("tp", None, None),
            P("tp", None),
            P("tp", None),
            P("tp", None),
            P("tp", None),
            P("tp", ctx, None),
        ),
        out_specs=P(ctx, "tp"),
        check_vma=False,
    )
```

time: 391 us -> 156 us (0.40)
  matrix products: 91.8 us -> 0 us
  other arithmetic: 75.4 us -> 0.01 us
  local copies, waits for them, and re-layouts: 60.7 us -> 18.7 us
  waiting for transfers between devices: 71.7 us -> 33.8 us
  blocking collectives: 23.8 us -> 58.4 us
  loops' own time: 22.3 us -> 0 us
  Pallas kernels: 0 us -> 14.4 us
  starting transfers between devices: 28.7 us -> 16.2 us
    dot_general x65 -> x0, matrix products: 91.8 us -> none  [the longest x16 22 us: advance(): jnp.dot(c_block, b_block.T, preferred_element_type=jnp.float32)]
    mul x48 -> x0, other arithmetic: 48.1 us -> none  [the longest x16 38.7 us: advance(): weighted = x_block * tail_weight[:, :, None]]
    all_to_all x1 -> x2, blocking collectives: 23.8 us -> 58.4 us  [the longest x1 34.9 us: on_device(): got = lax.all_to_all(send, ('z', 'y'), 0, 0, tiled=True)]
    slice x57 -> x1, local copies, waits for them, and re-layouts: 30.7 us -> 0.01 us  [on_device(): tail = mine[ROWS - 8:, GCH:GCH + GCONV]]
    reduce_scatter x1 -> x0, waiting for transfers between devices: 28.7 us -> none  [on_device(): shares = lax.psum_scatter(summed, 'tp', scatter_dimension=1, tiled=True)]
    all_to_all x2 -> x0, starting transfers between devices: 23.8 us -> none  [the longest x1 13.5 us: on_device(): lax.all_to_all(spread_steps, 'ctx', split_axis=2, concat_axis=0, tiled=True)]
    another operation x1 -> x0, loops' own time: 22.3 us -> none  [ssd_blocks(): lax.scan(advance, initial, (x_blocks, step_blocks, b_blocks, c_blocks))]
    all_to_all x2 -> x0, waiting for transfers between devices: 14.9 us -> none  [the longest x1 14.9 us: on_device(): lax.all_to_all(values, 'ctx', split_axis=2, concat_axis=0, tiled=True)]
  transfers between devices with their start and end apart: 6 -> 9, of which waited for: 4 -> 4; matrix products, arithmetic and copies ran while one was open for 55% -> 2% of each run, Pallas kernels for 0% -> 8%
where the time goes in v1:
time: 156 us; the launch traced here: 155 us
  blocking collectives  58.4 us (37%)
  waiting for transfers between devices  33.8 us (22%)
  local copies, waits for them, and re-layouts  18.7 us (12%)
  starting transfers between devices  16.2 us (10%)
  Pallas kernels  14.4 us (9%)
  between operations  13.6 us (9%)
    all_to_all x1, blocking collectives, on_device(): got = lax.all_to_all(send, ('z', 'y'), 0, 0, tiled=True)  34.9 us
    all_gather x1, waiting for transfers between devices, on_device(): weight = lax.all_gather(out_weight[0], ('z', 'y', 'c'), axis=0, tiled=True)  30.3 us
    all_to_all x1, blocking collectives, on_device(): state = lax.all_to_all(back, ('z', 'y'), 0, 0, tiled=True)  23.5 us
    unnamed x23, local copies, waits for them, and re-layouts  17 us
    pallas_call x4, Pallas kernels, project(): pl.pallas_call(project_kernel, out_shape=jax.ShapeDtypeStruct((PAIR, BLOC...  6.31 us
    ppermute x3, starting transfers between devices, on_device(): lax.ppermute(part, 'tp', [(i, (i + k) % T) for i in range(T)])  5.68 us
    pallas_call x1, Pallas kernels, on_device(): pl.pallas_call(scan_kernel, out_shape=(shape(PAIR, HALF, dtype=f32), shap...  4.17 us
    ppermute x1, starting transfers between devices, on_device(): other = lax.ppermute(mine, 'c', swap)  3.33 us
  transfers between devices with their start and end apart: 9, of which 4 were waited for; matrix products, arithmetic and copies ran while one was open for 2% of the time, Pallas kernels for 8%

profile of v1, /device:TPU:1, one launch (start us, length us, event | category | flops | bytes accessed | tf_op | source)
XLA Modules:
  0.0 155.2 jit_solution(9350703585259433212)
XLA Ops:
  6.5 0.7 all-gather.3.cloned.1.call-update
  7.3 3.3 %collective-permute-start = (bf16[128,4640]{0,1:T(8,128)(2,1)}, bf16[128,4640]{0,1:T(8,128)(2,1)}, u32[]{:S(2)}, u32[]{:S(2)}) collective-permute-start(bf16[128,4640]{0,1:T(8,128)(2,1)} %bitcast.25), channel_id=1, source_target_pairs={{0,4},{4,0},{1,5},{5,1},{2,6},{6,2},{3,7},{7,3},{8,12},{12,8},{9,1... | collective-permute-start | bytes 3563528 | tf_op jit(solution)/shard_map/ppermute | solution.py:258
  10.6 1.7 %copy.9 = bf16[128,1,4640]{2,0,1:T(8,128)(2,1)S(1)} copy(bf16[128,1,4640]{0,2,1:T(8,128)(2,1)} %param.7) | data formatting | bytes 2375680 | tf_op args[0]
  12.3 1.4 collective-permute-start.1
  13.7 3.2 %collective-permute-start.2 = (bf16[8,2560]{1,0:T(8,128)(2,1)S(1)}, bf16[8,2560]{1,0:T(8,128)(2,1)S(1)}, u32[]{:S(2)}, u32[]{:S(2)}) collective-permute-start(bf16[8,2560]{1,0:T(8,128)(2,1)S(1)} %slice.4), channel_id=1, source_target_pairs={{4,12},{12,20},{20,28},{28,36},{36,44},{44,52},{52,60},{60,68},{68... | collective-permute-start | bytes 122888 | tf_op jit(solution)/shard_map/ppermute | solution.py:262
  16.9 1.1 collective-permute-done.2
  18.1 1.7 %copy.11.other.gate_other = bf16[128,4640]{1,0:T(8,128)(2,1)S(1)} copy(bf16[128,4640]{0,1:T(8,128)(2,1)} %collective-permute-done) | data formatting | bytes 2375680 | tf_op jit(solution)/shard_map/ppermute | solution.py:258
  19.8 4.2 %scan.1 = (f32[256,1024]{1,0:T(8,128)S(1)}, bf16[256,256]{1,0:T(8,128)(2,1)S(1)}, bf16[256,128]{1,0:T(8,128)(2,1)S(1)}, bf16[256,1152]{1,0:T(8,128)(2,1)S(1)}) custom-call(s32[1]{0:T(128)} %bitcast.at, bf16[128,4640]{1,0:T(8,128)(2,1)S(1)} %bitcast.18, bf16[128,4640]{1,0:T(8,128)(2,1)S(1)} %copy.11.other.gate_other, ...), custom_call_target="tpu_custom_call" | custom-call | flops 536870912 | bytes 5242880 | tf_op jit(solution)/shard_map/scan/pallas_call | solution.py:267
  24.0 34.9 %all_to_all.22 = bf16[32,8,1152]{2,1,0:T(8,128)(2,1)S(1)} all-to-all(bf16[32,8,1152]{2,1,0:T(8,128)(2,1)S(1)} %bitcast.23), channel_id=1, replica_groups=mesh['z'=8,'y'=4,'c'=2,'tp'=4] {'z','y'}, dimensions={0} | all-to-all | bytes 1179648 | tf_op jit(solution)/shard_map/all_to_all | solution.py:289
  58.9 0.3 prefix.1
  59.3 23.5 %all_to_all.23 = bf16[32,8,1024]{2,1,0:T(8,128)(2,1)S(1)} all-to-all(bf16[32,8,1024]{2,1,0:T(8,128)(2,1)S(1)} %bitcast.21), channel_id=1, replica_groups=mesh['z'=8,'y'=4,'c'=2,'tp'=4] {'z','y'}, dimensions={0} | all-to-all | bytes 1048576 | tf_op jit(solution)/shard_map/all_to_all | solution.py:300
  82.8 0.4 carried.1.scanned
  83.2 1.4 collective-permute-start.3
  84.7 0.8 copy-done.2
  85.5 0.7 collective-permute-done.3.scanned_other
  86.2 0.8 copy-done.4
  87.0 1.0 copy-done.3
  88.0 1.1 copy-done.5
  89.1 2.3 %norm.1.normed = bf16[256,2048]{1,0:T(8,128)(2,1)S(1)} custom-call(s32[1]{0:T(128)} %bitcast.at, bf16[256,1024]{1,0:T(8,128)(2,1)S(1)} %copy-done.3, bf16[256,1024]{1,0:T(8,128)(2,1)S(1)} %copy-done.5, bf16[128,4640]{1,0:T(8,128)(2,1)S(1)} %bitcast.19, bf16[128,4640]{1,0:T(8,128)(2,1)S(1)} %copy.11.other.gate_other, f32[1,2048]{1,0:T(1,128)S(1)} %copy-done.8), custom_call_target="tpu_custom_call" | custom-call | flops 8388608 | bytes 4194304 | tf_op jit(solution)/shard_map/norm/pallas_call | solution.py:314
  91.4 30.3 %all-gather.3.cloned.1.call-done = bf16[1,2048,4096]{2,1,0:T(8,128)(2,1)} async-done(((bf16[1,32,4096]{2,1,0:T(8,128)(2,1)}), bf16[1,2048,4096]{2,1,0:T(8,128)(2,1)}) %all-gather.3.cloned.1.call-update) | async-done | bytes 16777232 | tf_op jit(solution)/shard_map/all_gather | solution.py:255
  121.7 5.8 %copy-done = bf16[1,2048,4096]{2,1,0:T(8,128)(2,1)S(1)} copy-done((bf16[1,2048,4096]{2,1,0:T(8,128)(2,1)S(1)}, bf16[1,2048,4096]{2,1,0:T(8,128)(2,1)}, u32[]{:S(2)}) %copy-start) | copy-done | bytes 16777240
  127.5 1.6 %project.5 = bf16[256,512]{1,0:T(8,128)(2,1)S(1)} custom-call(s32[1]{0:T(128)} %bitcast.10.at, bf16[256,2048]{1,0:T(8,128)(2,1)S(1)} %norm.1.normed, bf16[2048,4096]{1,0:T(8,128)(2,1)S(1)} %bitcast.13), custom_call_target="tpu_custom_call" | custom-call | flops 536870912 | bytes 2097152 | tf_op jit(solution)/shard_map/project/pallas_call | solution.py:215
  129.1 2.8 %collective-permute-start.4 = (bf16[256,512]{1,0:T(8,128)(2,1)S(1)}, bf16[256,512]{1,0:T(8,128)(2,1)S(1)}, u32[]{:S(2)}, u32[]{:S(2)}) collective-permute-start(bf16[256,512]{1,0:T(8,128)(2,1)S(1)} %project.5), channel_id=1, source_target_pairs={{0,2},{1,3},{2,0},{3,1},{4,6},{5,7},{6,4},{7,5},{8,10},{9,11},{10,... | collective-permute-start | bytes 786440 | tf_op jit(solution)/shard_map/ppermute | solution.py:330
  131.9 1.6 %project.6 = bf16[256,512]{1,0:T(8,128)(2,1)S(1)} custom-call(s32[1]{0:T(128)} %bitcast.11.at, bf16[256,2048]{1,0:T(8,128)(2,1)S(1)} %norm.1.normed, bf16[2048,4096]{1,0:T(8,128)(2,1)S(1)} %bitcast.14), custom_call_target="tpu_custom_call" | custom-call | flops 536870912 | bytes 2097152 | tf_op jit(solution)/shard_map/project/pallas_call | solution.py:215
  133.5 0.4 collective-permute-start.5
  133.9 1.6 %project.7 = bf16[256,512]{1,0:T(8,128)(2,1)S(1)} custom-call(s32[1]{0:T(128)} %bitcast.12.at, bf16[256,2048]{1,0:T(8,128)(2,1)S(1)} %norm.1.normed, bf16[2048,4096]{1,0:T(8,128)(2,1)S(1)} %bitcast.15), custom_call_target="tpu_custom_call" | custom-call | flops 536870912 | bytes 2097152 | tf_op jit(solution)/shard_map/project/pallas_call | solution.py:215
  135.4 2.5 %collective-permute-start.6 = (bf16[256,512]{1,0:T(8,128)(2,1)S(1)}, bf16[256,512]{1,0:T(8,128)(2,1)S(1)}, u32[]{:S(2)}, u32[]{:S(2)}) collective-permute-start(bf16[256,512]{1,0:T(8,128)(2,1)S(1)} %project.7), channel_id=1, source_target_pairs={{0,3},{1,0},{2,1},{3,2},{4,7},{5,4},{6,5},{7,6},{8,11},{9,8},{10,9... | collective-permute-start | bytes 786440 | tf_op jit(solution)/shard_map/ppermute | solution.py:330
  137.9 5.8 %copy-done.1 = bf16[1,2048,4096]{2,1,0:T(8,128)(2,1)S(1)} copy-done((bf16[1,2048,4096]{2,1,0:T(8,128)(2,1)S(1)}, bf16[1,2048,4096]{2,1,0:T(8,128)(2,1)}, u32[]{:S(2)}) %copy-start.1) | copy-done | bytes 16777240
  143.7 1.6 %project.4.own = f32[256,512]{1,0:T(8,128)S(1)} custom-call(s32[1]{0:T(128)} %bitcast.1.at, bf16[256,2048]{1,0:T(8,128)(2,1)S(1)} %norm.1.normed, bf16[2048,4096]{1,0:T(8,128)(2,1)S(1)} %bitcast.16), custom_call_target="tpu_custom_call" | custom-call | flops 536870912 | bytes 2097152 | tf_op jit(solution)/shard_map/project/pallas_call | solution.py:215
  145.4 1.2 collective-permute-start.7
  146.6 1.0 collective-permute-done.7.got
  147.6 0.7 join.1
  (25 shorter events, 0.2 us)
Async XLA Ops:
  6.5 115.2 %all-gather.3.cloned.1.call-start = ((), (), s32[]{:S(2)}) async-start(), calls=%async_computation.2 | async-start | bytes 17039360 | tf_op jit(solution)/shard_map/all_gather | solution.py:255
  7.3 10.8 %collective-permute-start = (bf16[128,4640]{0,1:T(8,128)(2,1)}, bf16[128,4640]{0,1:T(8,128)(2,1)}, u32[]{:S(2)}, u32[]{:S(2)}) collective-permute-start(bf16[128,4640]{0,1:T(8,128)(2,1)} %bitcast.25), channel_id=1, source_target_pairs={{0,4},{4,0},{1,5},{5,1},{2,6},{6,2},{3,7},{7,3},{8,12},{12,8},{9,1... | collective-permute-start | bytes 3563528 | tf_op jit(solution)/shard_map/ppermute | solution.py:258
  12.3 4.6 %collective-permute-start.1 = (bf16[8,2560]{1,0:T(8,128)(2,1)S(1)}, bf16[8,2560]{1,0:T(8,128)(2,1)S(1)}, u32[]{:S(2)}, u32[]{:S(2)}) collective-permute-start(bf16[8,2560]{1,0:T(8,128)(2,1)S(1)} %slice.4), channel_id=1, source_target_pairs={{4,8},{12,16},{20,24},{28,32},{36,40},{44,48},{52,56},{60,64},{68,... | collective-permute-start | bytes 122888 | tf_op jit(solution)/shard_map/ppermute | solution.py:261
  13.7 4.3 %collective-permute-start.2 = (bf16[8,2560]{1,0:T(8,128)(2,1)S(1)}, bf16[8,2560]{1,0:T(8,128)(2,1)S(1)}, u32[]{:S(2)}, u32[]{:S(2)}) collective-permute-start(bf16[8,2560]{1,0:T(8,128)(2,1)S(1)} %slice.4), channel_id=1, source_target_pairs={{4,12},{12,20},{20,28},{28,36},{36,44},{44,52},{52,60},{60,68},{68... | collective-permute-start | bytes 122888 | tf_op jit(solution)/shard_map/ppermute | solution.py:262
  18.0 1.8 %copy-start.6 = (f32[1,4,2560]{2,1,0:T(4,128)S(1)}, f32[1,4,2560]{2,1,0:T(4,128)}, u32[]{:S(2)}) copy-start(f32[1,4,2560]{2,1,0:T(4,128)} %param.8) | copy-start | bytes 122884
  18.0 1.8 %copy-start.7 = (f32[1,2560]{1,0:T(1,128)S(1)}, f32[1,2560]{1,0:T(1,128)}, u32[]{:S(2)}) copy-start(f32[1,2560]{1,0:T(1,128)} %bias.1) | copy-start | bytes 30724
  18.0 1.8 %copy-start.9 = (f32[1,32]{1,0:T(1,128)S(1)}, f32[1,32]{1,0:T(1,128)}, u32[]{:S(2)}) copy-start(f32[1,32]{1,0:T(1,128)} %step_bias.1) | copy-start | bytes 388
  18.0 1.8 %copy-start.10 = (f32[1,32]{1,0:T(1,128)S(1)}, f32[1,32]{1,0:T(1,128)}, u32[]{:S(2)}) copy-start(f32[1,32]{1,0:T(1,128)} %log_rates.1) | copy-start | bytes 388
  82.8 4.2 %copy-start.8 = (f32[1,2048]{1,0:T(1,128)S(1)}, f32[1,2048]{1,0:T(1,128)}, u32[]{:S(2)}) copy-start(f32[1,2048]{1,0:T(1,128)} %gain.1) | copy-start | bytes 24580
  83.2 3.0 %collective-permute-start.3 = (bf16[256,1024]{1,0:T(8,128)(2,1)S(1)}, bf16[256,1024]{1,0:T(8,128)(2,1)S(1)}, u32[]{:S(2)}, u32[]{:S(2)}) collective-permute-start(bf16[256,1024]{1,0:T(8,128)(2,1)S(1)} %carried.1.scanned), channel_id=1, source_target_pairs={{0,4},{4,0},{1,5},{5,1},{2,6},{6,2},{3,7},{7,3},{8,12},{12,8},{9,1... | collective-permute-start | bytes 1572872 | tf_op jit(solution)/shard_map/ppermute | solution.py:310
  84.7 0.8 copy-start.2
  86.2 0.8 copy-start.4
  87.0 1.0 copy-start.3
  88.0 1.1 copy-start.5
  121.7 5.8 %copy-start = (bf16[1,2048,4096]{2,1,0:T(8,128)(2,1)S(1)}, bf16[1,2048,4096]{2,1,0:T(8,128)(2,1)}, u32[]{:S(2)}) copy-start(bf16[1,2048,4096]{2,1,0:T(8,128)(2,1)} %all-gather.3.cloned.1.call-done) | copy-start | bytes 50331652
  129.1 16.2 %collective-permute-start.4 = (bf16[256,512]{1,0:T(8,128)(2,1)S(1)}, bf16[256,512]{1,0:T(8,128)(2,1)S(1)}, u32[]{:S(2)}, u32[]{:S(2)}) collective-permute-start(bf16[256,512]{1,0:T(8,128)(2,1)S(1)} %project.5), channel_id=1, source_target_pairs={{0,2},{1,3},{2,0},{3,1},{4,6},{5,7},{6,4},{7,5},{8,10},{9,11},{10,... | collective-permute-start | bytes 786440 | tf_op jit(solution)/shard_map/ppermute | solution.py:330
  133.5 11.8 %collective-permute-start.5 = (bf16[256,512]{1,0:T(8,128)(2,1)S(1)}, bf16[256,512]{1,0:T(8,128)(2,1)S(1)}, u32[]{:S(2)}, u32[]{:S(2)}) collective-permute-start(bf16[256,512]{1,0:T(8,128)(2,1)S(1)} %project.6), channel_id=1, source_target_pairs={{0,1},{1,2},{2,3},{3,0},{4,5},{5,6},{6,7},{7,4},{8,9},{9,10},{10,1... | collective-permute-start | bytes 786440 | tf_op jit(solution)/shard_map/ppermute | solution.py:330
  135.4 9.9 %collective-permute-start.6 = (bf16[256,512]{1,0:T(8,128)(2,1)S(1)}, bf16[256,512]{1,0:T(8,128)(2,1)S(1)}, u32[]{:S(2)}, u32[]{:S(2)}) collective-permute-start(bf16[256,512]{1,0:T(8,128)(2,1)S(1)} %project.7), channel_id=1, source_target_pairs={{0,3},{1,0},{2,1},{3,2},{4,7},{5,4},{6,5},{7,6},{8,11},{9,8},{10,9... | collective-permute-start | bytes 786440 | tf_op jit(solution)/shard_map/ppermute | solution.py:330
  137.9 5.8 %copy-start.1 = (bf16[1,2048,4096]{2,1,0:T(8,128)(2,1)S(1)}, bf16[1,2048,4096]{2,1,0:T(8,128)(2,1)}, u32[]{:S(2)}) copy-start(bf16[1,2048,4096]{2,1,0:T(8,128)(2,1)} %all-gather.3.cloned.1.call-done) | copy-start | bytes 50331652
  145.4 2.2 %collective-permute-start.7 = (bf16[128,512]{1,0:T(8,128)(2,1)S(1)}, bf16[128,512]{1,0:T(8,128)(2,1)S(1)}, u32[]{:S(2)}, u32[]{:S(2)}) collective-permute-start(bf16[128,512]{1,0:T(8,128)(2,1)S(1)} %get-tuple-element.16), channel_id=1, source_target_pairs={{0,4},{4,0},{1,5},{5,1},{2,6},{6,2},{3,7},{7,3},{8,12},{12,8},{9,1... | collective-permute-start | bytes 393224 | tf_op jit(solution)/shard_map/ppermute | solution.py:340
Sparse Core Ops, SparseCore 0:
  10.1 111.5 all-gather.2

commit v2 on v1

--- a/solution.py
+++ b/solution.py
@@ -182,8 +182,8 @@
     other_at = pl.multiple_of((1 - core) * HALF, 128)
     whole[:, pl.ds(own_at, HALF)] = scanned[...]
     whole[:, pl.ds(other_at, HALF)] = scanned_other[...]
-    gates[pl.ds(pl.multiple_of(core * ROWS, 128), ROWS), :] = gate[...]
-    gates[pl.ds(pl.multiple_of((1 - core) * ROWS, 128), ROWS), :] = gate_other[...]
+    gates[pl.ds(pl.multiple_of(core * ROWS, 128), ROWS), :] = gate[:, 0:GCH]
+    gates[pl.ds(pl.multiple_of((1 - core) * ROWS, 128), ROWS), :] = gate_other[:, 0:GCH]
 
     def body(i, carry):
         rows = pl.ds(pl.multiple_of(i * 16, 16), 16)
@@ -228,7 +228,7 @@
         cost_estimate=pl.CostEstimate(
             flops=2 * PAIR * GCH * BLOCK, bytes_accessed=2 * GCH * BLOCK, transcendentals=0
         ),
-        compiler_params=params(24),
+        compiler_params=params(52),
         name="project",
     )(block, normed, weight)
 
@@ -309,14 +309,11 @@
     )(within, queries, growth, state)
     scanned_other = lax.ppermute(scanned, "c", swap)
 
-    gate = pl.BlockSpec((ROWS, GCH), lambda i: (0, 0))
-    whole = pl.BlockSpec((PAIR, HALF), lambda i: (0, 0))
     normed = pl.pallas_call(
         norm_kernel,
-        grid=(1,),
         out_shape=shape(PAIR, GCH),
-        in_specs=[smem(), whole, whole, gate, gate, pl.BlockSpec((1, GCH), lambda i: (0, 0))],
-        out_specs=pl.BlockSpec((PAIR, GCH), lambda i: (0, 0)),
+        in_specs=[smem()] + [vmem()] * 5,
+        out_specs=vmem(),
         scratch_shapes=[pltpu.VMEM((PAIR, GCH), bf16), pltpu.VMEM((PAIR, GCH), bf16)],
         cost_estimate=pl.CostEstimate(flops=1 << 23, bytes_accessed=4 * MIB, transcendentals=1 << 19),
         compiler_params=params(24),

time: 156 us -> 153 us (0.981)
  local copies, waits for them, and re-layouts: 18.7 us -> 7.17 us
  Pallas kernels: 14.4 us -> 20.8 us
  waiting for transfers between devices: 33.8 us -> 35.4 us
    unnamed x23 -> x19, local copies, waits for them, and re-layouts: 17 us -> 5.44 us
    pallas_call x4, Pallas kernels: 6.31 us -> 12.8 us  [project(): pl.pallas_call(project_kernel, out_shape=jax.ShapeDtypeStruct((PAIR, BLOC...]
    ppermute x3, waiting for transfers between devices: 0.01 us -> 1.6 us  [on_device(): lax.ppermute(part, 'tp', [(i, (i + k) % T) for i in range(T)])]
  transfers between devices with their start and end apart: 9 -> 9, of which waited for: 4 -> 5; matrix products, arithmetic and copies ran while one was open for 2% -> 2% of each run, Pallas kernels for 8% -> 11%
where the time goes in v2:
time: 153 us; the launch traced here: 152 us
  blocking collectives  58.4 us (38%)
  waiting for transfers between devices  35.4 us (23%)
  Pallas kernels  20.8 us (14%)
  starting transfers between devices  16.8 us (11%)
  between operations  13.6 us (9%)
  local copies, waits for them, and re-layouts  7.17 us (5%)
    all_to_all x1, blocking collectives, on_device(): got = lax.all_to_all(send, ('z', 'y'), 0, 0, tiled=True)  34.9 us
    all_gather x1, waiting for transfers between devices, on_device(): weight = lax.all_gather(out_weight[0], ('z', 'y', 'c'), axis=0, tiled=True)  30.3 us
    all_to_all x1, blocking collectives, on_device(): state = lax.all_to_all(back, ('z', 'y'), 0, 0, tiled=True)  23.5 us
    pallas_call x4, Pallas kernels, project(): pl.pallas_call(project_kernel, out_shape=jax.ShapeDtypeStruct((PAIR, BLOC...  12.8 us
    ppermute x3, starting transfers between devices, on_device(): lax.ppermute(part, 'tp', [(i, (i + k) % T) for i in range(T)])  5.68 us
    unnamed x19, local copies, waits for them, and re-layouts  5.44 us
    pallas_call x1, Pallas kernels, on_device(): pl.pallas_call(scan_kernel, out_shape=(shape(PAIR, HALF, dtype=f32), shap...  4.17 us
    ppermute x1, starting transfers between devices, on_device(): other = lax.ppermute(mine, 'c', swap)  3.33 us
  transfers between devices with their start and end apart: 9, of which 5 were waited for; matrix products, arithmetic and copies ran while one was open for 2% of the time, Pallas kernels for 11%

profile of v2, /device:TPU:1, one launch (start us, length us, event | category | flops | bytes accessed | tf_op | source)
XLA Modules:
  0.0 152.3 jit_solution(3782433165900186776)
XLA Ops:
  6.5 0.7 all-gather.3.cloned.1.call-update
  7.3 3.3 %collective-permute-start = (bf16[128,4640]{0,1:T(8,128)(2,1)}, bf16[128,4640]{0,1:T(8,128)(2,1)}, u32[]{:S(2)}, u32[]{:S(2)}) collective-permute-start(bf16[128,4640]{0,1:T(8,128)(2,1)} %bitcast.25), channel_id=1, source_target_pairs={{0,4},{4,0},{1,5},{5,1},{2,6},{6,2},{3,7},{7,3},{8,12},{12,8},{9,1... | collective-permute-start | bytes 3563528 | tf_op jit(solution)/shard_map/ppermute | solution.py:258
  10.6 1.7 %copy.9 = bf16[128,1,4640]{2,0,1:T(8,128)(2,1)S(1)} copy(bf16[128,1,4640]{0,2,1:T(8,128)(2,1)} %param.7) | data formatting | bytes 2375680 | tf_op args[0]
  12.3 1.4 collective-permute-start.1
  13.7 3.2 %collective-permute-start.2 = (bf16[8,2560]{1,0:T(8,128)(2,1)S(1)}, bf16[8,2560]{1,0:T(8,128)(2,1)S(1)}, u32[]{:S(2)}, u32[]{:S(2)}) collective-permute-start(bf16[8,2560]{1,0:T(8,128)(2,1)S(1)} %slice.4), channel_id=1, source_target_pairs={{4,12},{12,20},{20,28},{28,36},{36,44},{44,52},{52,60},{60,68},{68... | collective-permute-start | bytes 122888 | tf_op jit(solution)/shard_map/ppermute | solution.py:262
  16.9 1.1 collective-permute-done.2
  18.1 1.7 %copy.11.other.gate_other = bf16[128,4640]{1,0:T(8,128)(2,1)S(1)} copy(bf16[128,4640]{0,1:T(8,128)(2,1)} %collective-permute-done) | data formatting | bytes 2375680 | tf_op jit(solution)/shard_map/ppermute | solution.py:258
  19.8 4.2 %scan.1 = (f32[256,1024]{1,0:T(8,128)S(1)}, bf16[256,256]{1,0:T(8,128)(2,1)S(1)}, bf16[256,128]{1,0:T(8,128)(2,1)S(1)}, bf16[256,1152]{1,0:T(8,128)(2,1)S(1)}) custom-call(s32[1]{0:T(128)} %bitcast.at, bf16[128,4640]{1,0:T(8,128)(2,1)S(1)} %bitcast.14, bf16[128,4640]{1,0:T(8,128)(2,1)S(1)} %copy.11.other.gate_other, ...), custom_call_target="tpu_custom_call" | custom-call | flops 536870912 | bytes 5242880 | tf_op jit(solution)/shard_map/scan/pallas_call | solution.py:267
  24.0 34.9 %all_to_all.22 = bf16[32,8,1152]{2,1,0:T(8,128)(2,1)S(1)} all-to-all(bf16[32,8,1152]{2,1,0:T(8,128)(2,1)S(1)} %bitcast.19), channel_id=1, replica_groups=mesh['z'=8,'y'=4,'c'=2,'tp'=4] {'z','y'}, dimensions={0} | all-to-all | bytes 1179648 | tf_op jit(solution)/shard_map/all_to_all | solution.py:289
  58.9 0.3 prefix.1
  59.3 23.5 %all_to_all.23 = bf16[32,8,1024]{2,1,0:T(8,128)(2,1)S(1)} all-to-all(bf16[32,8,1024]{2,1,0:T(8,128)(2,1)S(1)} %bitcast.17), channel_id=1, replica_groups=mesh['z'=8,'y'=4,'c'=2,'tp'=4] {'z','y'}, dimensions={0} | all-to-all | bytes 1048576 | tf_op jit(solution)/shard_map/all_to_all | solution.py:300
  82.8 0.4 carried.1.scanned
  83.2 1.4 collective-permute-start.3
  84.7 0.8 copy-done
  85.5 0.7 collective-permute-done.3.scanned_other
  86.2 0.8 copy-done.2
  87.0 1.0 copy-done.1
  88.0 1.1 copy-done.3
  89.1 2.3 %norm.1.normed = bf16[256,2048]{1,0:T(8,128)(2,1)S(1)} custom-call(s32[1]{0:T(128)} %bitcast.at, bf16[256,1024]{1,0:T(8,128)(2,1)S(1)} %copy-done.1, bf16[256,1024]{1,0:T(8,128)(2,1)S(1)} %copy-done.3, bf16[128,4640]{1,0:T(8,128)(2,1)S(1)} %bitcast.15, bf16[128,4640]{1,0:T(8,128)(2,1)S(1)} %copy.11.other.gate_other, f32[1,2048]{1,0:T(1,128)S(1)} %copy-done.6), custom_call_target="tpu_custom_call" | custom-call | flops 8388608 | bytes 4194304 | tf_op jit(solution)/shard_map/norm/pallas_call | solution.py:312
  91.4 30.3 %all-gather.3.cloned.1.call-done = bf16[1,2048,4096]{2,1,0:T(8,128)(2,1)} async-done(((bf16[1,32,4096]{2,1,0:T(8,128)(2,1)}), bf16[1,2048,4096]{2,1,0:T(8,128)(2,1)}) %all-gather.3.cloned.1.call-update) | async-done | bytes 16777232 | tf_op jit(solution)/shard_map/all_gather | solution.py:255
  121.7 3.2 %project.5 = bf16[256,512]{1,0:T(8,128)(2,1)S(1)} custom-call(s32[1]{0:T(128)} %bitcast.10.at, bf16[256,2048]{1,0:T(8,128)(2,1)S(1)} %norm.1.normed, bf16[2048,4096]{1,0:T(8,128)(2,1)} %bitcast.21), custom_call_target="tpu_custom_call" | custom-call | flops 536870912 | bytes 2097152 | tf_op jit(solution)/shard_map/project/pallas_call | solution.py:215
  124.9 2.8 %collective-permute-start.4 = (bf16[256,512]{1,0:T(8,128)(2,1)S(1)}, bf16[256,512]{1,0:T(8,128)(2,1)S(1)}, u32[]{:S(2)}, u32[]{:S(2)}) collective-permute-start(bf16[256,512]{1,0:T(8,128)(2,1)S(1)} %project.5), channel_id=1, source_target_pairs={{0,2},{1,3},{2,0},{3,1},{4,6},{5,7},{6,4},{7,5},{8,10},{9,11},{10,... | collective-permute-start | bytes 786440 | tf_op jit(solution)/shard_map/ppermute | solution.py:327
  127.8 3.2 %project.6 = bf16[256,512]{1,0:T(8,128)(2,1)S(1)} custom-call(s32[1]{0:T(128)} %bitcast.11.at, bf16[256,2048]{1,0:T(8,128)(2,1)S(1)} %norm.1.normed, bf16[2048,4096]{1,0:T(8,128)(2,1)} %bitcast.22), custom_call_target="tpu_custom_call" | custom-call | flops 536870912 | bytes 2097152 | tf_op jit(solution)/shard_map/project/pallas_call | solution.py:215
  131.0 0.4 collective-permute-start.5
  131.3 3.2 %project.7 = bf16[256,512]{1,0:T(8,128)(2,1)S(1)} custom-call(s32[1]{0:T(128)} %bitcast.12.at, bf16[256,2048]{1,0:T(8,128)(2,1)S(1)} %norm.1.normed, bf16[2048,4096]{1,0:T(8,128)(2,1)} %bitcast.23), custom_call_target="tpu_custom_call" | custom-call | flops 536870912 | bytes 2097152 | tf_op jit(solution)/shard_map/project/pallas_call | solution.py:215
  134.5 2.5 %collective-permute-start.6 = (bf16[256,512]{1,0:T(8,128)(2,1)S(1)}, bf16[256,512]{1,0:T(8,128)(2,1)S(1)}, u32[]{:S(2)}, u32[]{:S(2)}) collective-permute-start(bf16[256,512]{1,0:T(8,128)(2,1)S(1)} %project.7), channel_id=1, source_target_pairs={{0,3},{1,0},{2,1},{3,2},{4,7},{5,4},{6,5},{7,6},{8,11},{9,8},{10,9... | collective-permute-start | bytes 786440 | tf_op jit(solution)/shard_map/ppermute | solution.py:327
  137.0 3.2 %project.4.own = f32[256,512]{1,0:T(8,128)S(1)} custom-call(s32[1]{0:T(128)} %bitcast.1.at, bf16[256,2048]{1,0:T(8,128)(2,1)S(1)} %norm.1.normed, bf16[2048,4096]{1,0:T(8,128)(2,1)} %bitcast.24), custom_call_target="tpu_custom_call" | custom-call | flops 536870912 | bytes 2097152 | tf_op jit(solution)/shard_map/project/pallas_call | solution.py:215
  140.2 1.6 %collective-permute-done.6.c = bf16[256,512]{1,0:T(8,128)(2,1)S(1)} collective-permute-done((bf16[256,512]{1,0:T(8,128)(2,1)S(1)}, bf16[256,512]{1,0:T(8,128)(2,1)S(1)}, u32[]{:S(2)}, u32[]{:S(2)}) %collective-permute-start.6) | collective-permute-done | bytes 262176 | tf_op jit(solution)/shard_map/ppermute | solution.py:327
  141.8 0.1 add.42
  141.9 1.8 %collective-permute-start.7 = (bf16[128,512]{1,0:T(8,128)(2,1)S(1)}, bf16[128,512]{1,0:T(8,128)(2,1)S(1)}, u32[]{:S(2)}, u32[]{:S(2)}) collective-permute-start(bf16[128,512]{1,0:T(8,128)(2,1)S(1)} %get-tuple-element.16), channel_id=1, source_target_pairs={{0,4},{4,0},{1,5},{5,1},{2,6},{6,2},{3,7},{7,3},{8,12},{12,8},{9,1... | collective-permute-start | bytes 393224 | tf_op jit(solution)/shard_map/ppermute | solution.py:337
  143.7 1.0 collective-permute-done.7.got
  144.7 0.7 join.1
  (21 shorter events, 0.1 us)
Async XLA Ops:
  6.5 115.2 %all-gather.3.cloned.1.call-start = ((), (), s32[]{:S(2)}) async-start(), calls=%async_computation.2 | async-start | bytes 17039360 | tf_op jit(solution)/shard_map/all_gather | solution.py:255
  7.3 10.8 %collective-permute-start = (bf16[128,4640]{0,1:T(8,128)(2,1)}, bf16[128,4640]{0,1:T(8,128)(2,1)}, u32[]{:S(2)}, u32[]{:S(2)}) collective-permute-start(bf16[128,4640]{0,1:T(8,128)(2,1)} %bitcast.25), channel_id=1, source_target_pairs={{0,4},{4,0},{1,5},{5,1},{2,6},{6,2},{3,7},{7,3},{8,12},{12,8},{9,1... | collective-permute-start | bytes 3563528 | tf_op jit(solution)/shard_map/ppermute | solution.py:258
  12.3 4.6 %collective-permute-start.1 = (bf16[8,2560]{1,0:T(8,128)(2,1)S(1)}, bf16[8,2560]{1,0:T(8,128)(2,1)S(1)}, u32[]{:S(2)}, u32[]{:S(2)}) collective-permute-start(bf16[8,2560]{1,0:T(8,128)(2,1)S(1)} %slice.4), channel_id=1, source_target_pairs={{4,8},{12,16},{20,24},{28,32},{36,40},{44,48},{52,56},{60,64},{68,... | collective-permute-start | bytes 122888 | tf_op jit(solution)/shard_map/ppermute | solution.py:261
  13.7 4.3 %collective-permute-start.2 = (bf16[8,2560]{1,0:T(8,128)(2,1)S(1)}, bf16[8,2560]{1,0:T(8,128)(2,1)S(1)}, u32[]{:S(2)}, u32[]{:S(2)}) collective-permute-start(bf16[8,2560]{1,0:T(8,128)(2,1)S(1)} %slice.4), channel_id=1, source_target_pairs={{4,12},{12,20},{20,28},{28,36},{36,44},{44,52},{52,60},{60,68},{68... | collective-permute-start | bytes 122888 | tf_op jit(solution)/shard_map/ppermute | solution.py:262
  18.0 1.8 %copy-start.4 = (f32[1,4,2560]{2,1,0:T(4,128)S(1)}, f32[1,4,2560]{2,1,0:T(4,128)}, u32[]{:S(2)}) copy-start(f32[1,4,2560]{2,1,0:T(4,128)} %param.8) | copy-start | bytes 122884
  18.0 1.8 %copy-start.5 = (f32[1,2560]{1,0:T(1,128)S(1)}, f32[1,2560]{1,0:T(1,128)}, u32[]{:S(2)}) copy-start(f32[1,2560]{1,0:T(1,128)} %bias.1) | copy-start | bytes 30724
  18.0 1.8 %copy-start.7 = (f32[1,32]{1,0:T(1,128)S(1)}, f32[1,32]{1,0:T(1,128)}, u32[]{:S(2)}) copy-start(f32[1,32]{1,0:T(1,128)} %step_bias.1) | copy-start | bytes 388
  18.0 1.8 %copy-start.8 = (f32[1,32]{1,0:T(1,128)S(1)}, f32[1,32]{1,0:T(1,128)}, u32[]{:S(2)}) copy-start(f32[1,32]{1,0:T(1,128)} %log_rates.1) | copy-start | bytes 388
  82.8 4.2 %copy-start.6 = (f32[1,2048]{1,0:T(1,128)S(1)}, f32[1,2048]{1,0:T(1,128)}, u32[]{:S(2)}) copy-start(f32[1,2048]{1,0:T(1,128)} %gain.1) | copy-start | bytes 24580
  83.2 3.0 %collective-permute-start.3 = (bf16[256,1024]{1,0:T(8,128)(2,1)S(1)}, bf16[256,1024]{1,0:T(8,128)(2,1)S(1)}, u32[]{:S(2)}, u32[]{:S(2)}) collective-permute-start(bf16[256,1024]{1,0:T(8,128)(2,1)S(1)} %carried.1.scanned), channel_id=1, source_target_pairs={{0,4},{4,0},{1,5},{5,1},{2,6},{6,2},{3,7},{7,3},{8,12},{12,8},{9,1... | collective-permute-start | bytes 1572872 | tf_op jit(solution)/shard_map/ppermute | solution.py:310
  84.7 0.8 copy-start
  86.2 0.8 copy-start.2
  87.0 1.0 copy-start.1
  88.0 1.1 copy-start.3
  124.9 15.3 %collective-permute-start.4 = (bf16[256,512]{1,0:T(8,128)(2,1)S(1)}, bf16[256,512]{1,0:T(8,128)(2,1)S(1)}, u32[]{:S(2)}, u32[]{:S(2)}) collective-permute-start(bf16[256,512]{1,0:T(8,128)(2,1)S(1)} %project.5), channel_id=1, source_target_pairs={{0,2},{1,3},{2,0},{3,1},{4,6},{5,7},{6,4},{7,5},{8,10},{9,11},{10,... | collective-permute-start | bytes 786440 | tf_op jit(solution)/shard_map/ppermute | solution.py:327
  131.0 9.3 %collective-permute-start.5 = (bf16[256,512]{1,0:T(8,128)(2,1)S(1)}, bf16[256,512]{1,0:T(8,128)(2,1)S(1)}, u32[]{:S(2)}, u32[]{:S(2)}) collective-permute-start(bf16[256,512]{1,0:T(8,128)(2,1)S(1)} %project.6), channel_id=1, source_target_pairs={{0,1},{1,2},{2,3},{3,0},{4,5},{5,6},{6,7},{7,4},{8,9},{9,10},{10,1... | collective-permute-start | bytes 786440 | tf_op jit(solution)/shard_map/ppermute | solution.py:327
  134.5 7.3 %collective-permute-start.6 = (bf16[256,512]{1,0:T(8,128)(2,1)S(1)}, bf16[256,512]{1,0:T(8,128)(2,1)S(1)}, u32[]{:S(2)}, u32[]{:S(2)}) collective-permute-start(bf16[256,512]{1,0:T(8,128)(2,1)S(1)} %project.7), channel_id=1, source_target_pairs={{0,3},{1,0},{2,1},{3,2},{4,7},{5,4},{6,5},{7,6},{8,11},{9,8},{10,9... | collective-permute-start | bytes 786440 | tf_op jit(solution)/shard_map/ppermute | solution.py:327
  141.9 2.8 %collective-permute-start.7 = (bf16[128,512]{1,0:T(8,128)(2,1)S(1)}, bf16[128,512]{1,0:T(8,128)(2,1)S(1)}, u32[]{:S(2)}, u32[]{:S(2)}) collective-permute-start(bf16[128,512]{1,0:T(8,128)(2,1)S(1)} %get-tuple-element.16), channel_id=1, source_target_pairs={{0,4},{4,0},{1,5},{5,1},{2,6},{6,2},{3,7},{7,3},{8,12},{12,8},{9,1... | collective-permute-start | bytes 393224 | tf_op jit(solution)/shard_map/ppermute | solution.py:337
Sparse Core Ops, SparseCore 0:
  10.1 111.5 all-gather.2

commit v3 on v2

--- a/solution.py
+++ b/solution.py
@@ -1,3 +1,5 @@
+import functools
+
 import jax
 import jax.numpy as jnp
 from jax import lax
@@ -11,16 +13,19 @@
 KCONV = 4
 ROWS = 128
 PAIR = 256
+QUAD = 512
 GCH = 2048
 GCONV = 2560
 GCOLS = 4640
 HALF = 1024
 HEADS = 16
-BLOCK = 512
+BLOCK = 256
 Z, Y, C, T = 8, 4, 2, 4
 CHIPS = Z * Y
 f32, bf16 = jnp.float32, jnp.bfloat16
 MIB = 1 << 20
+QUERY, GROWTH, STATE, LOGS = 1024, 1280, 1408, 2432
+PACK = 2560
 
 
 def params(mib):
@@ -64,8 +69,8 @@
 
 def scan_kernel(
     at, mine, other, rim, taps, bias, step_bias, log_rates,
-    within, keys, growth, send,
-    padded, tap_rows, values, queries, raw, small,
+    pack, send,
+    within, keys, padded, tap_rows, values, queries, raw, small,
 ):
     core = at[0]
     x_at = pl.multiple_of(core * HALF, 128)
@@ -118,7 +123,7 @@
     running = dot(jnp.where(row >= column, 1.0, 0.0), logs, precision=lax.Precision.HIGHEST)
     running_t = running.T
     steps_t = steps.T
-    growth[...] = split_three(jnp.exp(running))
+    pack[:, GROWTH : GROWTH + 128] = split_three(jnp.exp(running))
 
     causal = row[:ROWS, :ROWS] >= column[:ROWS, :ROWS]
     products = []
@@ -152,8 +157,10 @@
         within[ROWS:, c0 : c0 + 256] += entering * dot(from_middle, table)
         weighted = (x * dot(to_end, table)).astype(bf16)
         send[:, c0 : c0 + 256] = dot(keys_t, weighted).astype(bf16)
+        pack[:, c0 : c0 + 256] = within[:, c0 : c0 + 256].astype(bf16)
     send[:, HALF:] = all_logs
-    keys[...] = queries[...]
+    pack[:, STATE:] = send[...]
+    pack[:, QUERY : QUERY + N] = queries[...]
 
 
 def prefix_kernel(got, back, decays):
@@ -165,86 +172,138 @@
         local = got[rows, 0:HALF].astype(f32)
         decay = decays[rows, :]
         second = state * decay[:8] + local[:8]
-        back[rows, :] = jnp.concatenate([state, second], axis=0).astype(bf16)
+        back[rows, :] = jnp.concatenate([state, state], axis=0).astype(bf16)
         state = second * decay[8:] + local[8:]
 
 
-def carried_kernel(within, queries, growth, state, scanned):
+def carried_kernel(at, own, got, own_gate, got_gate, state, gated, packs, gates):
+    gates[lax.rem(at[1], 2)] = own_gate[...]
+    gates[lax.rem(at[1] + 1, 2)] = got_gate[...]
+    packs[lax.rem(at[1], 2)] = own[...]
+    packs[lax.rem(at[1] + 1, 2)] = got[...]
     for c0 in range(0, HALF, 256):
-        carried = dot(queries[...], state[:, c0 : c0 + 256])
-        carried = carried * dot(growth[...], head_table(c0, 256))
-        scanned[:, c0 : c0 + 256] = (within[:, c0 : c0 + 256] + carried).astype(bf16)
-
-
-def norm_kernel(at, scanned, scanned_other, gate, gate_other, gain, normed, whole, gates):
+        table = head_table(c0, 256)
+        first = state[:, c0 : c0 + 256]
+        decay = jnp.exp(dot(packs[0, 0:16, LOGS:], table)[0:1])
+        second = first.astype(f32) * decay
+        second = second + packs[0, :, STATE + c0 : STATE + c0 + 256].astype(f32)
+        for i, before in ((0, first), (1, second.astype(bf16))):
+            carried = dot(packs[i, :, QUERY : QUERY + N], before)
+            carried = carried * dot(packs[i, :, GROWTH : GROWTH + 128], table)
+            scanned = (packs[i, :, c0 : c0 + 256].astype(f32) + carried).astype(bf16)
+            g = gates[i, :, c0 : c0 + 256].astype(f32)
+            result = scanned.astype(f32) * (g * jax.nn.sigmoid(g))
+            gated[i * PAIR : (i + 1) * PAIR, c0 : c0 + 256] = result.astype(bf16)
+
+
+def norm_kernel(at, own, got, gain, normed, whole):
     core = at[0]
-    own_at = pl.multiple_of(core * HALF, 128)
-    other_at = pl.multiple_of((1 - core) * HALF, 128)
-    whole[:, pl.ds(own_at, HALF)] = scanned[...]
-    whole[:, pl.ds(other_at, HALF)] = scanned_other[...]
-    gates[pl.ds(pl.multiple_of(core * ROWS, 128), ROWS), :] = gate[:, 0:GCH]
-    gates[pl.ds(pl.multiple_of((1 - core) * ROWS, 128), ROWS), :] = gate_other[:, 0:GCH]
+    whole[:, pl.ds(pl.multiple_of(core * HALF, 128), HALF)] = own[...]
+    whole[:, pl.ds(pl.multiple_of((1 - core) * HALF, 128), HALF)] = got[...]
 
     def body(i, carry):
-        rows = pl.ds(pl.multiple_of(i * 16, 16), 16)
-        g = gates[rows, :].astype(f32)
-        gated = whole[rows, :].astype(f32) * (g * jax.nn.sigmoid(g))
+        rows = pl.ds(pl.multiple_of(i * 32, 32), 32)
+        gated = whole[rows, :].astype(f32)
         scale = lax.rsqrt(jnp.mean(gated * gated, axis=1, keepdims=True) + 1e-05)
         normed[rows, :] = (gated * scale * gain[...]).astype(bf16)
         return carry
 
-    lax.fori_loop(0, PAIR // 16, body, 0)
-
-
-def project_kernel(at, normed, weight, out, total):
-    step = pl.program_id(0)
-
-    @pl.when(step == 0)
-    def _():
-        total[...] = jnp.zeros_like(total)
-
-    total[...] += dot(normed[...], weight[...])
-
-    @pl.when(step == pl.num_programs(0) - 1)
-    def _():
-        out[...] = total[...].astype(out.dtype)
-
-
-def project(block, normed, weight, dtype):
-    depth = 512
+    lax.fori_loop(0, QUAD // 32, body, 0)
+
+
+def gate_kernel(at, mine, other, gate):
+    core = at[0]
+    columns = pl.ds(pl.multiple_of(core * HALF, 128), HALF)
+    gate[pl.ds(pl.multiple_of(core * ROWS, 128), ROWS), :] = mine[:, columns]
+    gate[pl.ds(pl.multiple_of((1 - core) * ROWS, 128), ROWS), :] = other[:, columns]
+
+
+def pick_kernel(at, weight, own, away):
+    for ref, which in ((own, at[0]), (away, 1 - at[0])):
+        for chip in range(2):
+            for j in range(T):
+                source = pl.multiple_of((j * 4 + chip * 2 + which) * BLOCK, 128)
+                ref[chip, :, j * BLOCK : (j + 1) * BLOCK] = weight[:, pl.ds(source, BLOCK)]
+
+
+def stack_kernel(at, own, got, near, far):
+    chip = lax.rem(at[1], 2)
+    for ref, which in ((own, at[0]), (got, 1 - at[0])):
+        rows = pl.ds(pl.multiple_of(which * 32, 32), 32)
+        near[rows, :] = ref[chip]
+        far[rows, :] = ref[1 - chip]
+
+
+def order_kernel(at, *refs):
+    out = refs[-1]
+    for m, part in enumerate(refs[:-1]):
+        rows = pl.ds(pl.multiple_of(jnp.bitwise_xor(at[1], m) * 64, 64), 64)
+        for j in range(T):
+            out[j, rows, :] = part[:, j * BLOCK : (j + 1) * BLOCK]
+
+
+def project_kernel(at, normed, lower, upper, *outs):
+    total = jnp.zeros((QUAD, BLOCK), f32)
+    for z in range(Z):
+        block = lower[z, 0] if z < Z // 2 else upper[z - Z // 2, 0]
+        total = total + dot(normed[:, z * 256 : (z + 1) * 256], block)
+    for i, out in enumerate(outs):
+
+        @pl.when(pl.program_id(0) == i)
+        def _(out=out):
+            out[...] = total.astype(out.dtype)
+
+
+def project(blocks, normed, weight, dtype):
+    count = blocks.shape[0]
+
+    def all_of(i, at):
+        return (0, 0)
+
     return pl.pallas_call(
         project_kernel,
-        out_shape=jax.ShapeDtypeStruct((PAIR, BLOCK), dtype),
+        out_shape=(shape(QUAD, BLOCK, dtype=dtype),) * count,
         grid_spec=pltpu.PrefetchScalarGridSpec(
             num_scalar_prefetch=1,
-            grid=(GCH // depth,),
+            grid=(count,),
             in_specs=[
-                pl.BlockSpec((PAIR, depth), lambda k, at: (0, k)),
-                pl.BlockSpec((depth, BLOCK), lambda k, at: (k, at[0])),
+                pl.BlockSpec((QUAD, GCH), all_of),
+                pl.BlockSpec((Z // 2, 1, 256, BLOCK), lambda i, at: (0, at[i], 0, 0)),
+                pl.BlockSpec((Z // 2, 1, 256, BLOCK), lambda i, at: (1, at[i], 0, 0)),
             ],
-            out_specs=pl.BlockSpec((PAIR, BLOCK), lambda k, at: (0, 0)),
-            scratch_shapes=[pltpu.VMEM((PAIR, BLOCK), f32)],
+            out_specs=[pl.BlockSpec((QUAD, BLOCK), all_of)] * count,
         ),
         cost_estimate=pl.CostEstimate(
-            flops=2 * PAIR * GCH * BLOCK, bytes_accessed=2 * GCH * BLOCK, transcendentals=0
+            flops=2 * QUAD * GCH * BLOCK * count,
+            bytes_accessed=2 * GCH * BLOCK * count,
+            transcendentals=0,
         ),
         compiler_params=params(52),
         name="project",
-    )(block, normed, weight)
-
-
-def add_kernel(at, own, a, b, c, keep, away):
-    core = at[0]
-    for ref, which in ((keep, core), (away, 1 - core)):
+    )(blocks, normed, weight, weight)
+
+
+def add_kernel(at, own, a, b, c, *parts):
+    for m, part in enumerate(parts):
+        which = lax.rem(jnp.bitwise_xor(at[2], m), 4)
         rows = pl.ds(pl.multiple_of(which * ROWS, 128), ROWS)
         total = own[rows, :] + a[rows, :].astype(f32) + b[rows, :].astype(f32)
-        ref[...] = (total + c[rows, :].astype(f32)).astype(bf16)
-
-
-def join_kernel(at, keep, got, out):
-    core = at[0]
-    out[:, pl.ds(pl.multiple_of(core * BLOCK, 128), BLOCK)] = keep[...]
-    out[:, pl.ds(pl.multiple_of((1 - core) * BLOCK, 128), BLOCK)] = got[...]
+        part[...] = (total + c[rows, :].astype(f32)).astype(bf16)
+
+
+def join_kernel(at, *refs):
+    out = refs[-1]
+    for m, part in enumerate(refs[:-1]):
+        which = lax.rem(jnp.bitwise_xor(at[2], m), 4)
+        out[:, pl.ds(pl.multiple_of(which * BLOCK, 128), BLOCK)] = part[...]
+
+
+def flip(block, m):
+    return lax.ppermute(block, ("y", "c"), [(i, i ^ m) for i in range(Y * C)])
+
+
+def together(*groups):
+    return lax.optimization_barrier(groups)
 
 
 def shape(*dims, dtype=bf16):
@@ -252,7 +311,8 @@
 
 
 def on_device(projected, conv_weight, conv_bias, step_bias, log_rates, norm_gain, out_weight):
-    weight = lax.all_gather(out_weight[0], ("z", "y", "c"), axis=0, tiled=True)
+    core, y, tp = (lax.axis_index(name) for name in ("c", "y", "tp"))
+    at = jnp.stack([core, y, y * C + core]).astype(jnp.int32)
     mine = projected.reshape(ROWS, GCOLS)
     swap = [(0, 1), (1, 0)]
     other = lax.ppermute(mine, "c", swap)
@@ -260,18 +320,50 @@
     all_axes = ("z", "y", "c")
     rim_0 = lax.ppermute(tail, all_axes, [(2 * i + 1, 2 * i + 2) for i in range(CHIPS - 1)])
     rim_1 = lax.ppermute(tail, all_axes, [(2 * i + 1, 2 * i + 3) for i in range(CHIPS - 1)])
-    core, tp = lax.axis_index("c"), lax.axis_index("tp")
     rim = jnp.where(core == 0, rim_0, rim_1)
-    at = core.astype(jnp.int32).reshape(1)
-
-    within, queries, growth, send = pl.pallas_call(
+    own, away = pl.pallas_call(
+        pick_kernel,
+        out_shape=(shape(2, 32, T * BLOCK),) * 2,
+        in_specs=[smem(), vmem()],
+        out_specs=(vmem(),) * 2,
+        compiler_params=params(8),
+        name="pick",
+    )(at, out_weight[0])
+    near, far = pl.pallas_call(
+        stack_kernel,
+        out_shape=(shape(64, T * BLOCK),) * 2,
+        in_specs=[smem(), vmem(), vmem()],
+        out_specs=(vmem(),) * 2,
+        compiler_params=params(8),
+        name="stack",
+    )(at, own, lax.ppermute(away, "c", swap))
+    plane_weight = pl.pallas_call(
+        order_kernel,
+        out_shape=shape(T, 256, BLOCK),
+        in_specs=[smem()] + [vmem()] * 4,
+        out_specs=vmem(),
+        compiler_params=params(8),
+        name="order",
+    )(at, near, flip(far, 2), flip(near, 4), flip(far, 6))
+    gate = pl.pallas_call(
+        gate_kernel,
+        out_shape=shape(PAIR, HALF),
+        in_specs=[smem(), vmem(), vmem()],
+        out_specs=vmem(),
+        compiler_params=params(8),
+        name="gate",
+    )(at, mine, other)
+    gate, other, rim = together(gate, other, rim)
+    got_gate = flip(gate, 2)
+
+    pack, send = pl.pallas_call(
         scan_kernel,
-        out_shape=(
-            shape(PAIR, HALF, dtype=f32), shape(PAIR, N), shape(PAIR, 128), shape(N, HALF + 128),
-        ),
+        out_shape=(shape(PAIR, PACK), shape(N, HALF + 128)),
         in_specs=[smem()] + [vmem()] * 7,
-        out_specs=(vmem(),) * 4,
+        out_specs=(vmem(),) * 2,
         scratch_shapes=[
+            pltpu.VMEM((PAIR, HALF), f32),
+            pltpu.VMEM((PAIR, N), bf16),
             pltpu.VMEM((PAIR + 8, HALF + 2 * N), f32),
             pltpu.VMEM((8, HALF + 2 * N), f32),
             pltpu.VMEM((PAIR, HALF), bf16),
@@ -282,10 +374,14 @@
         cost_estimate=pl.CostEstimate(
             flops=1 << 29, bytes_accessed=5 * MIB, transcendentals=1 << 20
         ),
-        compiler_params=params(32),
+        compiler_params=params(20),
         name="scan",
     )(at, mine, other, rim, conv_weight[0], conv_bias, step_bias, log_rates)
 
+    plane_weight, send, pack, got_gate = together(plane_weight, send, pack, got_gate)
+    weight = lax.all_gather(plane_weight.reshape(T * 256, BLOCK), "z", axis=0, tiled=True)
+    weight = weight.reshape(Z, T, 256, BLOCK)
+    got_pack = flip(pack, 2)
     got = lax.all_to_all(send, ("z", "y"), 0, 0, tiled=True)
     back = pl.pallas_call(
         prefix_kernel,
@@ -298,51 +394,50 @@
         name="prefix",
     )(got)
     state = lax.all_to_all(back, ("z", "y"), 0, 0, tiled=True)
-    scanned = pl.pallas_call(
+    gated = pl.pallas_call(
         carried_kernel,
-        out_shape=shape(PAIR, HALF),
-        in_specs=[vmem()] * 4,
-        out_specs=vmem(),
-        cost_estimate=pl.CostEstimate(flops=1 << 28, bytes_accessed=2 * MIB, transcendentals=0),
+        out_shape=shape(QUAD, HALF),
+        in_specs=[smem()] + [vmem()] * 5,
+        out_specs=vmem(),
+        scratch_shapes=[pltpu.VMEM((2, PAIR, PACK), bf16), pltpu.VMEM((2, PAIR, HALF), bf16)],
+        cost_estimate=pl.CostEstimate(flops=1 << 29, bytes_accessed=4 * MIB, transcendentals=1 << 19),
         compiler_params=params(16),
         name="carried",
-    )(within, queries, growth, state)
-    scanned_other = lax.ppermute(scanned, "c", swap)
-
+    )(at, pack, got_pack, gate, got_gate, state)
     normed = pl.pallas_call(
         norm_kernel,
-        out_shape=shape(PAIR, GCH),
-        in_specs=[smem()] + [vmem()] * 5,
-        out_specs=vmem(),
-        scratch_shapes=[pltpu.VMEM((PAIR, GCH), bf16), pltpu.VMEM((PAIR, GCH), bf16)],
-        cost_estimate=pl.CostEstimate(flops=1 << 23, bytes_accessed=4 * MIB, transcendentals=1 << 19),
-        compiler_params=params(24),
+        out_shape=shape(QUAD, GCH),
+        in_specs=[smem()] + [vmem()] * 3,
+        out_specs=vmem(),
+        scratch_shapes=[pltpu.VMEM((QUAD, GCH), bf16)],
+        cost_estimate=pl.CostEstimate(flops=1 << 23, bytes_accessed=4 * MIB, transcendentals=0),
+        compiler_params=params(12),
         name="norm",
-    )(at, scanned, scanned_other, mine, other, norm_gain)
-
-    shares = []
-    for k in (2, 1, 3):
-        block = (((tp + k) % T) * C + core).astype(jnp.int32).reshape(1)
-        part = project(block, normed, weight, bf16)
-        shares.append(lax.ppermute(part, "tp", [(i, (i + k) % T) for i in range(T)]))
-    own = project((tp * C + core).astype(jnp.int32).reshape(1), normed, weight, f32)
-    keep, away = pl.pallas_call(
+    )(at, gated, lax.ppermute(gated, "c", swap), norm_gain)
+
+    offsets = (2, 1, 3)
+    blocks = lax.rem(tp + jnp.asarray(offsets + (0,), jnp.int32), T).astype(jnp.int32)
+    shares = [
+        lax.ppermute(part, "tp", [(i, (i + k) % T) for i in range(T)])
+        for k, part in zip(offsets, project(blocks[:3], normed, weight, bf16), strict=True)
+    ]
+    (own_share,) = project(blocks[3:], normed, weight, f32)
+    parts = pl.pallas_call(
         add_kernel,
-        out_shape=(shape(ROWS, BLOCK), shape(ROWS, BLOCK)),
+        out_shape=(shape(ROWS, BLOCK),) * 4,
         in_specs=[smem()] + [vmem()] * 4,
-        out_specs=(vmem(), vmem()),
-        compiler_params=params(16),
+        out_specs=(vmem(),) * 4,
+        compiler_params=params(8),
         name="add",
-    )(at, own, *shares)
-    got_half = lax.ppermute(away, "c", swap)
+    )(at, own_share, *shares)
     return pl.pallas_call(
         join_kernel,
-        out_shape=shape(ROWS, C * BLOCK),
-        in_specs=[smem(), vmem(), vmem()],
-        out_specs=vmem(),
-        compiler_params=params(16),
+        out_shape=shape(ROWS, 4 * BLOCK),
+        in_specs=[smem()] + [vmem()] * 4,
+        out_specs=vmem(),
+        compiler_params=params(8),
         name="join",
-    )(at, keep, got_half)
+    )(at, parts[0], *[flip(parts[m], m) for m in (1, 2, 3)])
 
 
 def solution(mesh):

time: 153 us -> 164 us (1.072)
  blocking collectives: 58.4 us -> 0 us
  waiting for transfers between devices: 35.4 us -> 74.6 us
  starting transfers between devices: 16.8 us -> 40.8 us
  Pallas kernels: 20.8 us -> 26.7 us
    all_to_all x2 -> x0, blocking collectives: 58.4 us -> none  [the longest x1 34.9 us: on_device(): got = lax.all_to_all(send, ('z', 'y'), 0, 0, tiled=True)]
    all_to_all x0 -> x2, waiting for transfers between devices: none -> 34.2 us  [the longest x1 21.5 us: on_device(): got = lax.all_to_all(send, ('z', 'y'), 0, 0, tiled=True)]
    ppermute x2 -> x10, waiting for transfers between devices: 1.71 us -> 29 us  [the longest x8 25.4 us: flip(): return lax.ppermute(block, ('y', 'c'), [(i, i ^ m) for i in range(Y * C)])]
    all_gather x1, waiting for transfers between devices: 30.3 us -> 4.22 us  [on_device(): lax.all_gather(plane_weight.reshape(T * 256, BLOCK), 'z', axis=0, tiled=T...]
    all_to_all x0 -> x2, starting transfers between devices: none -> 16.6 us  [the longest x1 11.6 us: on_device(): got = lax.all_to_all(send, ('z', 'y'), 0, 0, tiled=True)]
    ppermute x2 -> x10, starting transfers between devices: 3.24 us -> 10.9 us  [the longest x8 9.54 us: flip(): return lax.ppermute(block, ('y', 'c'), [(i, i ^ m) for i in range(Y * C)])]
    pallas_call x9 -> x11, Pallas kernels: 20.5 us -> 25.6 us  [the longest x2 8.39 us: project(): pl.pallas_call(project_kernel, out_shape=(shape(QUAD, BLOCK, dtype=dtype)...]
    ppermute x3, waiting for transfers between devices: 1.6 us -> 6.16 us  [on_device(): lax.ppermute(part, 'tp', [(i, (i + k) % T) for i in range(T)])]
  transfers between devices with their start and end apart: 9 -> 19, of which waited for: 5 -> 12; matrix products, arithmetic and copies ran while one was open for 2% -> 3% of each run, Pallas kernels for 11% -> 12%
where the time goes in v3:
time: 164 us
  waiting for transfers between devices  74.6 us (45%)
  starting transfers between devices  40.8 us (25%)
  Pallas kernels  26.7 us (16%)
  between operations  13.6 us (8%)
  local copies, waits for them, and re-layouts  7.94 us (5%)
    ppermute x8, waiting for transfers between devices, flip(): return lax.ppermute(block, ('y', 'c'), [(i, i ^ m) for i in range(Y * C)])  25.4 us
    all_to_all x1, waiting for transfers between devices, on_device(): got = lax.all_to_all(send, ('z', 'y'), 0, 0, tiled=True)  21.5 us
    all_to_all x1, waiting for transfers between devices, on_device(): state = lax.all_to_all(back, ('z', 'y'), 0, 0, tiled=True)  12.7 us
    all_to_all x1, starting transfers between devices, on_device(): got = lax.all_to_all(send, ('z', 'y'), 0, 0, tiled=True)  11.6 us
    ppermute x8, starting transfers between devices, flip(): return lax.ppermute(block, ('y', 'c'), [(i, i ^ m) for i in range(Y * C)])  9.54 us
    pallas_call x2, Pallas kernels, project(): pl.pallas_call(project_kernel, out_shape=(shape(QUAD, BLOCK, dtype=dtype)...  8.39 us
    ppermute x3, waiting for transfers between devices, on_device(): lax.ppermute(part, 'tp', [(i, (i + k) % T) for i in range(T)])  6.16 us
    pallas_call x1, Pallas kernels, on_device(): pl.pallas_call(scan_kernel, out_shape=(shape(PAIR, PACK), shape(N, HALF +...  6.04 us
  transfers between devices with their start and end apart: 19, of which 12 were waited for; matrix products, arithmetic and copies ran while one was open for 3% of the time, Pallas kernels for 12%

profile of v3, /device:TPU:1, one launch (start us, length us, event | category | flops | bytes accessed | tf_op | source)
XLA Modules:
  0.0 163.7 jit_solution(13276724764871834377)
XLA Ops:
  6.5 3.2 %collective-permute-start.4 = (bf16[128,4640]{0,1:T(8,128)(2,1)}, bf16[128,4640]{0,1:T(8,128)(2,1)}, u32[]{:S(2)}, u32[]{:S(2)}) collective-permute-start(bf16[128,4640]{0,1:T(8,128)(2,1)} %bitcast.26), channel_id=1, source_target_pairs={{0,4},{4,0},{1,5},{5,1},{2,6},{6,2},{3,7},{7,3},{8,12},{12,8},{9,1... | collective-permute-start | bytes 3563528 | tf_op jit(solution)/shard_map/ppermute | solution.py:318
  9.8 1.7 %copy.10 = bf16[128,1,4640]{2,0,1:T(8,128)(2,1)S(1)} copy(bf16[128,1,4640]{0,2,1:T(8,128)(2,1)} %param.8) | data formatting | bytes 2375680 | tf_op args[0]
  11.5 1.4 collective-permute-start.5
  12.9 3.2 %collective-permute-start.6 = (bf16[8,2560]{1,0:T(8,128)(2,1)S(1)}, bf16[8,2560]{1,0:T(8,128)(2,1)S(1)}, u32[]{:S(2)}, u32[]{:S(2)}) collective-permute-start(bf16[8,2560]{1,0:T(8,128)(2,1)S(1)} %slice.12), channel_id=1, source_target_pairs={{4,12},{12,20},{20,28},{28,36},{36,44},{44,52},{52,60},{60,68},{68... | collective-permute-start | bytes 122888 | tf_op jit(solution)/shard_map/ppermute | solution.py:322
  17.2 1.7 %copy.12.other = bf16[128,4640]{1,0:T(8,128)(2,1)S(1)} copy(bf16[128,4640]{0,1:T(8,128)(2,1)} %collective-permute-done.4) | data formatting | bytes 2375680 | tf_op jit(solution)/shard_map/ppermute | solution.py:318
  19.5 1.8 %collective-permute-start.7 = (bf16[256,1024]{1,0:T(8,128)(2,1)S(1)}, bf16[256,1024]{1,0:T(8,128)(2,1)S(1)}, u32[]{:S(2)}, u32[]{:S(2)}) collective-permute-start(bf16[256,1024]{1,0:T(8,128)(2,1)S(1)} %gate.1.own_gate), channel_id=1, source_target_pairs={{0,8},{4,12},{8,0},{12,4},{16,24},{20,28},{24,16},{28,20},{1,9},{5... | collective-permute-start | bytes 1572872 | tf_op jit(solution)/shard_map/ppermute | solution.py:302
  22.1 1.3 collective-permute-done.got
  24.3 2.6 %collective-permute-start.2 = (bf16[64,1024]{1,0:T(8,128)(2,1)S(1)}, bf16[64,1024]{1,0:T(8,128)(2,1)S(1)}, u32[]{:S(2)}, u32[]{:S(2)}) collective-permute-start(bf16[64,1024]{1,0:T(8,128)(2,1)S(1)} %get-tuple-element.27.refs_0_), channel_id=1, source_target_pairs={{0,16},{4,20},{8,24},{12,28},{16,0},{20,4},{24,8},{28,12},{1,17},{... | collective-permute-start | bytes 393224 | tf_op jit(solution)/shard_map/ppermute | solution.py:302
  27.9 7.8 %collective-permute-done.1.refs_1_ = bf16[64,1024]{1,0:T(8,128)(2,1)S(1)} collective-permute-done((bf16[64,1024]{1,0:T(8,128)(2,1)S(1)}, bf16[64,1024]{1,0:T(8,128)(2,1)S(1)}, u32[]{:S(2)}, u32[]{:S(2)}) %collective-permute-start.1) | collective-permute-done | bytes 131104 | tf_op jit(solution)/shard_map/ppermute | solution.py:302
  35.7 4.0 %collective-permute-done.2.refs_2_ = bf16[64,1024]{1,0:T(8,128)(2,1)S(1)} collective-permute-done((bf16[64,1024]{1,0:T(8,128)(2,1)S(1)}, bf16[64,1024]{1,0:T(8,128)(2,1)S(1)}, u32[]{:S(2)}, u32[]{:S(2)}) %collective-permute-start.2) | collective-permute-done | bytes 131104 | tf_op jit(solution)/shard_map/ppermute | solution.py:302
  39.7 1.4 order.1
  41.1 1.8 %copy.13.other = bf16[128,4640]{1,0:T(8,128)(2,1)S(1)} copy(bf16[128,4640]{0,1:T(8,128)(2,1)} %collective-permute-done.4) | data formatting | bytes 2375680 | tf_op jit(solution)/shard_map/optimization_barrier | solution.py:306
  43.7 6.0 %scan.1 = (bf16[256,2560]{1,0:T(8,128)(2,1)}, bf16[256,1152]{1,0:T(8,128)(2,1)}) custom-call(s32[3]{0:T(128)S(1)} %pad_add_fusion.at, bf16[128,4640]{1,0:T(8,128)(2,1)S(1)} %bitcast.16, bf16[128,4640]{1,0:T(8,128)(2,1)S(1)} %copy.13.other, bf16[8,2560]{1,0:T(8,128)(2,1)S(1)} %broadcast_select_fusion.rim, f32[4,2560]{1,0:T(4,128)S(1)} %bitcast.20, ...), custom_call_target="tpu_custom_call" | custom-call | flops 536870912 | bytes 5242880 | tf_op jit(solution)/shard_map/scan/pallas_call | solution.py:359
  49.8 11.6 %all-to-all-start = ((bf16[32,8,1152]{2,1,0:T(8,128)(2,1)}), bf16[32,8,1152]{2,1,0:T(8,128)(2,1)S(1)}, u32[]{:S(2)}, u32[]{:S(2)}) async-start(bf16[32,8,1152]{2,1,0:T(8,128)(2,1)} %bitcast.7), calls=%async_computation | async-start | bytes 1179648 | tf_op jit(solution)/shard_map/all_to_all | solution.py:385
  61.4 1.3 collective-permute-start.8
  62.7 21.5 %all-to-all-done = bf16[32,8,1152]{2,1,0:T(8,128)(2,1)S(1)} async-done(((bf16[32,8,1152]{2,1,0:T(8,128)(2,1)}), bf16[32,8,1152]{2,1,0:T(8,128)(2,1)S(1)}, u32[]{:S(2)}, u32[]{:S(2)}) %all-to-all-start) | async-done | bytes 589856 | tf_op jit(solution)/shard_map/all_to_all | solution.py:385
  85.3 5.1 %all-to-all-start.1 = ((bf16[32,8,1024]{2,1,0:T(8,128)(2,1)}), bf16[32,8,1024]{2,1,0:T(8,128)(2,1)S(1)}, u32[]{:S(2)}, u32[]{:S(2)}) async-start(bf16[32,8,1024]{2,1,0:T(8,128)(2,1)} %bitcast.9), calls=%async_computation.1 | async-start | bytes 1048576 | tf_op jit(solution)/shard_map/all_to_all | solution.py:396
  90.4 10.0 %collective-permute-done.8.got = bf16[256,2560]{1,0:T(8,128)(2,1)} collective-permute-done((bf16[256,2560]{1,0:T(8,128)(2,1)}, bf16[256,2560]{1,0:T(8,128)(2,1)}, u32[]{:S(2)}, u32[]{:S(2)}) %collective-permute-start.8) | collective-permute-done | bytes 1310752 | tf_op jit(solution)/shard_map/ppermute | solution.py:302
  100.3 12.7 %all-to-all-done.1 = bf16[32,8,1024]{2,1,0:T(8,128)(2,1)S(1)} async-done(((bf16[32,8,1024]{2,1,0:T(8,128)(2,1)}), bf16[32,8,1024]{2,1,0:T(8,128)(2,1)S(1)}, u32[]{:S(2)}, u32[]{:S(2)}) %all-to-all-start.1) | async-done | bytes 524320 | tf_op jit(solution)/shard_map/all_to_all | solution.py:396
  113.1 3.3 %carried.1.own = bf16[512,1024]{1,0:T(8,128)(2,1)S(1)} custom-call(s32[3]{0:T(128)S(1)} %pad_add_fusion.at, bf16[256,2560]{1,0:T(8,128)(2,1)} %get-tuple-element.34.own, bf16[256,2560]{1,0:T(8,128)(2,1)} %collective-permute-done.8.got, bf16[256,1024]{1,0:T(8,128)(2,1)S(1)} %gate.1.own_gate, bf16[256,1024]{1,0:T(8,128)(2,1)S(1)} %collective-permute-done.7.got_gate, ...), custom_call_target="tpu_custom_call" | custom-call | flops 536870912 | bytes 4194304 | tf_op jit(solution)/shard_map/carried/pallas_call | solution.py:397
  117.6 2.3 %collective-permute-done.9.got = bf16[512,1024]{1,0:T(8,128)(2,1)S(1)} collective-permute-done((bf16[512,1024]{1,0:T(8,128)(2,1)S(1)}, bf16[512,1024]{1,0:T(8,128)(2,1)S(1)}, u32[]{:S(2)}, u32[]{:S(2)}) %collective-permute-start.9) | collective-permute-done | bytes 1048608 | tf_op jit(solution)/shard_map/ppermute | solution.py:416
  119.9 2.8 %norm.1.normed = bf16[512,2048]{1,0:T(8,128)(2,1)S(1)} custom-call(s32[3]{0:T(128)S(1)} %pad_add_fusion.at, bf16[512,1024]{1,0:T(8,128)(2,1)S(1)} %carried.1.own, bf16[512,1024]{1,0:T(8,128)(2,1)S(1)} %collective-permute-done.9.got, f32[1,2048]{1,0:T(1,128)S(1)} %copy-done.4), custom_call_target="tpu_custom_call" | custom-call | flops 8388608 | bytes 4194304 | tf_op jit(solution)/shard_map/norm/pallas_call | solution.py:407
  122.7 1.4 copy-done
  124.1 4.2 %all-gather.2.cloned.1.call-done = bf16[8192,256]{1,0:T(8,128)(2,1)} async-done(((bf16[1024,256]{1,0:T(8,128)(2,1)}), bf16[8192,256]{1,0:T(8,128)(2,1)}) %all-gather.2.cloned.1.call-update) | async-done | bytes 4194320 | tf_op jit(solution)/shard_map/all_gather | solution.py:382
  128.3 5.2 %project.3 = (bf16[512,256]{1,0:T(8,128)(2,1)S(1)}, bf16[512,256]{1,0:T(8,128)(2,1)S(1)}, bf16[512,256]{1,0:T(8,128)(2,1)S(1)}) custom-call(s32[3]{0:T(128)S(1)} %bitcast.21, bf16[512,2048]{1,0:T(8,128)(2,1)} %copy-done, bf16[8,4,256,256]{3,2,1,0:T(8,128)(2,1)} %bitcast.22, bf16[8,4,256,256]{3,2,1,0:T(8,128)(2,1)} %bitcast.23), custom_call_target="tpu_custom_call" | custom-call | flops 1610612736 | bytes 3145728 | tf_op jit(solution)/shard_map/project/pallas_call | solution.py:263
  133.5 2.8 %collective-permute-start.10 = (bf16[512,256]{1,0:T(8,128)(2,1)S(1)}, bf16[512,256]{1,0:T(8,128)(2,1)S(1)}, u32[]{:S(2)}, u32[]{:S(2)}) collective-permute-start(bf16[512,256]{1,0:T(8,128)(2,1)S(1)} %get-tuple-element.38), channel_id=1, source_target_pairs={{0,2},{1,3},{2,0},{3,1},{4,6},{5,7},{6,4},{7,5},{8,10},{9,11},{10,... | collective-permute-start | bytes 786440 | tf_op jit(solution)/shard_map/ppermute | solution.py:421
  136.7 2.4 %collective-permute-start.12 = (bf16[512,256]{1,0:T(8,128)(2,1)S(1)}, bf16[512,256]{1,0:T(8,128)(2,1)S(1)}, u32[]{:S(2)}, u32[]{:S(2)}) collective-permute-start(bf16[512,256]{1,0:T(8,128)(2,1)S(1)} %get-tuple-element.40), channel_id=1, source_target_pairs={{0,3},{1,0},{2,1},{3,2},{4,7},{5,4},{6,5},{7,6},{8,11},{9,8},{10,9... | collective-permute-start | bytes 786440 | tf_op jit(solution)/shard_map/ppermute | solution.py:421
  139.6 3.2 %project.2.own = f32[512,256]{1,0:T(8,128)S(1)} custom-call(s32[1]{0:T(128)} %slice.9.at, bf16[512,2048]{1,0:T(8,128)(2,1)} %copy-done, bf16[8,4,256,256]{3,2,1,0:T(8,128)(2,1)} %bitcast.24, bf16[8,4,256,256]{3,2,1,0:T(8,128)(2,1)} %bitcast.25), custom_call_target="tpu_custom_call" | custom-call | flops 536870912 | bytes 1048576 | tf_op jit(solution)/shard_map/project/pallas_call | solution.py:263
  142.8 6.2 %collective-permute-done.11.b = bf16[512,256]{1,0:T(8,128)(2,1)S(1)} collective-permute-done((bf16[512,256]{1,0:T(8,128)(2,1)S(1)}, bf16[512,256]{1,0:T(8,128)(2,1)S(1)}, u32[]{:S(2)}, u32[]{:S(2)}) %collective-permute-start.11) | collective-permute-done | bytes 262176 | tf_op jit(solution)/shard_map/ppermute | solution.py:421
  152.1 1.9 %collective-permute-done.14.refs_2_ = bf16[128,256]{1,0:T(8,128)(2,1)S(1)} collective-permute-done((bf16[128,256]{1,0:T(8,128)(2,1)S(1)}, bf16[128,256]{1,0:T(8,128)(2,1)S(1)}, u32[]{:S(2)}, u32[]{:S(2)}) %collective-permute-start.14) | collective-permute-done | bytes 65568 | tf_op jit(solution)/shard_map/ppermute | solution.py:302
  154.0 1.6 collective-permute-done.15.refs_3_
  155.6 1.3 join.1
  (43 shorter events, 11.4 us)
Async XLA Ops:
  6.5 121.8 %all-gather.2.cloned.1.call-start = ((), (), s32[]{:S(2)}) async-start(), calls=%async_computation.2 | async-start | bytes 4718592 | tf_op jit(solution)/shard_map/all_gather | solution.py:382
  6.5 10.6 %collective-permute-start.4 = (bf16[128,4640]{0,1:T(8,128)(2,1)}, bf16[128,4640]{0,1:T(8,128)(2,1)}, u32[]{:S(2)}, u32[]{:S(2)}) collective-permute-start(bf16[128,4640]{0,1:T(8,128)(2,1)} %bitcast.26), channel_id=1, source_target_pairs={{0,4},{4,0},{1,5},{5,1},{2,6},{6,2},{3,7},{7,3},{8,12},{12,8},{9,1... | collective-permute-start | bytes 3563528 | tf_op jit(solution)/shard_map/ppermute | solution.py:318
  11.5 4.7 %collective-permute-start.5 = (bf16[8,2560]{1,0:T(8,128)(2,1)S(1)}, bf16[8,2560]{1,0:T(8,128)(2,1)S(1)}, u32[]{:S(2)}, u32[]{:S(2)}) collective-permute-start(bf16[8,2560]{1,0:T(8,128)(2,1)S(1)} %slice.12), channel_id=1, source_target_pairs={{4,8},{12,16},{20,24},{28,32},{36,40},{44,48},{52,56},{60,64},{68,... | collective-permute-start | bytes 122888 | tf_op jit(solution)/shard_map/ppermute | solution.py:321
  12.9 4.3 %collective-permute-start.6 = (bf16[8,2560]{1,0:T(8,128)(2,1)S(1)}, bf16[8,2560]{1,0:T(8,128)(2,1)S(1)}, u32[]{:S(2)}, u32[]{:S(2)}) collective-permute-start(bf16[8,2560]{1,0:T(8,128)(2,1)S(1)} %slice.12), channel_id=1, source_target_pairs={{4,12},{12,20},{20,28},{28,36},{36,44},{44,52},{52,60},{60,68},{68... | collective-permute-start | bytes 122888 | tf_op jit(solution)/shard_map/ppermute | solution.py:322
  18.9 2.4 %copy-start.1 = (bf16[1,32,4096]{2,1,0:T(8,128)(2,1)S(1)}, bf16[1,32,4096]{2,1,0:T(8,128)(2,1)}, u32[]{:S(2)}) copy-start(bf16[1,32,4096]{2,1,0:T(8,128)(2,1)} %param.14) | copy-start | bytes 786436
  19.5 30.2 %collective-permute-start.7 = (bf16[256,1024]{1,0:T(8,128)(2,1)S(1)}, bf16[256,1024]{1,0:T(8,128)(2,1)S(1)}, u32[]{:S(2)}, u32[]{:S(2)}) collective-permute-start(bf16[256,1024]{1,0:T(8,128)(2,1)S(1)} %gate.1.own_gate), channel_id=1, source_target_pairs={{0,8},{4,12},{8,0},{12,4},{16,24},{20,28},{24,16},{28,20},{1,9},{5... | collective-permute-start | bytes 1572872 | tf_op jit(solution)/shard_map/ppermute | solution.py:302
  21.9 1.4 collective-permute-start
  24.0 11.8 %collective-permute-start.1 = (bf16[64,1024]{1,0:T(8,128)(2,1)S(1)}, bf16[64,1024]{1,0:T(8,128)(2,1)S(1)}, u32[]{:S(2)}, u32[]{:S(2)}) collective-permute-start(bf16[64,1024]{1,0:T(8,128)(2,1)S(1)} %get-tuple-element.28), channel_id=1, source_target_pairs={{0,8},{4,12},{8,0},{12,4},{16,24},{20,28},{24,16},{28,20},{1,9},{5... | collective-permute-start | bytes 393224 | tf_op jit(solution)/shard_map/ppermute | solution.py:302
  24.3 15.4 %collective-permute-start.2 = (bf16[64,1024]{1,0:T(8,128)(2,1)S(1)}, bf16[64,1024]{1,0:T(8,128)(2,1)S(1)}, u32[]{:S(2)}, u32[]{:S(2)}) collective-permute-start(bf16[64,1024]{1,0:T(8,128)(2,1)S(1)} %get-tuple-element.27.refs_0_), channel_id=1, source_target_pairs={{0,16},{4,20},{8,24},{12,28},{16,0},{20,4},{24,8},{28,12},{1,17},{... | collective-permute-start | bytes 393224 | tf_op jit(solution)/shard_map/ppermute | solution.py:302
  26.9 12.8 %collective-permute-start.3 = (bf16[64,1024]{1,0:T(8,128)(2,1)S(1)}, bf16[64,1024]{1,0:T(8,128)(2,1)S(1)}, u32[]{:S(2)}, u32[]{:S(2)}) collective-permute-start(bf16[64,1024]{1,0:T(8,128)(2,1)S(1)} %get-tuple-element.28), channel_id=1, source_target_pairs={{0,24},{4,28},{8,16},{12,20},{16,8},{20,12},{24,0},{28,4},{1,25},{... | collective-permute-start | bytes 393224 | tf_op jit(solution)/shard_map/ppermute | solution.py:302
  41.1 1.8 %copy-start.3 = (f32[1,2560]{1,0:T(1,128)S(1)}, f32[1,2560]{1,0:T(1,128)}, u32[]{:S(2)}) copy-start(f32[1,2560]{1,0:T(1,128)} %bias.1) | copy-start | bytes 30724
  41.1 1.8 %copy-start.5 = (f32[1,32]{1,0:T(1,128)S(1)}, f32[1,32]{1,0:T(1,128)}, u32[]{:S(2)}) copy-start(f32[1,32]{1,0:T(1,128)} %step_bias.1) | copy-start | bytes 388
  41.1 1.8 %copy-start.6 = (f32[1,32]{1,0:T(1,128)S(1)}, f32[1,32]{1,0:T(1,128)}, u32[]{:S(2)}) copy-start(f32[1,32]{1,0:T(1,128)} %log_rates.1) | copy-start | bytes 388
  42.9 0.8 copy-start.2
  49.8 34.4 %all-to-all-start = ((bf16[32,8,1152]{2,1,0:T(8,128)(2,1)}), bf16[32,8,1152]{2,1,0:T(8,128)(2,1)S(1)}, u32[]{:S(2)}, u32[]{:S(2)}) async-start(bf16[32,8,1152]{2,1,0:T(8,128)(2,1)} %bitcast.7), calls=%async_computation | async-start | bytes 1179648 | tf_op jit(solution)/shard_map/all_to_all | solution.py:385
  61.4 39.0 %collective-permute-start.8 = (bf16[256,2560]{1,0:T(8,128)(2,1)}, bf16[256,2560]{1,0:T(8,128)(2,1)}, u32[]{:S(2)}, u32[]{:S(2)}) collective-permute-start(bf16[256,2560]{1,0:T(8,128)(2,1)} %get-tuple-element.34.own), channel_id=1, source_target_pairs={{0,8},{4,12},{8,0},{12,4},{16,24},{20,28},{24,16},{28,20},{1,9},{5... | collective-permute-start | bytes 3932168 | tf_op jit(solution)/shard_map/ppermute | solution.py:302
  85.3 27.8 %all-to-all-start.1 = ((bf16[32,8,1024]{2,1,0:T(8,128)(2,1)}), bf16[32,8,1024]{2,1,0:T(8,128)(2,1)S(1)}, u32[]{:S(2)}, u32[]{:S(2)}) async-start(bf16[32,8,1024]{2,1,0:T(8,128)(2,1)} %bitcast.9), calls=%async_computation.1 | async-start | bytes 1048576 | tf_op jit(solution)/shard_map/all_to_all | solution.py:396
  113.1 4.6 %copy-start.7 = (s32[4]{0:T(128)S(1)}, s32[4]{0:T(128)}, u32[]{:S(2)}) copy-start(s32[4]{0:T(128)} %constant.22.clone) | copy-start | bytes 52
  113.1 6.8 %copy-start.4 = (f32[1,2048]{1,0:T(1,128)S(1)}, f32[1,2048]{1,0:T(1,128)}, u32[]{:S(2)}) copy-start(f32[1,2048]{1,0:T(1,128)} %gain.1) | copy-start | bytes 24580
  116.4 3.5 %collective-permute-start.9 = (bf16[512,1024]{1,0:T(8,128)(2,1)S(1)}, bf16[512,1024]{1,0:T(8,128)(2,1)S(1)}, u32[]{:S(2)}, u32[]{:S(2)}) collective-permute-start(bf16[512,1024]{1,0:T(8,128)(2,1)S(1)} %carried.1.own), channel_id=1, source_target_pairs={{0,4},{4,0},{1,5},{5,1},{2,6},{6,2},{3,7},{7,3},{8,12},{12,8},{9,1... | collective-permute-start | bytes 3145736 | tf_op jit(solution)/shard_map/ppermute | solution.py:416
  122.7 1.4 copy-start
  133.5 9.3 %collective-permute-start.10 = (bf16[512,256]{1,0:T(8,128)(2,1)S(1)}, bf16[512,256]{1,0:T(8,128)(2,1)S(1)}, u32[]{:S(2)}, u32[]{:S(2)}) collective-permute-start(bf16[512,256]{1,0:T(8,128)(2,1)S(1)} %get-tuple-element.38), channel_id=1, source_target_pairs={{0,2},{1,3},{2,0},{3,1},{4,6},{5,7},{6,4},{7,5},{8,10},{9,11},{10,... | collective-permute-start | bytes 786440 | tf_op jit(solution)/shard_map/ppermute | solution.py:421
  136.3 12.6 %collective-permute-start.11 = (bf16[512,256]{1,0:T(8,128)(2,1)S(1)}, bf16[512,256]{1,0:T(8,128)(2,1)S(1)}, u32[]{:S(2)}, u32[]{:S(2)}) collective-permute-start(bf16[512,256]{1,0:T(8,128)(2,1)S(1)} %get-tuple-element.39), channel_id=1, source_target_pairs={{0,1},{1,2},{2,3},{3,0},{4,5},{5,6},{6,7},{7,4},{8,9},{9,10},{10,1... | collective-permute-start | bytes 786440 | tf_op jit(solution)/shard_map/ppermute | solution.py:421
  136.7 12.3 %collective-permute-start.12 = (bf16[512,256]{1,0:T(8,128)(2,1)S(1)}, bf16[512,256]{1,0:T(8,128)(2,1)S(1)}, u32[]{:S(2)}, u32[]{:S(2)}) collective-permute-start(bf16[512,256]{1,0:T(8,128)(2,1)S(1)} %get-tuple-element.40), channel_id=1, source_target_pairs={{0,3},{1,0},{2,1},{3,2},{4,7},{5,4},{6,5},{7,6},{8,11},{9,8},{10,9... | collective-permute-start | bytes 786440 | tf_op jit(solution)/shard_map/ppermute | solution.py:421
  149.6 2.4 %collective-permute-start.13 = (bf16[128,256]{1,0:T(8,128)(2,1)S(1)}, bf16[128,256]{1,0:T(8,128)(2,1)S(1)}, u32[]{:S(2)}, u32[]{:S(2)}) collective-permute-start(bf16[128,256]{1,0:T(8,128)(2,1)S(1)} %get-tuple-element.42), channel_id=1, source_target_pairs={{0,4},{4,0},{8,12},{12,8},{16,20},{20,16},{24,28},{28,24},{1,5},{5... | collective-permute-start | bytes 196616 | tf_op jit(solution)/shard_map/ppermute | solution.py:302
  150.3 3.7 %collective-permute-start.14 = (bf16[128,256]{1,0:T(8,128)(2,1)S(1)}, bf16[128,256]{1,0:T(8,128)(2,1)S(1)}, u32[]{:S(2)}, u32[]{:S(2)}) collective-permute-start(bf16[128,256]{1,0:T(8,128)(2,1)S(1)} %get-tuple-element.43), channel_id=1, source_target_pairs={{0,8},{4,12},{8,0},{12,4},{16,24},{20,28},{24,16},{28,20},{1,9},{5... | collective-permute-start | bytes 196616 | tf_op jit(solution)/shard_map/ppermute | solution.py:302
  151.5 4.1 %collective-permute-start.15 = (bf16[128,256]{1,0:T(8,128)(2,1)S(1)}, bf16[128,256]{1,0:T(8,128)(2,1)S(1)}, u32[]{:S(2)}, u32[]{:S(2)}) collective-permute-start(bf16[128,256]{1,0:T(8,128)(2,1)S(1)} %get-tuple-element.44), channel_id=1, source_target_pairs={{0,12},{4,8},{8,4},{12,0},{16,28},{20,24},{24,20},{28,16},{1,13},{... | collective-permute-start | bytes 196616 | tf_op jit(solution)/shard_map/ppermute | solution.py:302
Sparse Core Ops, SparseCore 0:
  49.9 78.3 all-gather.1

commit v4 on v2

--- a/solution.py
+++ b/solution.py
@@ -1,3 +1,5 @@
+import functools
+
 import jax
 import jax.numpy as jnp
 from jax import lax
@@ -16,6 +18,8 @@
 GCOLS = 4640
 HALF = 1024
 HEADS = 16
+QUARTER = HALF // 4
+SLICE = N // 8
 BLOCK = 512
 Z, Y, C, T = 8, 4, 2, 4
 CHIPS = Z * Y
@@ -62,9 +66,22 @@
     return jnp.where(hit, 1.0, 0.0).astype(bf16)
 
 
+def three_rows(v):
+    row = lax.broadcasted_iota(jnp.int32, v.shape, 0)
+    high = v.astype(bf16).astype(f32)
+    middle = (v - high).astype(bf16).astype(f32)
+    low = (v - high - middle).astype(bf16).astype(f32)
+    picked = jnp.where(row == 0, high, jnp.where(row == 1, middle, jnp.where(row == 2, low, 0.0)))
+    return picked.astype(bf16)
+
+
+def log_row(rows):
+    return jnp.sum(rows.astype(f32), axis=0, keepdims=True)
+
+
 def scan_kernel(
     at, mine, other, rim, taps, bias, step_bias, log_rates,
-    within, keys, growth, send,
+    within, keys, growth, send_0, send_1, send_2, send_3,
     padded, tap_rows, values, queries, raw, small,
 ):
     core = at[0]
@@ -143,37 +160,65 @@
     to_end = split_three(jnp.exp(end - running) * steps)
     to_middle = split_three(jnp.exp(middle - running[:ROWS]) * steps[:ROWS])
     from_middle = split_three(jnp.exp(running[ROWS:] - middle))
-    all_logs = split_three(jnp.broadcast_to(end, (PAIR, 128)))
+    all_logs = split_three(jnp.broadcast_to(end, (16, 128)))
     keys_t = keys[...].astype(f32).T.astype(bf16)
-    for c0 in range(0, HALF, 256):
-        table = head_table(c0, 256)
-        x = values[:, c0 : c0 + 256].astype(f32)
+    for k, send in enumerate((send_0, send_1, send_2, send_3)):
+        c0 = pl.multiple_of(lax.rem(at[1] + k, Y) * QUARTER, 128)
+        columns = pl.ds(c0, QUARTER)
+        table = head_table(c0, QUARTER)
+        x = values[:, columns].astype(f32)
         entering = dot(across, (x[:ROWS] * dot(to_middle, table)).astype(bf16))
-        within[ROWS:, c0 : c0 + 256] += entering * dot(from_middle, table)
+        within[ROWS:, columns] += entering * dot(from_middle, table)
         weighted = (x * dot(to_end, table)).astype(bf16)
-        send[:, c0 : c0 + 256] = dot(keys_t, weighted).astype(bf16)
-    send[:, HALF:] = all_logs
+        send[0:N, :] = dot(keys_t, weighted).astype(bf16)
+        send[N:, :] = three_rows(dot(all_logs, table))
     keys[...] = queries[...]
 
 
-def prefix_kernel(got, back, decays):
-    for c0 in range(0, HALF, 256):
-        decays[:, c0 : c0 + 256] = jnp.exp(dot(got[:, HALF:], head_table(c0, 256)))
-    state = jnp.zeros((8, HALF), f32)
-    for pair in range(CHIPS // 2):
-        rows = slice(16 * pair, 16 * pair + 16)
-        local = got[rows, 0:HALF].astype(f32)
-        decay = decays[rows, :]
-        second = state * decay[:8] + local[:8]
-        back[rows, :] = jnp.concatenate([state, second], axis=0).astype(bf16)
-        state = second * decay[8:] + local[8:]
-
-
-def carried_kernel(within, queries, growth, state, scanned):
-    for c0 in range(0, HALF, 256):
-        carried = dot(queries[...], state[:, c0 : c0 + 256])
-        carried = carried * dot(growth[...], head_table(c0, 256))
-        scanned[:, c0 : c0 + 256] = (within[:, c0 : c0 + 256] + carried).astype(bf16)
+def in_order(at, parts, ordered):
+    for k, part in enumerate(parts):
+        ordered[lax.rem(at[1] + (Y - k), Y)] = part[...]
+
+
+def plane_kernel(at, part_0, part_1, part_2, part_3, send, ordered):
+    in_order(at, (part_0, part_1, part_2, part_3), ordered)
+    logs = [log_row(ordered[y, N : N + 16, :]) for y in range(Y)]
+    total = ordered[0, 0:N, :].astype(f32)
+    for y in range(1, Y):
+        total = total * jnp.exp(logs[y]) + ordered[y, 0:N, :].astype(f32)
+    rows = three_rows(jnp.broadcast_to(logs[0] + logs[1] + logs[2] + logs[3], (16, QUARTER)))
+    total = total.astype(bf16)
+    for z in range(Z):
+        send[z, 0:SLICE, :] = total[z * SLICE : (z + 1) * SLICE]
+        send[z, SLICE:, :] = rows
+
+
+def prefix_kernel(got, back):
+    state = jnp.zeros((SLICE, QUARTER), f32)
+    for z in range(Z):
+        back[z] = state.astype(bf16)
+        decay = jnp.exp(log_row(got[z, SLICE : SLICE + 16, :]))
+        state = state * decay + got[z, 0:SLICE, :].astype(f32)
+
+
+def chip_kernel(at, before, part_0, part_1, part_2, part_3, send_0, send_1, send_2, send_3, ordered, states):
+    in_order(at, (part_0, part_1, part_2, part_3), ordered)
+    state = before[...].reshape(N, QUARTER).astype(f32)
+    for y in range(Y):
+        states[y] = state.astype(bf16)
+        if y < Y - 1:
+            decay = jnp.exp(log_row(ordered[y, N : N + 16, :]))
+            state = state * decay + ordered[y, 0:N, :].astype(f32)
+    for k, send in enumerate((send_0, send_1, send_2, send_3)):
+        send[...] = states[lax.rem(at[1] + k, Y)]
+
+
+def carried_kernel(at, within, queries, growth, state_0, state_1, state_2, state_3, scanned):
+    for k, state in enumerate((state_0, state_1, state_2, state_3)):
+        c0 = pl.multiple_of(lax.rem(at[1] + (Y - k), Y) * QUARTER, 128)
+        columns = pl.ds(c0, QUARTER)
+        carried = dot(queries[...], state[...]) * dot(growth[...], head_table(c0, QUARTER))
+        scanned[:, columns] = (within[:, columns] + carried).astype(bf16)
 
 
 def norm_kernel(at, scanned, scanned_other, gate, gate_other, gain, normed, whole, gates):
@@ -196,41 +241,41 @@
     lax.fori_loop(0, PAIR // 16, body, 0)
 
 
-def project_kernel(at, normed, weight, out, total):
-    step = pl.program_id(0)
-
-    @pl.when(step == 0)
-    def _():
-        total[...] = jnp.zeros_like(total)
-
-    total[...] += dot(normed[...], weight[...])
-
-    @pl.when(step == pl.num_programs(0) - 1)
-    def _():
-        out[...] = total[...].astype(out.dtype)
-
-
-def project(block, normed, weight, dtype):
-    depth = 512
+def project_kernel(at, normed, weight, *outs):
+    total = dot(normed[...], weight[...])
+    for i, out in enumerate(outs):
+
+        @pl.when(pl.program_id(0) == i)
+        def _(out=out):
+            out[...] = total.astype(out.dtype)
+
+
+def project(blocks, normed, weight, dtype):
+    count = blocks.shape[0]
+
+    def all_of(i, at):
+        return (0, 0)
+
     return pl.pallas_call(
         project_kernel,
-        out_shape=jax.ShapeDtypeStruct((PAIR, BLOCK), dtype),
+        out_shape=(shape(PAIR, BLOCK, dtype=dtype),) * count,
         grid_spec=pltpu.PrefetchScalarGridSpec(
             num_scalar_prefetch=1,
-            grid=(GCH // depth,),
+            grid=(count,),
             in_specs=[
-                pl.BlockSpec((PAIR, depth), lambda k, at: (0, k)),
-                pl.BlockSpec((depth, BLOCK), lambda k, at: (k, at[0])),
+                pl.BlockSpec((PAIR, GCH), all_of),
+                pl.BlockSpec((GCH, BLOCK), lambda i, at: (0, at[i])),
             ],
-            out_specs=pl.BlockSpec((PAIR, BLOCK), lambda k, at: (0, 0)),
-            scratch_shapes=[pltpu.VMEM((PAIR, BLOCK), f32)],
+            out_specs=[pl.BlockSpec((PAIR, BLOCK), all_of)] * count,
         ),
         cost_estimate=pl.CostEstimate(
-            flops=2 * PAIR * GCH * BLOCK, bytes_accessed=2 * GCH * BLOCK, transcendentals=0
+            flops=2 * PAIR * GCH * BLOCK * count,
+            bytes_accessed=2 * GCH * BLOCK * count,
+            transcendentals=0,
         ),
         compiler_params=params(52),
         name="project",
-    )(block, normed, weight)
+    )(blocks, normed, weight)
 
 
 def add_kernel(at, own, a, b, c, keep, away):
@@ -252,6 +297,8 @@
 
 
 def on_device(projected, conv_weight, conv_bias, step_bias, log_rates, norm_gain, out_weight):
+    core, y, z, tp = (lax.axis_index(name) for name in ("c", "y", "z", "tp"))
+    at = jnp.stack([core, y, z, tp]).astype(jnp.int32)
     weight = lax.all_gather(out_weight[0], ("z", "y", "c"), axis=0, tiled=True)
     mine = projected.reshape(ROWS, GCOLS)
     swap = [(0, 1), (1, 0)]
@@ -260,17 +307,15 @@
     all_axes = ("z", "y", "c")
     rim_0 = lax.ppermute(tail, all_axes, [(2 * i + 1, 2 * i + 2) for i in range(CHIPS - 1)])
     rim_1 = lax.ppermute(tail, all_axes, [(2 * i + 1, 2 * i + 3) for i in range(CHIPS - 1)])
-    core, tp = lax.axis_index("c"), lax.axis_index("tp")
     rim = jnp.where(core == 0, rim_0, rim_1)
-    at = core.astype(jnp.int32).reshape(1)
-
-    within, queries, growth, send = pl.pallas_call(
+
+    within, queries, growth, *sends = pl.pallas_call(
         scan_kernel,
         out_shape=(
-            shape(PAIR, HALF, dtype=f32), shape(PAIR, N), shape(PAIR, 128), shape(N, HALF + 128),
-        ),
+            shape(PAIR, HALF, dtype=f32), shape(PAIR, N), shape(PAIR, 128),
+        ) + (shape(N + 16, QUARTER),) * Y,
         in_specs=[smem()] + [vmem()] * 7,
-        out_specs=(vmem(),) * 4,
+        out_specs=(vmem(),) * (3 + Y),
         scratch_shapes=[
             pltpu.VMEM((PAIR + 8, HALF + 2 * N), f32),
             pltpu.VMEM((8, HALF + 2 * N), f32),
@@ -282,32 +327,56 @@
         cost_estimate=pl.CostEstimate(
             flops=1 << 29, bytes_accessed=5 * MIB, transcendentals=1 << 20
         ),
-        compiler_params=params(32),
+        compiler_params=params(20),
         name="scan",
     )(at, mine, other, rim, conv_weight[0], conv_bias, step_bias, log_rates)
 
-    got = lax.all_to_all(send, ("z", "y"), 0, 0, tiled=True)
+    def along_y(parts):
+        moves = [[(i, (i + k) % Y) for i in range(Y)] for k in range(Y)]
+        return [parts[0]] + [lax.ppermute(parts[k], "y", moves[k]) for k in range(1, Y)]
+
+    parts = along_y(sends)
+    plane = pl.pallas_call(
+        plane_kernel,
+        out_shape=shape(Z, SLICE + 16, QUARTER),
+        in_specs=[smem()] + [vmem()] * Y,
+        out_specs=vmem(),
+        scratch_shapes=[pltpu.VMEM((Y, N + 16, QUARTER), bf16)],
+        compiler_params=params(8),
+        name="plane",
+    )(at, *parts)
+    plane = lax.all_to_all(plane, "z", 0, 0, tiled=True)
     back = pl.pallas_call(
         prefix_kernel,
-        out_shape=shape(N, HALF),
+        out_shape=shape(Z, SLICE, QUARTER),
         in_specs=[vmem()],
         out_specs=vmem(),
-        scratch_shapes=[pltpu.VMEM((N, HALF), f32)],
-        cost_estimate=pl.CostEstimate(flops=1 << 26, bytes_accessed=MIB, transcendentals=1 << 18),
-        compiler_params=params(16),
+        compiler_params=params(8),
         name="prefix",
-    )(got)
-    state = lax.all_to_all(back, ("z", "y"), 0, 0, tiled=True)
+    )(plane)
+    before = lax.all_to_all(back, "z", 0, 0, tiled=True)
+    states = pl.pallas_call(
+        chip_kernel,
+        out_shape=(shape(N, QUARTER),) * Y,
+        in_specs=[smem()] + [vmem()] * (1 + Y),
+        out_specs=(vmem(),) * Y,
+        scratch_shapes=[
+            pltpu.VMEM((Y, N + 16, QUARTER), bf16),
+            pltpu.VMEM((Y, N, QUARTER), bf16),
+        ],
+        compiler_params=params(8),
+        name="chip",
+    )(at, before, *parts)
+    states = along_y(states)
     scanned = pl.pallas_call(
         carried_kernel,
         out_shape=shape(PAIR, HALF),
-        in_specs=[vmem()] * 4,
+        in_specs=[smem()] + [vmem()] * (3 + Y),
         out_specs=vmem(),
         cost_estimate=pl.CostEstimate(flops=1 << 28, bytes_accessed=2 * MIB, transcendentals=0),
-        compiler_params=params(16),
+        compiler_params=params(8),
         name="carried",
-    )(within, queries, growth, state)
-    scanned_other = lax.ppermute(scanned, "c", swap)
+    )(at, within, queries, growth, *states)
 
     normed = pl.pallas_call(
         norm_kernel,
@@ -315,34 +384,37 @@
         in_specs=[smem()] + [vmem()] * 5,
         out_specs=vmem(),
         scratch_shapes=[pltpu.VMEM((PAIR, GCH), bf16), pltpu.VMEM((PAIR, GCH), bf16)],
-        cost_estimate=pl.CostEstimate(flops=1 << 23, bytes_accessed=4 * MIB, transcendentals=1 << 19),
-        compiler_params=params(24),
+        cost_estimate=pl.CostEstimate(
+            flops=1 << 23, bytes_accessed=4 * MIB, transcendentals=1 << 19
+        ),
+        compiler_params=params(10),
         name="norm",
-    )(at, scanned, scanned_other, mine, other, norm_gain)
-
-    shares = []
-    for k in (2, 1, 3):
-        block = (((tp + k) % T) * C + core).astype(jnp.int32).reshape(1)
-        part = project(block, normed, weight, bf16)
-        shares.append(lax.ppermute(part, "tp", [(i, (i + k) % T) for i in range(T)]))
-    own = project((tp * C + core).astype(jnp.int32).reshape(1), normed, weight, f32)
+    )(at, scanned, lax.ppermute(scanned, "c", swap), mine, other, norm_gain)
+
+    offsets = (2, 1, 3)
+    places = lax.rem(tp + jnp.asarray(offsets + (0,), jnp.int32), T).astype(jnp.int32)
+    blocks = places * C + core.astype(jnp.int32)
+    shares = [
+        lax.ppermute(part, "tp", [(i, (i + k) % T) for i in range(T)])
+        for k, part in zip(offsets, project(blocks[:3], normed, weight, bf16), strict=True)
+    ]
+    (own_share,) = project(blocks[3:], normed, weight, f32)
     keep, away = pl.pallas_call(
         add_kernel,
         out_shape=(shape(ROWS, BLOCK), shape(ROWS, BLOCK)),
         in_specs=[smem()] + [vmem()] * 4,
         out_specs=(vmem(), vmem()),
-        compiler_params=params(16),
+        compiler_params=params(8),
         name="add",
-    )(at, own, *shares)
-    got_half = lax.ppermute(away, "c", swap)
+    )(at, own_share, *shares)
     return pl.pallas_call(
         join_kernel,
         out_shape=shape(ROWS, C * BLOCK),
         in_specs=[smem(), vmem(), vmem()],
         out_specs=vmem(),
-        compiler_params=params(16),
+        compiler_params=params(8),
         name="join",
-    )(at, keep, got_half)
+    )(at, keep, lax.ppermute(away, "c", swap))
 
 
 def solution(mesh):

time: 153 us -> 152 us (level)
  blocking collectives: 58.4 us -> 33.5 us
  waiting for transfers between devices: 35.4 us -> 55.3 us
  starting transfers between devices: 16.8 us -> 25 us
  local copies, waits for them, and re-layouts: 7.17 us -> 4.06 us
    all_to_all x2, blocking collectives: 58.4 us -> 33.5 us  [the longest x1 22.8 us: on_device(): plane = lax.all_to_all(plane, 'z', 0, 0, tiled=True)]
    ppermute x2 -> x8, waiting for transfers between devices: 1.71 us -> 21.1 us  [the longest x6 18.6 us: along_y(): lax.ppermute(parts[k], 'y', moves[k])]
    ppermute x2 -> x8, starting transfers between devices: 3.24 us -> 11.7 us  [the longest x6 7.98 us: along_y(): lax.ppermute(parts[k], 'y', moves[k])]
    ppermute x3, waiting for transfers between devices: 1.6 us -> 6.46 us  [on_device(): lax.ppermute(part, 'tp', [(i, (i + k) % T) for i in range(T)])]
    all_gather x1, waiting for transfers between devices: 30.3 us -> 26 us  [on_device(): weight = lax.all_gather(out_weight[0], ('z', 'y', 'c'), axis=0, tiled=True)]
    unnamed x19 -> x13, local copies, waits for them, and re-layouts: 5.44 us -> 1.75 us
    pallas_call x6, Pallas kernels: 13.5 us -> 10.7 us  [the longest x2 8.15 us: project(): pl.pallas_call(project_kernel, out_shape=(shape(PAIR, BLOCK, dtype=dtype)...]
  transfers between devices with their start and end apart: 9 -> 15, of which waited for: 5 -> 12; matrix products, arithmetic and copies ran while one was open for 2% -> 3% of each run, Pallas kernels for 11% -> 9%
where the time goes in v4:
time: 152 us
  waiting for transfers between devices  55.3 us (36%)
  blocking collectives  33.5 us (22%)
  starting transfers between devices  25 us (16%)
  Pallas kernels  20.2 us (13%)
  between operations  13.6 us (9%)
  local copies, waits for them, and re-layouts  4.06 us (3%)
    all_gather x1, waiting for transfers between devices, on_device(): weight = lax.all_gather(out_weight[0], ('z', 'y', 'c'), axis=0, tiled=True)  26 us
    all_to_all x1, blocking collectives, on_device(): plane = lax.all_to_all(plane, 'z', 0, 0, tiled=True)  22.8 us
    ppermute x6, waiting for transfers between devices, along_y(): lax.ppermute(parts[k], 'y', moves[k])  18.6 us
    all_to_all x1, blocking collectives, on_device(): before = lax.all_to_all(back, 'z', 0, 0, tiled=True)  10.8 us
    pallas_call x2, Pallas kernels, project(): pl.pallas_call(project_kernel, out_shape=(shape(PAIR, BLOCK, dtype=dtype)...  8.15 us
    ppermute x6, starting transfers between devices, along_y(): lax.ppermute(parts[k], 'y', moves[k])  7.98 us
    ppermute x3, waiting for transfers between devices, on_device(): lax.ppermute(part, 'tp', [(i, (i + k) % T) for i in range(T)])  6.46 us
    ppermute x3, starting transfers between devices, on_device(): lax.ppermute(part, 'tp', [(i, (i + k) % T) for i in range(T)])  5.46 us
  transfers between devices with their start and end apart: 15, of which 12 were waited for; matrix products, arithmetic and copies ran while one was open for 3% of the time, Pallas kernels for 9%

profile of v4, /device:TPU:1, one launch (start us, length us, event | category | flops | bytes accessed | tf_op | source)
XLA Modules:
  0.0 151.8 jit_solution(1900295580796842318)
XLA Ops:
  7.3 3.3 %collective-permute-start = (bf16[128,4640]{0,1:T(8,128)(2,1)}, bf16[128,4640]{0,1:T(8,128)(2,1)}, u32[]{:S(2)}, u32[]{:S(2)}) collective-permute-start(bf16[128,4640]{0,1:T(8,128)(2,1)} %bitcast.16), channel_id=1, source_target_pairs={{0,4},{4,0},{1,5},{5,1},{2,6},{6,2},{3,7},{7,3},{8,12},{12,8},{9,1... | collective-permute-start | bytes 3563528 | tf_op jit(solution)/shard_map/ppermute | solution.py:305
  10.6 1.7 %copy.10 = bf16[128,1,4640]{2,0,1:T(8,128)(2,1)S(1)} copy(bf16[128,1,4640]{0,2,1:T(8,128)(2,1)} %param.8) | data formatting | bytes 2375680 | tf_op args[0]
  12.3 1.4 collective-permute-start.1
  13.7 3.2 %collective-permute-start.2 = (bf16[8,2560]{1,0:T(8,128)(2,1)S(1)}, bf16[8,2560]{1,0:T(8,128)(2,1)S(1)}, u32[]{:S(2)}, u32[]{:S(2)}) collective-permute-start(bf16[8,2560]{1,0:T(8,128)(2,1)S(1)} %slice.12), channel_id=1, source_target_pairs={{4,12},{12,20},{20,28},{28,36},{36,44},{44,52},{52,60},{60,68},{68... | collective-permute-start | bytes 122888 | tf_op jit(solution)/shard_map/ppermute | solution.py:309
  17.0 1.0 collective-permute-done.2
  18.1 1.7 %copy.12.other.gate_other = bf16[128,4640]{1,0:T(8,128)(2,1)S(1)} copy(bf16[128,4640]{0,1:T(8,128)(2,1)} %collective-permute-done) | data formatting | bytes 2375680 | tf_op jit(solution)/shard_map/ppermute | solution.py:305
  19.8 4.7 %scan.1 = (f32[256,1024]{1,0:T(8,128)S(1)}, bf16[256,256]{1,0:T(8,128)(2,1)S(1)}, bf16[256,128]{1,0:T(8,128)(2,1)S(1)}, bf16[272,256]{1,0:T(8,128)(2,1)S(1)}, bf...) custom-call(s32[4]{0:T(128)S(1)} %pad_add_fusion.at, ...), custom_call_target="tpu_custom_call" | custom-call | flops 536870912 | bytes 5242880 | tf_op jit(solution)/shard_map/scan/pallas_call | solution.py:312
  24.6 1.8 %collective-permute-start.3 = (bf16[272,256]{1,0:T(8,128)(2,1)S(1)}, bf16[272,256]{1,0:T(8,128)(2,1)S(1)}, u32[]{:S(2)}, u32[]{:S(2)}) collective-permute-start(bf16[272,256]{1,0:T(8,128)(2,1)S(1)} %get-tuple-element.25), channel_id=1, source_target_pairs={{0,8},{8,16},{16,24},{24,0},{1,9},{9,17},{17,25},{25,1},{2,10},{10... | collective-permute-start | bytes 417800 | tf_op jit(solution)/shard_map/ppermute | solution.py:336
  26.4 2.6 %collective-permute-start.4 = (bf16[272,256]{1,0:T(8,128)(2,1)S(1)}, bf16[272,256]{1,0:T(8,128)(2,1)S(1)}, u32[]{:S(2)}, u32[]{:S(2)}) collective-permute-start(bf16[272,256]{1,0:T(8,128)(2,1)S(1)} %get-tuple-element.26), channel_id=1, source_target_pairs={{0,16},{8,24},{16,0},{24,8},{1,17},{9,25},{17,1},{25,9},{2,18},{10... | collective-permute-start | bytes 417800 | tf_op jit(solution)/shard_map/ppermute | solution.py:336
  29.0 0.8 collective-permute-start.5
  29.8 3.7 %collective-permute-done.3.part_1 = bf16[272,256]{1,0:T(8,128)(2,1)S(1)} collective-permute-done((bf16[272,256]{1,0:T(8,128)(2,1)S(1)}, bf16[272,256]{1,0:T(8,128)(2,1)S(1)}, u32[]{:S(2)}, u32[]{:S(2)}) %collective-permute-start.3) | collective-permute-done | bytes 139296 | tf_op jit(solution)/shard_map/ppermute | solution.py:336
  33.5 2.4 %collective-permute-done.4.part_2 = bf16[272,256]{1,0:T(8,128)(2,1)S(1)} collective-permute-done((bf16[272,256]{1,0:T(8,128)(2,1)S(1)}, bf16[272,256]{1,0:T(8,128)(2,1)S(1)}, u32[]{:S(2)}, u32[]{:S(2)}) %collective-permute-start.4) | collective-permute-done | bytes 139296 | tf_op jit(solution)/shard_map/ppermute | solution.py:336
  36.9 22.8 %all_to_all.10.got = bf16[8,48,256]{2,1,0:T(8,128)(2,1)S(1)} all-to-all(bf16[8,48,256]{2,1,0:T(8,128)(2,1)S(1)} %plane.1), channel_id=1, replica_groups=mesh['z'=8,'y'=4,'c'=2,'tp'=4] {'z'}, dimensions={0} | all-to-all | bytes 393216 | tf_op jit(solution)/shard_map/all_to_all | solution.py:348
  59.7 10.8 %all_to_all.11.before = bf16[8,32,256]{2,1,0:T(8,128)(2,1)S(1)} all-to-all(bf16[8,32,256]{2,1,0:T(8,128)(2,1)S(1)} %prefix.1), channel_id=1, replica_groups=mesh['z'=8,'y'=4,'c'=2,'tp'=4] {'z'}, dimensions={0} | all-to-all | bytes 262144 | tf_op jit(solution)/shard_map/all_to_all | solution.py:357
  70.5 0.8 chip.1
  71.4 1.9 %collective-permute-start.7 = (bf16[256,256]{1,0:T(8,128)(2,1)S(1)}, bf16[256,256]{1,0:T(8,128)(2,1)S(1)}, u32[]{:S(2)}, u32[]{:S(2)}) collective-permute-start(bf16[256,256]{1,0:T(8,128)(2,1)S(1)} %get-tuple-element.30), channel_id=1, source_target_pairs={{0,16},{8,24},{16,0},{24,8},{1,17},{9,25},{17,1},{25,9},{2,18},{10... | collective-permute-start | bytes 393224 | tf_op jit(solution)/shard_map/ppermute | solution.py:336
  73.3 0.8 collective-permute-start.8
  74.0 6.5 %collective-permute-done.6.state_1 = bf16[256,256]{1,0:T(8,128)(2,1)S(1)} collective-permute-done((bf16[256,256]{1,0:T(8,128)(2,1)S(1)}, bf16[256,256]{1,0:T(8,128)(2,1)S(1)}, u32[]{:S(2)}, u32[]{:S(2)}) %collective-permute-start.6) | collective-permute-done | bytes 131104 | tf_op jit(solution)/shard_map/ppermute | solution.py:336
  80.5 4.3 %collective-permute-done.7.state_2 = bf16[256,256]{1,0:T(8,128)(2,1)S(1)} collective-permute-done((bf16[256,256]{1,0:T(8,128)(2,1)S(1)}, bf16[256,256]{1,0:T(8,128)(2,1)S(1)}, u32[]{:S(2)}, u32[]{:S(2)}) %collective-permute-start.7) | collective-permute-done | bytes 131104 | tf_op jit(solution)/shard_map/ppermute | solution.py:336
  84.8 1.5 %collective-permute-done.8.state_3 = bf16[256,256]{1,0:T(8,128)(2,1)S(1)} collective-permute-done((bf16[256,256]{1,0:T(8,128)(2,1)S(1)}, bf16[256,256]{1,0:T(8,128)(2,1)S(1)}, u32[]{:S(2)}, u32[]{:S(2)}) %collective-permute-start.8) | collective-permute-done | bytes 131104 | tf_op jit(solution)/shard_map/ppermute | solution.py:336
  86.3 1.0 carried.1.scanned
  87.3 3.1 %collective-permute-start.9 = (bf16[256,1024]{1,0:T(8,128)(2,1)S(1)}, bf16[256,1024]{1,0:T(8,128)(2,1)S(1)}, u32[]{:S(2)}, u32[]{:S(2)}) collective-permute-start(bf16[256,1024]{1,0:T(8,128)(2,1)S(1)} %carried.1.scanned), channel_id=1, source_target_pairs={{0,4},{4,0},{1,5},{5,1},{2,6},{6,2},{3,7},{7,3},{8,12},{12,8},{9,1... | collective-permute-start | bytes 1572872 | tf_op jit(solution)/shard_map/ppermute | solution.py:392
  90.4 1.5 %collective-permute-done.9.scanned_other = bf16[256,1024]{1,0:T(8,128)(2,1)S(1)} collective-permute-done((bf16[256,1024]{1,0:T(8,128)(2,1)S(1)}, bf16[256,1024]{1,0:T(8,128)(2,1)S(1)}, u32[]{:S(2)}, u32[]{:S(2)}) %collective-permute-start.9) | collective-permute-done | bytes 524320 | tf_op jit(solution)/shard_map/ppermute | solution.py:392
  91.9 2.8 %norm.1.normed = bf16[256,2048]{1,0:T(8,128)(2,1)S(1)} custom-call(s32[4]{0:T(128)S(1)} %pad_add_fusion.at, bf16[256,1024]{1,0:T(8,128)(2,1)S(1)} %carried.1.scanned, bf16[256,1024]{1,0:T(8,128)(2,1)S(1)} %collective-permute-done.9.scanned_other, bf16[128,4640]{1,0:T(8,128)(2,1)S(1)} %bitcast.11, bf16[128,4640]{1,0:T(8,128)(2,1)S(1)} %copy.12.other.gate_other, ...), custom_call_target="tpu_custom_call" | custom-call | flops 8388608 | bytes 4194304 | tf_op jit(solution)/shard_map/norm/pallas_call | solution.py:381
  94.7 26.0 %all-gather.3.cloned.1.call-done = bf16[1,2048,4096]{2,1,0:T(8,128)(2,1)} async-done(((bf16[1,32,4096]{2,1,0:T(8,128)(2,1)}), bf16[1,2048,4096]{2,1,0:T(8,128)(2,1)}) %all-gather.3.cloned.1.call-update) | async-done | bytes 16777232 | tf_op jit(solution)/shard_map/all_gather | solution.py:302
  120.7 5.2 %project.3 = (bf16[256,512]{1,0:T(8,128)(2,1)S(1)}, bf16[256,512]{1,0:T(8,128)(2,1)S(1)}, bf16[256,512]{1,0:T(8,128)(2,1)S(1)}) custom-call(s32[3]{0:T(128)S(1)} %bitcast.13, bf16[256,2048]{1,0:T(8,128)(2,1)S(1)} %norm.1.normed, bf16[2048,4096]{1,0:T(8,128)(2,1)} %bitcast.14), custom_call_target="tpu_custom_call" | custom-call | flops 1610612736 | bytes 6291456 | tf_op jit(solution)/shard_map/project/pallas_call | solution.py:259
  126.0 2.8 %collective-permute-start.10 = (bf16[256,512]{1,0:T(8,128)(2,1)S(1)}, bf16[256,512]{1,0:T(8,128)(2,1)S(1)}, u32[]{:S(2)}, u32[]{:S(2)}) collective-permute-start(bf16[256,512]{1,0:T(8,128)(2,1)S(1)} %get-tuple-element.32), channel_id=1, source_target_pairs={{0,2},{1,3},{2,0},{3,1},{4,6},{5,7},{6,4},{7,5},{8,10},{9,11},{10,... | collective-permute-start | bytes 786440 | tf_op jit(solution)/shard_map/ppermute | solution.py:398
  129.0 2.4 %collective-permute-start.12 = (bf16[256,512]{1,0:T(8,128)(2,1)S(1)}, bf16[256,512]{1,0:T(8,128)(2,1)S(1)}, u32[]{:S(2)}, u32[]{:S(2)}) collective-permute-start(bf16[256,512]{1,0:T(8,128)(2,1)S(1)} %get-tuple-element.34), channel_id=1, source_target_pairs={{0,3},{1,0},{2,1},{3,2},{4,7},{5,4},{6,5},{7,6},{8,11},{9,8},{10,9... | collective-permute-start | bytes 786440 | tf_op jit(solution)/shard_map/ppermute | solution.py:398
  132.0 2.9 %project.2.own = f32[256,512]{1,0:T(8,128)S(1)} custom-call(s32[1]{0:T(128)} %slice.9.at, bf16[256,2048]{1,0:T(8,128)(2,1)S(1)} %norm.1.normed, bf16[2048,4096]{1,0:T(8,128)(2,1)} %bitcast.15), custom_call_target="tpu_custom_call" | custom-call | flops 536870912 | bytes 2097152 | tf_op jit(solution)/shard_map/project/pallas_call | solution.py:259
  135.3 6.2 %collective-permute-done.11.b = bf16[256,512]{1,0:T(8,128)(2,1)S(1)} collective-permute-done((bf16[256,512]{1,0:T(8,128)(2,1)S(1)}, bf16[256,512]{1,0:T(8,128)(2,1)S(1)}, u32[]{:S(2)}, u32[]{:S(2)}) %collective-permute-start.11) | collective-permute-done | bytes 262176 | tf_op jit(solution)/shard_map/ppermute | solution.py:398
  142.7 1.0 collective-permute-done.13.got
  143.7 1.3 join.1
  (30 shorter events, 4.5 us)
Async XLA Ops:
  6.5 114.2 %all-gather.3.cloned.1.call-start = ((), (), s32[]{:S(2)}) async-start(), calls=%async_computation.2 | async-start | bytes 17039360 | tf_op jit(solution)/shard_map/all_gather | solution.py:302
  7.3 10.8 %collective-permute-start = (bf16[128,4640]{0,1:T(8,128)(2,1)}, bf16[128,4640]{0,1:T(8,128)(2,1)}, u32[]{:S(2)}, u32[]{:S(2)}) collective-permute-start(bf16[128,4640]{0,1:T(8,128)(2,1)} %bitcast.16), channel_id=1, source_target_pairs={{0,4},{4,0},{1,5},{5,1},{2,6},{6,2},{3,7},{7,3},{8,12},{12,8},{9,1... | collective-permute-start | bytes 3563528 | tf_op jit(solution)/shard_map/ppermute | solution.py:305
  12.3 4.7 %collective-permute-start.1 = (bf16[8,2560]{1,0:T(8,128)(2,1)S(1)}, bf16[8,2560]{1,0:T(8,128)(2,1)S(1)}, u32[]{:S(2)}, u32[]{:S(2)}) collective-permute-start(bf16[8,2560]{1,0:T(8,128)(2,1)S(1)} %slice.12), channel_id=1, source_target_pairs={{4,8},{12,16},{20,24},{28,32},{36,40},{44,48},{52,56},{60,64},{68,... | collective-permute-start | bytes 122888 | tf_op jit(solution)/shard_map/ppermute | solution.py:308
  13.7 4.3 %collective-permute-start.2 = (bf16[8,2560]{1,0:T(8,128)(2,1)S(1)}, bf16[8,2560]{1,0:T(8,128)(2,1)S(1)}, u32[]{:S(2)}, u32[]{:S(2)}) collective-permute-start(bf16[8,2560]{1,0:T(8,128)(2,1)S(1)} %slice.12), channel_id=1, source_target_pairs={{4,12},{12,20},{20,28},{28,36},{36,44},{44,52},{52,60},{60,68},{68... | collective-permute-start | bytes 122888 | tf_op jit(solution)/shard_map/ppermute | solution.py:309
  18.0 1.8 %copy-start = (f32[1,4,2560]{2,1,0:T(4,128)S(1)}, f32[1,4,2560]{2,1,0:T(4,128)}, u32[]{:S(2)}) copy-start(f32[1,4,2560]{2,1,0:T(4,128)} %param.9) | copy-start | bytes 122884
  18.0 1.8 %copy-start.1 = (f32[1,2560]{1,0:T(1,128)S(1)}, f32[1,2560]{1,0:T(1,128)}, u32[]{:S(2)}) copy-start(f32[1,2560]{1,0:T(1,128)} %bias.1) | copy-start | bytes 30724
  18.0 1.8 %copy-start.3 = (f32[1,32]{1,0:T(1,128)S(1)}, f32[1,32]{1,0:T(1,128)}, u32[]{:S(2)}) copy-start(f32[1,32]{1,0:T(1,128)} %step_bias.1) | copy-start | bytes 388
  18.0 1.8 %copy-start.4 = (f32[1,32]{1,0:T(1,128)S(1)}, f32[1,32]{1,0:T(1,128)}, u32[]{:S(2)}) copy-start(f32[1,32]{1,0:T(1,128)} %log_rates.1) | copy-start | bytes 388
  24.6 8.9 %collective-permute-start.3 = (bf16[272,256]{1,0:T(8,128)(2,1)S(1)}, bf16[272,256]{1,0:T(8,128)(2,1)S(1)}, u32[]{:S(2)}, u32[]{:S(2)}) collective-permute-start(bf16[272,256]{1,0:T(8,128)(2,1)S(1)} %get-tuple-element.25), channel_id=1, source_target_pairs={{0,8},{8,16},{16,24},{24,0},{1,9},{9,17},{17,25},{25,1},{2,10},{10... | collective-permute-start | bytes 417800 | tf_op jit(solution)/shard_map/ppermute | solution.py:336
  26.4 9.5 %collective-permute-start.4 = (bf16[272,256]{1,0:T(8,128)(2,1)S(1)}, bf16[272,256]{1,0:T(8,128)(2,1)S(1)}, u32[]{:S(2)}, u32[]{:S(2)}) collective-permute-start(bf16[272,256]{1,0:T(8,128)(2,1)S(1)} %get-tuple-element.26), channel_id=1, source_target_pairs={{0,16},{8,24},{16,0},{24,8},{1,17},{9,25},{17,1},{25,9},{2,18},{10... | collective-permute-start | bytes 417800 | tf_op jit(solution)/shard_map/ppermute | solution.py:336
  29.0 7.1 %collective-permute-start.5 = (bf16[272,256]{1,0:T(8,128)(2,1)S(1)}, bf16[272,256]{1,0:T(8,128)(2,1)S(1)}, u32[]{:S(2)}, u32[]{:S(2)}) collective-permute-start(bf16[272,256]{1,0:T(8,128)(2,1)S(1)} %get-tuple-element.27), channel_id=1, source_target_pairs={{0,24},{8,0},{16,8},{24,16},{1,25},{9,1},{17,9},{25,17},{2,26},{10... | collective-permute-start | bytes 417800 | tf_op jit(solution)/shard_map/ppermute | solution.py:336
  71.2 19.1 %copy-start.5 = (s32[4]{0:T(128)S(1)}, s32[4]{0:T(128)}, u32[]{:S(2)}) copy-start(s32[4]{0:T(128)} %constant.27.clone) | copy-start | bytes 52
  71.3 20.6 %copy-start.2 = (f32[1,2048]{1,0:T(1,128)S(1)}, f32[1,2048]{1,0:T(1,128)}, u32[]{:S(2)}) copy-start(f32[1,2048]{1,0:T(1,128)} %gain.1) | copy-start | bytes 24580
  71.3 9.3 %collective-permute-start.6 = (bf16[256,256]{1,0:T(8,128)(2,1)S(1)}, bf16[256,256]{1,0:T(8,128)(2,1)S(1)}, u32[]{:S(2)}, u32[]{:S(2)}) collective-permute-start(bf16[256,256]{1,0:T(8,128)(2,1)S(1)} %get-tuple-element.29), channel_id=1, source_target_pairs={{0,8},{8,16},{16,24},{24,0},{1,9},{9,17},{17,25},{25,1},{2,10},{10... | collective-permute-start | bytes 393224 | tf_op jit(solution)/shard_map/ppermute | solution.py:336
  71.4 13.4 %collective-permute-start.7 = (bf16[256,256]{1,0:T(8,128)(2,1)S(1)}, bf16[256,256]{1,0:T(8,128)(2,1)S(1)}, u32[]{:S(2)}, u32[]{:S(2)}) collective-permute-start(bf16[256,256]{1,0:T(8,128)(2,1)S(1)} %get-tuple-element.30), channel_id=1, source_target_pairs={{0,16},{8,24},{16,0},{24,8},{1,17},{9,25},{17,1},{25,9},{2,18},{10... | collective-permute-start | bytes 393224 | tf_op jit(solution)/shard_map/ppermute | solution.py:336
  73.3 13.0 %collective-permute-start.8 = (bf16[256,256]{1,0:T(8,128)(2,1)S(1)}, bf16[256,256]{1,0:T(8,128)(2,1)S(1)}, u32[]{:S(2)}, u32[]{:S(2)}) collective-permute-start(bf16[256,256]{1,0:T(8,128)(2,1)S(1)} %get-tuple-element.31), channel_id=1, source_target_pairs={{0,24},{8,0},{16,8},{24,16},{1,25},{9,1},{17,9},{25,17},{2,26},{10... | collective-permute-start | bytes 393224 | tf_op jit(solution)/shard_map/ppermute | solution.py:336
  87.3 4.6 %collective-permute-start.9 = (bf16[256,1024]{1,0:T(8,128)(2,1)S(1)}, bf16[256,1024]{1,0:T(8,128)(2,1)S(1)}, u32[]{:S(2)}, u32[]{:S(2)}) collective-permute-start(bf16[256,1024]{1,0:T(8,128)(2,1)S(1)} %carried.1.scanned), channel_id=1, source_target_pairs={{0,4},{4,0},{1,5},{5,1},{2,6},{6,2},{3,7},{7,3},{8,12},{12,8},{9,1... | collective-permute-start | bytes 1572872 | tf_op jit(solution)/shard_map/ppermute | solution.py:392
  126.0 9.3 %collective-permute-start.10 = (bf16[256,512]{1,0:T(8,128)(2,1)S(1)}, bf16[256,512]{1,0:T(8,128)(2,1)S(1)}, u32[]{:S(2)}, u32[]{:S(2)}) collective-permute-start(bf16[256,512]{1,0:T(8,128)(2,1)S(1)} %get-tuple-element.32), channel_id=1, source_target_pairs={{0,2},{1,3},{2,0},{3,1},{4,6},{5,7},{6,4},{7,5},{8,10},{9,11},{10,... | collective-permute-start | bytes 786440 | tf_op jit(solution)/shard_map/ppermute | solution.py:398
  128.7 12.7 %collective-permute-start.11 = (bf16[256,512]{1,0:T(8,128)(2,1)S(1)}, bf16[256,512]{1,0:T(8,128)(2,1)S(1)}, u32[]{:S(2)}, u32[]{:S(2)}) collective-permute-start(bf16[256,512]{1,0:T(8,128)(2,1)S(1)} %get-tuple-element.33), channel_id=1, source_target_pairs={{0,1},{1,2},{2,3},{3,0},{4,5},{5,6},{6,7},{7,4},{8,9},{9,10},{10,1... | collective-permute-start | bytes 786440 | tf_op jit(solution)/shard_map/ppermute | solution.py:398
  129.0 12.4 %collective-permute-start.12 = (bf16[256,512]{1,0:T(8,128)(2,1)S(1)}, bf16[256,512]{1,0:T(8,128)(2,1)S(1)}, u32[]{:S(2)}, u32[]{:S(2)}) collective-permute-start(bf16[256,512]{1,0:T(8,128)(2,1)S(1)} %get-tuple-element.34), channel_id=1, source_target_pairs={{0,3},{1,0},{2,1},{3,2},{4,7},{5,4},{6,5},{7,6},{8,11},{9,8},{10,9... | collective-permute-start | bytes 786440 | tf_op jit(solution)/shard_map/ppermute | solution.py:398
  142.1 1.6 %collective-permute-start.13 = (bf16[128,512]{1,0:T(8,128)(2,1)S(1)}, bf16[128,512]{1,0:T(8,128)(2,1)S(1)}, u32[]{:S(2)}, u32[]{:S(2)}) collective-permute-start(bf16[128,512]{1,0:T(8,128)(2,1)S(1)} %get-tuple-element.36), channel_id=1, source_target_pairs={{0,4},{4,0},{1,5},{5,1},{2,6},{6,2},{3,7},{7,3},{8,12},{12,8},{9,1... | collective-permute-start | bytes 393224 | tf_op jit(solution)/shard_map/ppermute | solution.py:417
Sparse Core Ops, SparseCore 0:
  10.1 110.5 all-gather.2

commit v5 on v4

--- a/solution.py
+++ b/solution.py
@@ -20,7 +20,8 @@
 HEADS = 16
 QUARTER = HALF // 4
 SLICE = N // 8
-BLOCK = 512
+COLUMNS = 1024
+WIDE = 512
 Z, Y, C, T = 8, 4, 2, 4
 CHIPS = Z * Y
 f32, bf16 = jnp.float32, jnp.bfloat16
@@ -221,75 +222,63 @@
         scanned[:, columns] = (within[:, columns] + carried).astype(bf16)
 
 
-def norm_kernel(at, scanned, scanned_other, gate, gate_other, gain, normed, whole, gates):
+def split_kernel(at, scanned, keep, away):
+    for ref, which in ((keep, at[0]), (away, 1 - at[0])):
+        ref[...] = scanned[pl.ds(pl.multiple_of(which * ROWS, 128), ROWS), :]
+
+
+def norm_kernel(at, keep, got, gate, gain, normed, whole):
     core = at[0]
-    own_at = pl.multiple_of(core * HALF, 128)
-    other_at = pl.multiple_of((1 - core) * HALF, 128)
-    whole[:, pl.ds(own_at, HALF)] = scanned[...]
-    whole[:, pl.ds(other_at, HALF)] = scanned_other[...]
-    gates[pl.ds(pl.multiple_of(core * ROWS, 128), ROWS), :] = gate[:, 0:GCH]
-    gates[pl.ds(pl.multiple_of((1 - core) * ROWS, 128), ROWS), :] = gate_other[:, 0:GCH]
+    whole[:, pl.ds(pl.multiple_of(core * HALF, 128), HALF)] = keep[...]
+    whole[:, pl.ds(pl.multiple_of((1 - core) * HALF, 128), HALF)] = got[...]
 
     def body(i, carry):
         rows = pl.ds(pl.multiple_of(i * 16, 16), 16)
-        g = gates[rows, :].astype(f32)
+        g = gate[rows, 0:GCH].astype(f32)
         gated = whole[rows, :].astype(f32) * (g * jax.nn.sigmoid(g))
         scale = lax.rsqrt(jnp.mean(gated * gated, axis=1, keepdims=True) + 1e-05)
         normed[rows, :] = (gated * scale * gain[...]).astype(bf16)
         return carry
 
-    lax.fori_loop(0, PAIR // 16, body, 0)
-
-
-def project_kernel(at, normed, weight, *outs):
-    total = dot(normed[...], weight[...])
-    for i, out in enumerate(outs):
-
-        @pl.when(pl.program_id(0) == i)
-        def _(out=out):
-            out[...] = total.astype(out.dtype)
-
-
-def project(blocks, normed, weight, dtype):
-    count = blocks.shape[0]
-
-    def all_of(i, at):
-        return (0, 0)
-
-    return pl.pallas_call(
-        project_kernel,
-        out_shape=(shape(PAIR, BLOCK, dtype=dtype),) * count,
-        grid_spec=pltpu.PrefetchScalarGridSpec(
-            num_scalar_prefetch=1,
-            grid=(count,),
-            in_specs=[
-                pl.BlockSpec((PAIR, GCH), all_of),
-                pl.BlockSpec((GCH, BLOCK), lambda i, at: (0, at[i])),
-            ],
-            out_specs=[pl.BlockSpec((PAIR, BLOCK), all_of)] * count,
-        ),
-        cost_estimate=pl.CostEstimate(
-            flops=2 * PAIR * GCH * BLOCK * count,
-            bytes_accessed=2 * GCH * BLOCK * count,
-            transcendentals=0,
-        ),
-        compiler_params=params(52),
-        name="project",
-    )(blocks, normed, weight)
-
-
-def add_kernel(at, own, a, b, c, keep, away):
-    core = at[0]
-    for ref, which in ((keep, core), (away, 1 - core)):
-        rows = pl.ds(pl.multiple_of(which * ROWS, 128), ROWS)
-        total = own[rows, :] + a[rows, :].astype(f32) + b[rows, :].astype(f32)
-        ref[...] = (total + c[rows, :].astype(f32)).astype(bf16)
-
-
-def join_kernel(at, keep, got, out):
-    core = at[0]
-    out[:, pl.ds(pl.multiple_of(core * BLOCK, 128), BLOCK)] = keep[...]
-    out[:, pl.ds(pl.multiple_of((1 - core) * BLOCK, 128), BLOCK)] = got[...]
+    lax.fori_loop(0, ROWS // 16, body, 0)
+
+
+def pick_kernel(at, weight, *parts):
+    for k, part in enumerate(parts):
+        first = pl.multiple_of(lax.rem(at[3] + k, T) * COLUMNS, 128)
+        part[...] = weight[:, pl.ds(first, COLUMNS)]
+
+
+def order_kernel(at, *refs):
+    out = refs[-1]
+    for k, part in enumerate(refs[:-1]):
+        out[lax.rem(at[3] + (T - k), T)] = part[...]
+
+
+def groups_kernel(at, own, behind, far_low, far_high, ahead, out):
+    out[at[3]] = own[...]
+    out[lax.rem(at[3] + 3, T)] = behind[...]
+    out[lax.rem(at[3] + 1, T)] = ahead[...]
+    far = lax.rem(at[3] + 2, T)
+    out[far, 0 : ROWS // 2, :] = far_low[...]
+    out[far, ROWS // 2 :, :] = far_high[...]
+
+
+def project_kernel(normed, weight, out, total):
+    group = pl.program_id(1)
+    product = dot(normed[group], weight[...].reshape(GCH, weight.shape[-1]))
+
+    @pl.when(group == 0)
+    def _():
+        total[...] = product
+
+    @pl.when((group > 0) & (group < T - 1))
+    def _():
+        total[...] += product
+
+    @pl.when(group == T - 1)
+    def _():
+        out[...] = (total[...] + product).astype(bf16)
 
 
 def shape(*dims, dtype=bf16):
@@ -299,7 +288,25 @@
 def on_device(projected, conv_weight, conv_bias, step_bias, log_rates, norm_gain, out_weight):
     core, y, z, tp = (lax.axis_index(name) for name in ("c", "y", "z", "tp"))
     at = jnp.stack([core, y, z, tp]).astype(jnp.int32)
-    weight = lax.all_gather(out_weight[0], ("z", "y", "c"), axis=0, tiled=True)
+    parts = pl.pallas_call(
+        pick_kernel,
+        out_shape=(shape(32, COLUMNS),) * T,
+        in_specs=[smem(), vmem()],
+        out_specs=(vmem(),) * T,
+        compiler_params=params(8),
+        name="pick",
+    )(at, out_weight[0])
+    on = [[(i, (i + k) % T) for i in range(T)] for k in range(T)]
+    rows = pl.pallas_call(
+        order_kernel,
+        out_shape=shape(T, 32, COLUMNS),
+        in_specs=[smem()] + [vmem()] * T,
+        out_specs=vmem(),
+        compiler_params=params(8),
+        name="order",
+    )(at, parts[0], *[lax.ppermute(parts[k], "tp", on[k]) for k in (1, 2, 3)])
+    weight = lax.all_gather(rows, ("z", "y", "c"), axis=0, tiled=True)
+    weight = weight.reshape(CHIPS * C, T, 32, COLUMNS)
     mine = projected.reshape(ROWS, GCOLS)
     swap = [(0, 1), (1, 0)]
     other = lax.ppermute(mine, "c", swap)
@@ -378,43 +385,57 @@
         name="carried",
     )(at, within, queries, growth, *states)
 
+    keep, away = pl.pallas_call(
+        split_kernel,
+        out_shape=(shape(ROWS, HALF),) * 2,
+        in_specs=[smem(), vmem()],
+        out_specs=(vmem(),) * 2,
+        compiler_params=params(8),
+        name="split",
+    )(at, scanned)
     normed = pl.pallas_call(
         norm_kernel,
-        out_shape=shape(PAIR, GCH),
-        in_specs=[smem()] + [vmem()] * 5,
-        out_specs=vmem(),
-        scratch_shapes=[pltpu.VMEM((PAIR, GCH), bf16), pltpu.VMEM((PAIR, GCH), bf16)],
+        out_shape=shape(ROWS, GCH),
+        in_specs=[smem()] + [vmem()] * 4,
+        out_specs=vmem(),
+        scratch_shapes=[pltpu.VMEM((ROWS, GCH), bf16)],
         cost_estimate=pl.CostEstimate(
-            flops=1 << 23, bytes_accessed=4 * MIB, transcendentals=1 << 19
+            flops=1 << 22, bytes_accessed=2 * MIB, transcendentals=1 << 18
         ),
         compiler_params=params(10),
         name="norm",
-    )(at, scanned, lax.ppermute(scanned, "c", swap), mine, other, norm_gain)
-
-    offsets = (2, 1, 3)
-    places = lax.rem(tp + jnp.asarray(offsets + (0,), jnp.int32), T).astype(jnp.int32)
-    blocks = places * C + core.astype(jnp.int32)
-    shares = [
-        lax.ppermute(part, "tp", [(i, (i + k) % T) for i in range(T)])
-        for k, part in zip(offsets, project(blocks[:3], normed, weight, bf16), strict=True)
-    ]
-    (own_share,) = project(blocks[3:], normed, weight, f32)
-    keep, away = pl.pallas_call(
-        add_kernel,
-        out_shape=(shape(ROWS, BLOCK), shape(ROWS, BLOCK)),
-        in_specs=[smem()] + [vmem()] * 4,
-        out_specs=(vmem(), vmem()),
-        compiler_params=params(8),
-        name="add",
-    )(at, own_share, *shares)
+    )(at, keep, lax.ppermute(away, "c", swap), mine, norm_gain)
+
+    behind = lax.ppermute(normed, "tp", on[1])
+    ahead = lax.ppermute(normed, "tp", on[3])
+    far_low = lax.ppermute(behind[: ROWS // 2], "tp", on[1])
+    far_high = lax.ppermute(ahead[ROWS // 2 :], "tp", on[3])
+    groups = pl.pallas_call(
+        groups_kernel,
+        out_shape=shape(T, ROWS, GCH),
+        in_specs=[smem()] + [vmem()] * 5,
+        out_specs=vmem(),
+        compiler_params=params(10),
+        name="groups",
+    )(at, normed, behind, far_low, far_high, ahead)
     return pl.pallas_call(
-        join_kernel,
-        out_shape=shape(ROWS, C * BLOCK),
-        in_specs=[smem(), vmem(), vmem()],
-        out_specs=vmem(),
-        compiler_params=params(8),
-        name="join",
-    )(at, keep, lax.ppermute(away, "c", swap))
+        project_kernel,
+        grid=(COLUMNS // WIDE, T),
+        out_shape=shape(ROWS, COLUMNS),
+        in_specs=[
+            vmem(),
+            pl.BlockSpec((CHIPS * C, 1, 32, WIDE), lambda n, g: (0, g, 0, n)),
+        ],
+        out_specs=pl.BlockSpec((ROWS, WIDE), lambda n, g: (0, n)),
+        scratch_shapes=[pltpu.VMEM((ROWS, WIDE), f32)],
+        cost_estimate=pl.CostEstimate(
+            flops=2 * ROWS * T * GCH * COLUMNS,
+            bytes_accessed=2 * T * GCH * COLUMNS,
+            transcendentals=0,
+        ),
+        compiler_params=params(50),
+        name="project",
+    )(groups, weight)
 
 
 def solution(mesh):

time: 152 us -> 146 us (0.961)
  waiting for transfers between devices: 55.3 us -> 43 us
  starting transfers between devices: 25 us -> 32.4 us
  blocking collectives: 33.5 us -> 30.2 us
  Pallas kernels: 20.2 us -> 22.3 us
    all_gather x1, waiting for transfers between devices: 26 us -> 3.01 us  [on_device(): weight = lax.all_gather(rows, ('z', 'y', 'c'), axis=0, tiled=True)]
    ppermute x4 -> x7, waiting for transfers between devices: 7.99 us -> 19.8 us  [the longest x1 12 us: on_device(): behind = lax.ppermute(normed, 'tp', on[1])]
    ppermute x4 -> x7, starting transfers between devices: 8.52 us -> 11.6 us  [the longest x3 5.72 us: on_device(): lax.ppermute(parts[k], 'tp', on[k])]
    all_to_all x1, blocking collectives: 22.8 us -> 19.9 us  [on_device(): plane = lax.all_to_all(plane, 'z', 0, 0, tiled=True)]
    ppermute x1, starting transfers between devices: 0.63 us -> 3.34 us  [on_device(): lax.ppermute(away, 'c', swap)]
    pallas_call x5 -> x6, Pallas kernels: 12.9 us -> 15 us  [the longest x1 10.3 us: on_device(): pl.pallas_call(project_kernel, grid=(COLUMNS // WIDE, T), out_shape=shape...]
  transfers between devices with their start and end apart: 15 -> 18, of which waited for: 12 -> 11; matrix products, arithmetic and copies ran while one was open for 3% -> 2% of each run, Pallas kernels for 9% -> 7%
where the time goes in v5:
time: 146 us
  waiting for transfers between devices  43 us (29%)
  starting transfers between devices  32.4 us (22%)
  blocking collectives  30.2 us (21%)
  Pallas kernels  22.3 us (15%)
  between operations  13.6 us (9%)
  local copies, waits for them, and re-layouts  4.46 us (3%)
    all_to_all x1, blocking collectives, on_device(): plane = lax.all_to_all(plane, 'z', 0, 0, tiled=True)  19.9 us
    ppermute x6, waiting for transfers between devices, along_y(): lax.ppermute(parts[k], 'y', moves[k])  17.9 us
    ppermute x1, waiting for transfers between devices, on_device(): behind = lax.ppermute(normed, 'tp', on[1])  12 us
    all_to_all x1, blocking collectives, on_device(): before = lax.all_to_all(back, 'z', 0, 0, tiled=True)  10.4 us
    pallas_call x1, Pallas kernels, on_device(): pl.pallas_call(project_kernel, grid=(COLUMNS // WIDE, T), out_shape=shape...  10.3 us
    ppermute x6, starting transfers between devices, along_y(): lax.ppermute(parts[k], 'y', moves[k])  8.97 us
    ppermute x3, starting transfers between devices, on_device(): lax.ppermute(parts[k], 'tp', on[k])  5.72 us
    ppermute x1, waiting for transfers between devices, on_device(): far_low = lax.ppermute(behind[:ROWS // 2], 'tp', on[1])  5.56 us
  transfers between devices with their start and end apart: 18, of which 11 were waited for; matrix products, arithmetic and copies ran while one was open for 2% of the time, Pallas kernels for 7%

profile of v5, /device:TPU:1, one launch (start us, length us, event | category | flops | bytes accessed | tf_op | source)
XLA Modules:
  0.0 146.1 jit_solution(139672777368638775)
XLA Ops:
  8.1 2.1 %collective-permute-start.14 = (bf16[32,1024]{1,0:T(8,128)(2,1)S(1)}, bf16[32,1024]{1,0:T(8,128)(2,1)S(1)}, u32[]{:S(2)}, u32[]{:S(2)}) collective-permute-start(bf16[32,1024]{1,0:T(8,128)(2,1)S(1)} %get-tuple-element.36), channel_id=1, source_target_pairs={{0,1},{1,2},{2,3},{3,0},{4,5},{5,6},{6,7},{7,4},{8,9},{9,10},{10,1... | collective-permute-start | bytes 196616 | tf_op jit(solution)/shard_map/ppermute | solution.py:307
  10.3 2.5 %collective-permute-start.15 = (bf16[32,1024]{1,0:T(8,128)(2,1)S(1)}, bf16[32,1024]{1,0:T(8,128)(2,1)S(1)}, u32[]{:S(2)}, u32[]{:S(2)}) collective-permute-start(bf16[32,1024]{1,0:T(8,128)(2,1)S(1)} %get-tuple-element.37), channel_id=1, source_target_pairs={{0,2},{1,3},{2,0},{3,1},{4,6},{5,7},{6,4},{7,5},{8,10},{9,11},{10,... | collective-permute-start | bytes 196616 | tf_op jit(solution)/shard_map/ppermute | solution.py:307
  12.7 1.2 collective-permute-start.16
  13.9 1.4 collective-permute-done.15.refs_2_
  16.1 1.3 order.1
  17.4 2.5 %collective-permute-start = (bf16[128,4640]{0,1:T(8,128)(2,1)}, bf16[128,4640]{0,1:T(8,128)(2,1)}, u32[]{:S(2)}, u32[]{:S(2)}) collective-permute-start(bf16[128,4640]{0,1:T(8,128)(2,1)} %bitcast.15), channel_id=1, source_target_pairs={{0,4},{4,0},{1,5},{5,1},{2,6},{6,2},{3,7},{7,3},{8,12},{12,8},{9,1... | collective-permute-start | bytes 3563528 | tf_op jit(solution)/shard_map/ppermute | solution.py:312
  19.9 1.7 %copy.9 = bf16[128,1,4640]{2,0,1:T(8,128)(2,1)S(1)} copy(bf16[128,1,4640]{0,2,1:T(8,128)(2,1)} %param.7) | data formatting | bytes 2375680 | tf_op args[0]
  21.6 2.8 %collective-permute-start.1 = (bf16[8,2560]{1,0:T(8,128)(2,1)S(1)}, bf16[8,2560]{1,0:T(8,128)(2,1)S(1)}, u32[]{:S(2)}, u32[]{:S(2)}) collective-permute-start(bf16[8,2560]{1,0:T(8,128)(2,1)S(1)} %slice.12), channel_id=1, source_target_pairs={{4,8},{12,16},{20,24},{28,32},{36,40},{44,48},{52,56},{60,64},{68,... | collective-permute-start | bytes 122888 | tf_op jit(solution)/shard_map/ppermute | solution.py:315
  24.4 3.2 %collective-permute-start.2 = (bf16[8,2560]{1,0:T(8,128)(2,1)S(1)}, bf16[8,2560]{1,0:T(8,128)(2,1)S(1)}, u32[]{:S(2)}, u32[]{:S(2)}) collective-permute-start(bf16[8,2560]{1,0:T(8,128)(2,1)S(1)} %slice.12), channel_id=1, source_target_pairs={{4,12},{12,20},{20,28},{28,36},{36,44},{44,52},{52,60},{60,68},{68... | collective-permute-start | bytes 122888 | tf_op jit(solution)/shard_map/ppermute | solution.py:316
  27.7 1.1 collective-permute-done.2
  28.8 1.7 %copy.11.other = bf16[128,4640]{1,0:T(8,128)(2,1)S(1)} copy(bf16[128,4640]{0,1:T(8,128)(2,1)} %collective-permute-done) | data formatting | bytes 2375680 | tf_op jit(solution)/shard_map/ppermute | solution.py:312
  30.6 4.7 %scan.1 = (f32[256,1024]{1,0:T(8,128)S(1)}, bf16[256,256]{1,0:T(8,128)(2,1)S(1)}, bf16[256,128]{1,0:T(8,128)(2,1)S(1)}, bf16[272,256]{1,0:T(8,128)(2,1)S(1)}, bf...) custom-call(s32[4]{0:T(128)S(1)} %pad_add_fusion.at, ...), custom_call_target="tpu_custom_call" | custom-call | flops 536870912 | bytes 5242880 | tf_op jit(solution)/shard_map/scan/pallas_call | solution.py:319
  35.3 1.8 %collective-permute-start.3 = (bf16[272,256]{1,0:T(8,128)(2,1)S(1)}, bf16[272,256]{1,0:T(8,128)(2,1)S(1)}, u32[]{:S(2)}, u32[]{:S(2)}) collective-permute-start(bf16[272,256]{1,0:T(8,128)(2,1)S(1)} %get-tuple-element.26), channel_id=1, source_target_pairs={{0,8},{8,16},{16,24},{24,0},{1,9},{9,17},{17,25},{25,1},{2,10},{10... | collective-permute-start | bytes 417800 | tf_op jit(solution)/shard_map/ppermute | solution.py:343
  37.1 2.6 %collective-permute-start.4 = (bf16[272,256]{1,0:T(8,128)(2,1)S(1)}, bf16[272,256]{1,0:T(8,128)(2,1)S(1)}, u32[]{:S(2)}, u32[]{:S(2)}) collective-permute-start(bf16[272,256]{1,0:T(8,128)(2,1)S(1)} %get-tuple-element.27), channel_id=1, source_target_pairs={{0,16},{8,24},{16,0},{24,8},{1,17},{9,25},{17,1},{25,9},{2,18},{10... | collective-permute-start | bytes 417800 | tf_op jit(solution)/shard_map/ppermute | solution.py:343
  40.5 1.8 %collective-permute-done.3.part_1 = bf16[272,256]{1,0:T(8,128)(2,1)S(1)} collective-permute-done((bf16[272,256]{1,0:T(8,128)(2,1)S(1)}, bf16[272,256]{1,0:T(8,128)(2,1)S(1)}, u32[]{:S(2)}, u32[]{:S(2)}) %collective-permute-start.3) | collective-permute-done | bytes 139296 | tf_op jit(solution)/shard_map/ppermute | solution.py:343
  42.3 4.8 %collective-permute-done.4.part_2 = bf16[272,256]{1,0:T(8,128)(2,1)S(1)} collective-permute-done((bf16[272,256]{1,0:T(8,128)(2,1)S(1)}, bf16[272,256]{1,0:T(8,128)(2,1)S(1)}, u32[]{:S(2)}, u32[]{:S(2)}) %collective-permute-start.4) | collective-permute-done | bytes 139296 | tf_op jit(solution)/shard_map/ppermute | solution.py:343
  47.9 19.9 %all_to_all.10.got = bf16[8,48,256]{2,1,0:T(8,128)(2,1)S(1)} all-to-all(bf16[8,48,256]{2,1,0:T(8,128)(2,1)S(1)} %plane.1), channel_id=1, replica_groups=mesh['z'=8,'y'=4,'c'=2,'tp'=4] {'z'}, dimensions={0} | all-to-all | bytes 393216 | tf_op jit(solution)/shard_map/all_to_all | solution.py:355
  67.8 10.4 %all_to_all.11.before = bf16[8,32,256]{2,1,0:T(8,128)(2,1)S(1)} all-to-all(bf16[8,32,256]{2,1,0:T(8,128)(2,1)S(1)} %prefix.1), channel_id=1, replica_groups=mesh['z'=8,'y'=4,'c'=2,'tp'=4] {'z'}, dimensions={0} | all-to-all | bytes 262144 | tf_op jit(solution)/shard_map/all_to_all | solution.py:364
  78.9 1.2 collective-permute-start.6
  80.2 2.3 %collective-permute-start.7 = (bf16[256,256]{1,0:T(8,128)(2,1)S(1)}, bf16[256,256]{1,0:T(8,128)(2,1)S(1)}, u32[]{:S(2)}, u32[]{:S(2)}) collective-permute-start(bf16[256,256]{1,0:T(8,128)(2,1)S(1)} %get-tuple-element.31), channel_id=1, source_target_pairs={{0,16},{8,24},{16,0},{24,8},{1,17},{9,25},{17,1},{25,9},{2,18},{10... | collective-permute-start | bytes 393224 | tf_op jit(solution)/shard_map/ppermute | solution.py:343
  82.7 5.1 %collective-permute-done.6.state_1 = bf16[256,256]{1,0:T(8,128)(2,1)S(1)} collective-permute-done((bf16[256,256]{1,0:T(8,128)(2,1)S(1)}, bf16[256,256]{1,0:T(8,128)(2,1)S(1)}, u32[]{:S(2)}, u32[]{:S(2)}) %collective-permute-start.6) | collective-permute-done | bytes 131104 | tf_op jit(solution)/shard_map/ppermute | solution.py:343
  87.7 6.3 %collective-permute-done.7.state_2 = bf16[256,256]{1,0:T(8,128)(2,1)S(1)} collective-permute-done((bf16[256,256]{1,0:T(8,128)(2,1)S(1)}, bf16[256,256]{1,0:T(8,128)(2,1)S(1)}, u32[]{:S(2)}, u32[]{:S(2)}) %collective-permute-start.7) | collective-permute-done | bytes 131104 | tf_op jit(solution)/shard_map/ppermute | solution.py:343
  95.6 3.3 %collective-permute-start.9 = (bf16[128,1024]{1,0:T(8,128)(2,1)S(1)}, bf16[128,1024]{1,0:T(8,128)(2,1)S(1)}, u32[]{:S(2)}, u32[]{:S(2)}) collective-permute-start(bf16[128,1024]{1,0:T(8,128)(2,1)S(1)} %get-tuple-element.34), channel_id=1, source_target_pairs={{0,4},{4,0},{1,5},{5,1},{2,6},{6,2},{3,7},{7,3},{8,12},{12,8},{9,1... | collective-permute-start | bytes 786440 | tf_op jit(solution)/shard_map/ppermute | solution.py:407
  98.9 1.2 collective-permute-done.9.got
  100.1 1.6 %norm.1.own = bf16[128,2048]{1,0:T(8,128)(2,1)S(1)} custom-call(s32[4]{0:T(128)S(1)} %pad_add_fusion.at, bf16[128,1024]{1,0:T(8,128)(2,1)S(1)} %get-tuple-element.33.keep, bf16[128,1024]{1,0:T(8,128)(2,1)S(1)} %collective-permute-done.9.got, bf16[128,4640]{1,0:T(8,128)(2,1)S(1)} %bitcast.11, f32[1,2048]{1,0:T(1,128)S(1)} %copy-done.3), custom_call_target="tpu_custom_call" | custom-call | flops 4194304 | bytes 2097152 | tf_op jit(solution)/shard_map/norm/pallas_call | solution.py:396
  101.7 1.1 collective-permute-start.10
  102.8 2.0 %collective-permute-start.12 = (bf16[128,2048]{1,0:T(8,128)(2,1)S(1)}, bf16[128,2048]{1,0:T(8,128)(2,1)S(1)}, u32[]{:S(2)}, u32[]{:S(2)}) collective-permute-start(bf16[128,2048]{1,0:T(8,128)(2,1)S(1)} %norm.1.own), channel_id=1, source_target_pairs={{0,3},{1,0},{2,1},{3,2},{4,7},{5,4},{6,5},{7,6},{8,11},{9,8},{10,9... | collective-permute-start | bytes 1572872 | tf_op jit(solution)/shard_map/ppermute | solution.py:410
  104.8 12.0 %collective-permute-done.10.behind = bf16[128,2048]{1,0:T(8,128)(2,1)S(1)} collective-permute-done((bf16[128,2048]{1,0:T(8,128)(2,1)S(1)}, bf16[128,2048]{1,0:T(8,128)(2,1)S(1)}, u32[]{:S(2)}, u32[]{:S(2)}) %collective-permute-start.10) | collective-permute-done | bytes 524320 | tf_op jit(solution)/shard_map/ppermute | solution.py:409
  117.0 2.7 %collective-permute-start.13 = (bf16[64,2048]{1,0:T(8,128)(2,1)S(1)}, bf16[64,2048]{1,0:T(8,128)(2,1)S(1)}, u32[]{:S(2)}, u32[]{:S(2)}) collective-permute-start(bf16[64,2048]{1,0:T(8,128)(2,1)S(1)} %slice.14), channel_id=1, source_target_pairs={{0,3},{1,0},{2,1},{3,2},{4,7},{5,4},{6,5},{7,6},{8,11},{9,8},{10,9... | collective-permute-start | bytes 786440 | tf_op jit(solution)/shard_map/ppermute | solution.py:412
  119.7 5.6 %collective-permute-done.11.far_low = bf16[64,2048]{1,0:T(8,128)(2,1)S(1)} collective-permute-done((bf16[64,2048]{1,0:T(8,128)(2,1)S(1)}, bf16[64,2048]{1,0:T(8,128)(2,1)S(1)}, u32[]{:S(2)}, u32[]{:S(2)}) %collective-permute-start.11) | collective-permute-done | bytes 262176 | tf_op jit(solution)/shard_map/ppermute | solution.py:411
  125.9 3.0 %all-gather.2.cloned.1.call-done = bf16[256,32,1024]{2,1,0:T(8,128)(2,1)} async-done(((bf16[4,32,1024]{2,1,0:T(8,128)(2,1)}), bf16[256,32,1024]{2,1,0:T(8,128)(2,1)}) %all-gather.2.cloned.1.call-update) | async-done | bytes 16777232 | tf_op jit(solution)/shard_map/all_gather | solution.py:308
  129.0 10.3 %project.1 = bf16[128,1024]{1,0:T(8,128)(2,1)} custom-call(bf16[4,128,2048]{2,1,0:T(8,128)(2,1)S(1)} %groups.1.normed, bf16[64,4,32,1024]{3,2,1,0:T(8,128)(2,1)} %bitcast.14), custom_call_target="tpu_custom_call" | custom-call | flops 2147483648 | bytes 16777216 | tf_op jit(solution)/shard_map/project/pallas_call | solution.py:421
  (37 shorter events, 7.3 us)
Async XLA Ops:
  6.5 122.4 %all-gather.2.cloned.1.call-start = ((), (), s32[]{:S(2)}) async-start(), calls=%async_computation.2 | async-start | bytes 17039360 | tf_op jit(solution)/shard_map/all_gather | solution.py:308
  6.6 1.0 copy-start
  8.1 5.7 %collective-permute-start.14 = (bf16[32,1024]{1,0:T(8,128)(2,1)S(1)}, bf16[32,1024]{1,0:T(8,128)(2,1)S(1)}, u32[]{:S(2)}, u32[]{:S(2)}) collective-permute-start(bf16[32,1024]{1,0:T(8,128)(2,1)S(1)} %get-tuple-element.36), channel_id=1, source_target_pairs={{0,1},{1,2},{2,3},{3,0},{4,5},{5,6},{6,7},{7,4},{8,9},{9,10},{10,1... | collective-permute-start | bytes 196616 | tf_op jit(solution)/shard_map/ppermute | solution.py:307
  10.3 5.1 %collective-permute-start.15 = (bf16[32,1024]{1,0:T(8,128)(2,1)S(1)}, bf16[32,1024]{1,0:T(8,128)(2,1)S(1)}, u32[]{:S(2)}, u32[]{:S(2)}) collective-permute-start(bf16[32,1024]{1,0:T(8,128)(2,1)S(1)} %get-tuple-element.37), channel_id=1, source_target_pairs={{0,2},{1,3},{2,0},{3,1},{4,6},{5,7},{6,4},{7,5},{8,10},{9,11},{10,... | collective-permute-start | bytes 196616 | tf_op jit(solution)/shard_map/ppermute | solution.py:307
  12.7 3.4 %collective-permute-start.16 = (bf16[32,1024]{1,0:T(8,128)(2,1)S(1)}, bf16[32,1024]{1,0:T(8,128)(2,1)S(1)}, u32[]{:S(2)}, u32[]{:S(2)}) collective-permute-start(bf16[32,1024]{1,0:T(8,128)(2,1)S(1)} %get-tuple-element.38), channel_id=1, source_target_pairs={{0,3},{1,0},{2,1},{3,2},{4,7},{5,4},{6,5},{7,6},{8,11},{9,8},{10,9... | collective-permute-start | bytes 196616 | tf_op jit(solution)/shard_map/ppermute | solution.py:307
  17.4 11.4 %collective-permute-start = (bf16[128,4640]{0,1:T(8,128)(2,1)}, bf16[128,4640]{0,1:T(8,128)(2,1)}, u32[]{:S(2)}, u32[]{:S(2)}) collective-permute-start(bf16[128,4640]{0,1:T(8,128)(2,1)} %bitcast.15), channel_id=1, source_target_pairs={{0,4},{4,0},{1,5},{5,1},{2,6},{6,2},{3,7},{7,3},{8,12},{12,8},{9,1... | collective-permute-start | bytes 3563528 | tf_op jit(solution)/shard_map/ppermute | solution.py:312
  21.6 6.1 %collective-permute-start.1 = (bf16[8,2560]{1,0:T(8,128)(2,1)S(1)}, bf16[8,2560]{1,0:T(8,128)(2,1)S(1)}, u32[]{:S(2)}, u32[]{:S(2)}) collective-permute-start(bf16[8,2560]{1,0:T(8,128)(2,1)S(1)} %slice.12), channel_id=1, source_target_pairs={{4,8},{12,16},{20,24},{28,32},{36,40},{44,48},{52,56},{60,64},{68,... | collective-permute-start | bytes 122888 | tf_op jit(solution)/shard_map/ppermute | solution.py:315
  24.4 4.3 %collective-permute-start.2 = (bf16[8,2560]{1,0:T(8,128)(2,1)S(1)}, bf16[8,2560]{1,0:T(8,128)(2,1)S(1)}, u32[]{:S(2)}, u32[]{:S(2)}) collective-permute-start(bf16[8,2560]{1,0:T(8,128)(2,1)S(1)} %slice.12), channel_id=1, source_target_pairs={{4,12},{12,20},{20,28},{28,36},{36,44},{44,52},{52,60},{60,68},{68... | collective-permute-start | bytes 122888 | tf_op jit(solution)/shard_map/ppermute | solution.py:316
  28.7 1.8 %copy-start.1 = (f32[1,4,2560]{2,1,0:T(4,128)S(1)}, f32[1,4,2560]{2,1,0:T(4,128)}, u32[]{:S(2)}) copy-start(f32[1,4,2560]{2,1,0:T(4,128)} %param.8) | copy-start | bytes 122884
  28.8 1.8 %copy-start.2 = (f32[1,2560]{1,0:T(1,128)S(1)}, f32[1,2560]{1,0:T(1,128)}, u32[]{:S(2)}) copy-start(f32[1,2560]{1,0:T(1,128)} %bias.1) | copy-start | bytes 30724
  28.8 1.8 %copy-start.4 = (f32[1,32]{1,0:T(1,128)S(1)}, f32[1,32]{1,0:T(1,128)}, u32[]{:S(2)}) copy-start(f32[1,32]{1,0:T(1,128)} %step_bias.1) | copy-start | bytes 388
  28.8 1.8 %copy-start.5 = (f32[1,32]{1,0:T(1,128)S(1)}, f32[1,32]{1,0:T(1,128)}, u32[]{:S(2)}) copy-start(f32[1,32]{1,0:T(1,128)} %log_rates.1) | copy-start | bytes 388
  35.3 7.0 %collective-permute-start.3 = (bf16[272,256]{1,0:T(8,128)(2,1)S(1)}, bf16[272,256]{1,0:T(8,128)(2,1)S(1)}, u32[]{:S(2)}, u32[]{:S(2)}) collective-permute-start(bf16[272,256]{1,0:T(8,128)(2,1)S(1)} %get-tuple-element.26), channel_id=1, source_target_pairs={{0,8},{8,16},{16,24},{24,0},{1,9},{9,17},{17,25},{25,1},{2,10},{10... | collective-permute-start | bytes 417800 | tf_op jit(solution)/shard_map/ppermute | solution.py:343
  37.1 10.0 %collective-permute-start.4 = (bf16[272,256]{1,0:T(8,128)(2,1)S(1)}, bf16[272,256]{1,0:T(8,128)(2,1)S(1)}, u32[]{:S(2)}, u32[]{:S(2)}) collective-permute-start(bf16[272,256]{1,0:T(8,128)(2,1)S(1)} %get-tuple-element.27), channel_id=1, source_target_pairs={{0,16},{8,24},{16,0},{24,8},{1,17},{9,25},{17,1},{25,9},{2,18},{10... | collective-permute-start | bytes 417800 | tf_op jit(solution)/shard_map/ppermute | solution.py:343
  39.8 7.3 %collective-permute-start.5 = (bf16[272,256]{1,0:T(8,128)(2,1)S(1)}, bf16[272,256]{1,0:T(8,128)(2,1)S(1)}, u32[]{:S(2)}, u32[]{:S(2)}) collective-permute-start(bf16[272,256]{1,0:T(8,128)(2,1)S(1)} %get-tuple-element.28), channel_id=1, source_target_pairs={{0,24},{8,0},{16,8},{24,16},{1,25},{9,1},{17,9},{25,17},{2,26},{10... | collective-permute-start | bytes 417800 | tf_op jit(solution)/shard_map/ppermute | solution.py:343
  78.9 8.8 %collective-permute-start.6 = (bf16[256,256]{1,0:T(8,128)(2,1)S(1)}, bf16[256,256]{1,0:T(8,128)(2,1)S(1)}, u32[]{:S(2)}, u32[]{:S(2)}) collective-permute-start(bf16[256,256]{1,0:T(8,128)(2,1)S(1)} %get-tuple-element.30), channel_id=1, source_target_pairs={{0,8},{8,16},{16,24},{24,0},{1,9},{9,17},{17,25},{25,1},{2,10},{10... | collective-permute-start | bytes 393224 | tf_op jit(solution)/shard_map/ppermute | solution.py:343
  80.2 13.8 %collective-permute-start.7 = (bf16[256,256]{1,0:T(8,128)(2,1)S(1)}, bf16[256,256]{1,0:T(8,128)(2,1)S(1)}, u32[]{:S(2)}, u32[]{:S(2)}) collective-permute-start(bf16[256,256]{1,0:T(8,128)(2,1)S(1)} %get-tuple-element.31), channel_id=1, source_target_pairs={{0,16},{8,24},{16,0},{24,8},{1,17},{9,25},{17,1},{25,9},{2,18},{10... | collective-permute-start | bytes 393224 | tf_op jit(solution)/shard_map/ppermute | solution.py:343
  82.5 11.5 %collective-permute-start.8 = (bf16[256,256]{1,0:T(8,128)(2,1)S(1)}, bf16[256,256]{1,0:T(8,128)(2,1)S(1)}, u32[]{:S(2)}, u32[]{:S(2)}) collective-permute-start(bf16[256,256]{1,0:T(8,128)(2,1)S(1)} %get-tuple-element.32), channel_id=1, source_target_pairs={{0,24},{8,0},{16,8},{24,16},{1,25},{9,1},{17,9},{25,17},{2,26},{10... | collective-permute-start | bytes 393224 | tf_op jit(solution)/shard_map/ppermute | solution.py:343
  94.0 6.1 %copy-start.3 = (f32[1,2048]{1,0:T(1,128)S(1)}, f32[1,2048]{1,0:T(1,128)}, u32[]{:S(2)}) copy-start(f32[1,2048]{1,0:T(1,128)} %gain.1) | copy-start | bytes 24580
  95.6 4.5 %collective-permute-start.9 = (bf16[128,1024]{1,0:T(8,128)(2,1)S(1)}, bf16[128,1024]{1,0:T(8,128)(2,1)S(1)}, u32[]{:S(2)}, u32[]{:S(2)}) collective-permute-start(bf16[128,1024]{1,0:T(8,128)(2,1)S(1)} %get-tuple-element.34), channel_id=1, source_target_pairs={{0,4},{4,0},{1,5},{5,1},{2,6},{6,2},{3,7},{7,3},{8,12},{12,8},{9,1... | collective-permute-start | bytes 786440 | tf_op jit(solution)/shard_map/ppermute | solution.py:407
  101.7 15.1 %collective-permute-start.10 = (bf16[128,2048]{1,0:T(8,128)(2,1)S(1)}, bf16[128,2048]{1,0:T(8,128)(2,1)S(1)}, u32[]{:S(2)}, u32[]{:S(2)}) collective-permute-start(bf16[128,2048]{1,0:T(8,128)(2,1)S(1)} %norm.1.own), channel_id=1, source_target_pairs={{0,1},{1,2},{2,3},{3,0},{4,5},{5,6},{6,7},{7,4},{8,9},{9,10},{10,1... | collective-permute-start | bytes 1572872 | tf_op jit(solution)/shard_map/ppermute | solution.py:409
  102.8 14.1 %collective-permute-start.12 = (bf16[128,2048]{1,0:T(8,128)(2,1)S(1)}, bf16[128,2048]{1,0:T(8,128)(2,1)S(1)}, u32[]{:S(2)}, u32[]{:S(2)}) collective-permute-start(bf16[128,2048]{1,0:T(8,128)(2,1)S(1)} %norm.1.own), channel_id=1, source_target_pairs={{0,3},{1,0},{2,1},{3,2},{4,7},{5,4},{6,5},{7,6},{8,11},{9,8},{10,9... | collective-permute-start | bytes 1572872 | tf_op jit(solution)/shard_map/ppermute | solution.py:410
  116.8 8.4 %collective-permute-start.11 = (bf16[64,2048]{1,0:T(8,128)(2,1)S(1)}, bf16[64,2048]{1,0:T(8,128)(2,1)S(1)}, u32[]{:S(2)}, u32[]{:S(2)}) collective-permute-start(bf16[64,2048]{1,0:T(8,128)(2,1)S(1)} %slice.13), channel_id=1, source_target_pairs={{0,1},{1,2},{2,3},{3,0},{4,5},{5,6},{6,7},{7,4},{8,9},{9,10},{10,1... | collective-permute-start | bytes 786440 | tf_op jit(solution)/shard_map/ppermute | solution.py:411
  117.0 8.3 %collective-permute-start.13 = (bf16[64,2048]{1,0:T(8,128)(2,1)S(1)}, bf16[64,2048]{1,0:T(8,128)(2,1)S(1)}, u32[]{:S(2)}, u32[]{:S(2)}) collective-permute-start(bf16[64,2048]{1,0:T(8,128)(2,1)S(1)} %slice.14), channel_id=1, source_target_pairs={{0,3},{1,0},{2,1},{3,2},{4,7},{5,4},{6,5},{7,6},{8,11},{9,8},{10,9... | collective-permute-start | bytes 786440 | tf_op jit(solution)/shard_map/ppermute | solution.py:412
Sparse Core Ops, SparseCore 0:
  17.5 111.3 all-gather.1

commit v6 on v5

--- a/solution.py
+++ b/solution.py
@@ -264,9 +264,10 @@
     out[far, ROWS // 2 :, :] = far_high[...]
 
 
-def project_kernel(normed, weight, out, total):
+def project_kernel(normed, lower, upper, out, total):
     group = pl.program_id(1)
-    product = dot(normed[group], weight[...].reshape(GCH, weight.shape[-1]))
+    product = dot(normed[group, :, 0:HALF], lower[...].reshape(HALF, WIDE))
+    product = product + dot(normed[group, :, HALF:], upper[...].reshape(HALF, WIDE))
 
     @pl.when(group == 0)
     def _():
@@ -290,9 +291,10 @@
     at = jnp.stack([core, y, z, tp]).astype(jnp.int32)
     parts = pl.pallas_call(
         pick_kernel,
+        grid=(1,),
         out_shape=(shape(32, COLUMNS),) * T,
-        in_specs=[smem(), vmem()],
-        out_specs=(vmem(),) * T,
+        in_specs=[smem(), pl.BlockSpec((32, T * COLUMNS), lambda i: (0, 0))],
+        out_specs=(pl.BlockSpec((32, COLUMNS), lambda i: (0, 0)),) * T,
         compiler_params=params(8),
         name="pick",
     )(at, out_weight[0])
@@ -424,7 +426,8 @@
         out_shape=shape(ROWS, COLUMNS),
         in_specs=[
             vmem(),
-            pl.BlockSpec((CHIPS * C, 1, 32, WIDE), lambda n, g: (0, g, 0, n)),
+            pl.BlockSpec((CHIPS, 1, 32, WIDE), lambda n, g: (0, g, 0, n)),
+            pl.BlockSpec((CHIPS, 1, 32, WIDE), lambda n, g: (1, g, 0, n)),
         ],
         out_specs=pl.BlockSpec((ROWS, WIDE), lambda n, g: (0, n)),
         scratch_shapes=[pltpu.VMEM((ROWS, WIDE), f32)],
@@ -435,7 +438,7 @@
         ),
         compiler_params=params(50),
         name="project",
-    )(groups, weight)
+    )(groups, weight, weight)
 
 
 def solution(mesh):

time: 146 us -> 146 us (level)
  no operation moved by 1% of the time
where the time goes in v6:
time: 146 us
  waiting for transfers between devices  43 us (29%)
  starting transfers between devices  32.4 us (22%)
  blocking collectives  30.2 us (21%)
  Pallas kernels  22.1 us (15%)
  between operations  13.6 us (9%)
  local copies, waits for them, and re-layouts  4.46 us (3%)
    all_to_all x1, blocking collectives, on_device(): plane = lax.all_to_all(plane, 'z', 0, 0, tiled=True)  19.9 us
    ppermute x6, waiting for transfers between devices, along_y(): lax.ppermute(parts[k], 'y', moves[k])  17.9 us
    ppermute x1, waiting for transfers between devices, on_device(): behind = lax.ppermute(normed, 'tp', on[1])  12 us
    all_to_all x1, blocking collectives, on_device(): before = lax.all_to_all(back, 'z', 0, 0, tiled=True)  10.4 us
    pallas_call x1, Pallas kernels, on_device(): pl.pallas_call(project_kernel, grid=(COLUMNS // WIDE, T), out_shape=shape...  10 us
    ppermute x6, starting transfers between devices, along_y(): lax.ppermute(parts[k], 'y', moves[k])  8.97 us
    ppermute x3, starting transfers between devices, on_device(): lax.ppermute(parts[k], 'tp', on[k])  5.72 us
    ppermute x1, waiting for transfers between devices, on_device(): far_low = lax.ppermute(behind[:ROWS // 2], 'tp', on[1])  5.56 us
  transfers between devices with their start and end apart: 18, of which 11 were waited for; matrix products, arithmetic and copies ran while one was open for 2% of the time, Pallas kernels for 7%

profile of v6, /device:TPU:1, one launch (start us, length us, event | category | flops | bytes accessed | tf_op | source)
XLA Modules:
  0.0 145.8 jit_solution(131938573309403269)
XLA Ops:
  8.1 2.1 %collective-permute-start.14 = (bf16[32,1024]{1,0:T(8,128)(2,1)S(1)}, bf16[32,1024]{1,0:T(8,128)(2,1)S(1)}, u32[]{:S(2)}, u32[]{:S(2)}) collective-permute-start(bf16[32,1024]{1,0:T(8,128)(2,1)S(1)} %get-tuple-element.36), channel_id=1, source_target_pairs={{0,1},{1,2},{2,3},{3,0},{4,5},{5,6},{6,7},{7,4},{8,9},{9,10},{10,1... | collective-permute-start | bytes 196616 | tf_op jit(solution)/shard_map/ppermute | solution.py:309
  10.3 2.5 %collective-permute-start.15 = (bf16[32,1024]{1,0:T(8,128)(2,1)S(1)}, bf16[32,1024]{1,0:T(8,128)(2,1)S(1)}, u32[]{:S(2)}, u32[]{:S(2)}) collective-permute-start(bf16[32,1024]{1,0:T(8,128)(2,1)S(1)} %get-tuple-element.37), channel_id=1, source_target_pairs={{0,2},{1,3},{2,0},{3,1},{4,6},{5,7},{6,4},{7,5},{8,10},{9,11},{10,... | collective-permute-start | bytes 196616 | tf_op jit(solution)/shard_map/ppermute | solution.py:309
  12.7 1.2 collective-permute-start.16
  13.9 1.4 collective-permute-done.15.refs_2_
  16.1 1.3 order.1
  17.4 2.5 %collective-permute-start = (bf16[128,4640]{0,1:T(8,128)(2,1)}, bf16[128,4640]{0,1:T(8,128)(2,1)}, u32[]{:S(2)}, u32[]{:S(2)}) collective-permute-start(bf16[128,4640]{0,1:T(8,128)(2,1)} %bitcast.16), channel_id=1, source_target_pairs={{0,4},{4,0},{1,5},{5,1},{2,6},{6,2},{3,7},{7,3},{8,12},{12,8},{9,1... | collective-permute-start | bytes 3563528 | tf_op jit(solution)/shard_map/ppermute | solution.py:314
  19.9 1.7 %copy.9 = bf16[128,1,4640]{2,0,1:T(8,128)(2,1)S(1)} copy(bf16[128,1,4640]{0,2,1:T(8,128)(2,1)} %param.7) | data formatting | bytes 2375680 | tf_op args[0]
  21.6 2.8 %collective-permute-start.1 = (bf16[8,2560]{1,0:T(8,128)(2,1)S(1)}, bf16[8,2560]{1,0:T(8,128)(2,1)S(1)}, u32[]{:S(2)}, u32[]{:S(2)}) collective-permute-start(bf16[8,2560]{1,0:T(8,128)(2,1)S(1)} %slice.12), channel_id=1, source_target_pairs={{4,8},{12,16},{20,24},{28,32},{36,40},{44,48},{52,56},{60,64},{68,... | collective-permute-start | bytes 122888 | tf_op jit(solution)/shard_map/ppermute | solution.py:317
  24.4 3.2 %collective-permute-start.2 = (bf16[8,2560]{1,0:T(8,128)(2,1)S(1)}, bf16[8,2560]{1,0:T(8,128)(2,1)S(1)}, u32[]{:S(2)}, u32[]{:S(2)}) collective-permute-start(bf16[8,2560]{1,0:T(8,128)(2,1)S(1)} %slice.12), channel_id=1, source_target_pairs={{4,12},{12,20},{20,28},{28,36},{36,44},{44,52},{52,60},{60,68},{68... | collective-permute-start | bytes 122888 | tf_op jit(solution)/shard_map/ppermute | solution.py:318
  27.7 1.1 collective-permute-done.2
  28.8 1.7 %copy.11.other = bf16[128,4640]{1,0:T(8,128)(2,1)S(1)} copy(bf16[128,4640]{0,1:T(8,128)(2,1)} %collective-permute-done) | data formatting | bytes 2375680 | tf_op jit(solution)/shard_map/ppermute | solution.py:314
  30.6 4.7 %scan.1 = (f32[256,1024]{1,0:T(8,128)S(1)}, bf16[256,256]{1,0:T(8,128)(2,1)S(1)}, bf16[256,128]{1,0:T(8,128)(2,1)S(1)}, bf16[272,256]{1,0:T(8,128)(2,1)S(1)}, bf...) custom-call(s32[4]{0:T(128)S(1)} %pad_add_fusion.at, ...), custom_call_target="tpu_custom_call" | custom-call | flops 536870912 | bytes 5242880 | tf_op jit(solution)/shard_map/scan/pallas_call | solution.py:321
  35.3 1.8 %collective-permute-start.3 = (bf16[272,256]{1,0:T(8,128)(2,1)S(1)}, bf16[272,256]{1,0:T(8,128)(2,1)S(1)}, u32[]{:S(2)}, u32[]{:S(2)}) collective-permute-start(bf16[272,256]{1,0:T(8,128)(2,1)S(1)} %get-tuple-element.26), channel_id=1, source_target_pairs={{0,8},{8,16},{16,24},{24,0},{1,9},{9,17},{17,25},{25,1},{2,10},{10... | collective-permute-start | bytes 417800 | tf_op jit(solution)/shard_map/ppermute | solution.py:345
  37.1 2.6 %collective-permute-start.4 = (bf16[272,256]{1,0:T(8,128)(2,1)S(1)}, bf16[272,256]{1,0:T(8,128)(2,1)S(1)}, u32[]{:S(2)}, u32[]{:S(2)}) collective-permute-start(bf16[272,256]{1,0:T(8,128)(2,1)S(1)} %get-tuple-element.27), channel_id=1, source_target_pairs={{0,16},{8,24},{16,0},{24,8},{1,17},{9,25},{17,1},{25,9},{2,18},{10... | collective-permute-start | bytes 417800 | tf_op jit(solution)/shard_map/ppermute | solution.py:345
  40.5 1.8 %collective-permute-done.3.part_1 = bf16[272,256]{1,0:T(8,128)(2,1)S(1)} collective-permute-done((bf16[272,256]{1,0:T(8,128)(2,1)S(1)}, bf16[272,256]{1,0:T(8,128)(2,1)S(1)}, u32[]{:S(2)}, u32[]{:S(2)}) %collective-permute-start.3) | collective-permute-done | bytes 139296 | tf_op jit(solution)/shard_map/ppermute | solution.py:345
  42.3 4.8 %collective-permute-done.4.part_2 = bf16[272,256]{1,0:T(8,128)(2,1)S(1)} collective-permute-done((bf16[272,256]{1,0:T(8,128)(2,1)S(1)}, bf16[272,256]{1,0:T(8,128)(2,1)S(1)}, u32[]{:S(2)}, u32[]{:S(2)}) %collective-permute-start.4) | collective-permute-done | bytes 139296 | tf_op jit(solution)/shard_map/ppermute | solution.py:345
  47.9 19.9 %all_to_all.10.got = bf16[8,48,256]{2,1,0:T(8,128)(2,1)S(1)} all-to-all(bf16[8,48,256]{2,1,0:T(8,128)(2,1)S(1)} %plane.1), channel_id=1, replica_groups=mesh['z'=8,'y'=4,'c'=2,'tp'=4] {'z'}, dimensions={0} | all-to-all | bytes 393216 | tf_op jit(solution)/shard_map/all_to_all | solution.py:357
  67.8 10.4 %all_to_all.11.before = bf16[8,32,256]{2,1,0:T(8,128)(2,1)S(1)} all-to-all(bf16[8,32,256]{2,1,0:T(8,128)(2,1)S(1)} %prefix.1), channel_id=1, replica_groups=mesh['z'=8,'y'=4,'c'=2,'tp'=4] {'z'}, dimensions={0} | all-to-all | bytes 262144 | tf_op jit(solution)/shard_map/all_to_all | solution.py:366
  78.9 1.2 collective-permute-start.6
  80.2 2.3 %collective-permute-start.7 = (bf16[256,256]{1,0:T(8,128)(2,1)S(1)}, bf16[256,256]{1,0:T(8,128)(2,1)S(1)}, u32[]{:S(2)}, u32[]{:S(2)}) collective-permute-start(bf16[256,256]{1,0:T(8,128)(2,1)S(1)} %get-tuple-element.31), channel_id=1, source_target_pairs={{0,16},{8,24},{16,0},{24,8},{1,17},{9,25},{17,1},{25,9},{2,18},{10... | collective-permute-start | bytes 393224 | tf_op jit(solution)/shard_map/ppermute | solution.py:345
  82.7 5.1 %collective-permute-done.6.state_1 = bf16[256,256]{1,0:T(8,128)(2,1)S(1)} collective-permute-done((bf16[256,256]{1,0:T(8,128)(2,1)S(1)}, bf16[256,256]{1,0:T(8,128)(2,1)S(1)}, u32[]{:S(2)}, u32[]{:S(2)}) %collective-permute-start.6) | collective-permute-done | bytes 131104 | tf_op jit(solution)/shard_map/ppermute | solution.py:345
  87.7 6.3 %collective-permute-done.7.state_2 = bf16[256,256]{1,0:T(8,128)(2,1)S(1)} collective-permute-done((bf16[256,256]{1,0:T(8,128)(2,1)S(1)}, bf16[256,256]{1,0:T(8,128)(2,1)S(1)}, u32[]{:S(2)}, u32[]{:S(2)}) %collective-permute-start.7) | collective-permute-done | bytes 131104 | tf_op jit(solution)/shard_map/ppermute | solution.py:345
  95.6 3.3 %collective-permute-start.9 = (bf16[128,1024]{1,0:T(8,128)(2,1)S(1)}, bf16[128,1024]{1,0:T(8,128)(2,1)S(1)}, u32[]{:S(2)}, u32[]{:S(2)}) collective-permute-start(bf16[128,1024]{1,0:T(8,128)(2,1)S(1)} %get-tuple-element.34), channel_id=1, source_target_pairs={{0,4},{4,0},{1,5},{5,1},{2,6},{6,2},{3,7},{7,3},{8,12},{12,8},{9,1... | collective-permute-start | bytes 786440 | tf_op jit(solution)/shard_map/ppermute | solution.py:409
  98.9 1.2 collective-permute-done.9.got
  100.1 1.6 %norm.1.own = bf16[128,2048]{1,0:T(8,128)(2,1)S(1)} custom-call(s32[4]{0:T(128)S(1)} %pad_add_fusion.at, bf16[128,1024]{1,0:T(8,128)(2,1)S(1)} %get-tuple-element.33.keep, bf16[128,1024]{1,0:T(8,128)(2,1)S(1)} %collective-permute-done.9.got, bf16[128,4640]{1,0:T(8,128)(2,1)S(1)} %bitcast.11, f32[1,2048]{1,0:T(1,128)S(1)} %copy-done.3), custom_call_target="tpu_custom_call" | custom-call | flops 4194304 | bytes 2097152 | tf_op jit(solution)/shard_map/norm/pallas_call | solution.py:398
  101.7 1.1 collective-permute-start.10
  102.8 2.0 %collective-permute-start.12 = (bf16[128,2048]{1,0:T(8,128)(2,1)S(1)}, bf16[128,2048]{1,0:T(8,128)(2,1)S(1)}, u32[]{:S(2)}, u32[]{:S(2)}) collective-permute-start(bf16[128,2048]{1,0:T(8,128)(2,1)S(1)} %norm.1.own), channel_id=1, source_target_pairs={{0,3},{1,0},{2,1},{3,2},{4,7},{5,4},{6,5},{7,6},{8,11},{9,8},{10,9... | collective-permute-start | bytes 1572872 | tf_op jit(solution)/shard_map/ppermute | solution.py:412
  104.8 12.0 %collective-permute-done.10.behind = bf16[128,2048]{1,0:T(8,128)(2,1)S(1)} collective-permute-done((bf16[128,2048]{1,0:T(8,128)(2,1)S(1)}, bf16[128,2048]{1,0:T(8,128)(2,1)S(1)}, u32[]{:S(2)}, u32[]{:S(2)}) %collective-permute-start.10) | collective-permute-done | bytes 524320 | tf_op jit(solution)/shard_map/ppermute | solution.py:411
  117.0 2.7 %collective-permute-start.13 = (bf16[64,2048]{1,0:T(8,128)(2,1)S(1)}, bf16[64,2048]{1,0:T(8,128)(2,1)S(1)}, u32[]{:S(2)}, u32[]{:S(2)}) collective-permute-start(bf16[64,2048]{1,0:T(8,128)(2,1)S(1)} %slice.14), channel_id=1, source_target_pairs={{0,3},{1,0},{2,1},{3,2},{4,7},{5,4},{6,5},{7,6},{8,11},{9,8},{10,9... | collective-permute-start | bytes 786440 | tf_op jit(solution)/shard_map/ppermute | solution.py:414
  119.7 5.6 %collective-permute-done.11.far_low = bf16[64,2048]{1,0:T(8,128)(2,1)S(1)} collective-permute-done((bf16[64,2048]{1,0:T(8,128)(2,1)S(1)}, bf16[64,2048]{1,0:T(8,128)(2,1)S(1)}, u32[]{:S(2)}, u32[]{:S(2)}) %collective-permute-start.11) | collective-permute-done | bytes 262176 | tf_op jit(solution)/shard_map/ppermute | solution.py:413
  125.9 3.0 %all-gather.2.cloned.1.call-done = bf16[256,32,1024]{2,1,0:T(8,128)(2,1)} async-done(((bf16[4,32,1024]{2,1,0:T(8,128)(2,1)}), bf16[256,32,1024]{2,1,0:T(8,128)(2,1)}) %all-gather.2.cloned.1.call-update) | async-done | bytes 16777232 | tf_op jit(solution)/shard_map/all_gather | solution.py:310
  129.0 10.0 %project.1 = bf16[128,1024]{1,0:T(8,128)(2,1)} custom-call(bf16[4,128,2048]{2,1,0:T(8,128)(2,1)S(1)} %groups.1.normed, bf16[64,4,32,1024]{3,2,1,0:T(8,128)(2,1)} %bitcast.14, bf16[64,4,32,1024]{3,2,1,0:T(8,128)(2,1)} %bitcast.15), custom_call_target="tpu_custom_call" | custom-call | flops 2147483648 | bytes 16777216 | tf_op jit(solution)/shard_map/project/pallas_call | solution.py:423
  (37 shorter events, 7.3 us)
Async XLA Ops:
  6.5 122.4 %all-gather.2.cloned.1.call-start = ((), (), s32[]{:S(2)}) async-start(), calls=%async_computation.2 | async-start | bytes 17039360 | tf_op jit(solution)/shard_map/all_gather | solution.py:310
  6.6 1.0 copy-start
  8.1 5.7 %collective-permute-start.14 = (bf16[32,1024]{1,0:T(8,128)(2,1)S(1)}, bf16[32,1024]{1,0:T(8,128)(2,1)S(1)}, u32[]{:S(2)}, u32[]{:S(2)}) collective-permute-start(bf16[32,1024]{1,0:T(8,128)(2,1)S(1)} %get-tuple-element.36), channel_id=1, source_target_pairs={{0,1},{1,2},{2,3},{3,0},{4,5},{5,6},{6,7},{7,4},{8,9},{9,10},{10,1... | collective-permute-start | bytes 196616 | tf_op jit(solution)/shard_map/ppermute | solution.py:309
  10.3 5.1 %collective-permute-start.15 = (bf16[32,1024]{1,0:T(8,128)(2,1)S(1)}, bf16[32,1024]{1,0:T(8,128)(2,1)S(1)}, u32[]{:S(2)}, u32[]{:S(2)}) collective-permute-start(bf16[32,1024]{1,0:T(8,128)(2,1)S(1)} %get-tuple-element.37), channel_id=1, source_target_pairs={{0,2},{1,3},{2,0},{3,1},{4,6},{5,7},{6,4},{7,5},{8,10},{9,11},{10,... | collective-permute-start | bytes 196616 | tf_op jit(solution)/shard_map/ppermute | solution.py:309
  12.7 3.4 %collective-permute-start.16 = (bf16[32,1024]{1,0:T(8,128)(2,1)S(1)}, bf16[32,1024]{1,0:T(8,128)(2,1)S(1)}, u32[]{:S(2)}, u32[]{:S(2)}) collective-permute-start(bf16[32,1024]{1,0:T(8,128)(2,1)S(1)} %get-tuple-element.38), channel_id=1, source_target_pairs={{0,3},{1,0},{2,1},{3,2},{4,7},{5,4},{6,5},{7,6},{8,11},{9,8},{10,9... | collective-permute-start | bytes 196616 | tf_op jit(solution)/shard_map/ppermute | solution.py:309
  17.4 11.4 %collective-permute-start = (bf16[128,4640]{0,1:T(8,128)(2,1)}, bf16[128,4640]{0,1:T(8,128)(2,1)}, u32[]{:S(2)}, u32[]{:S(2)}) collective-permute-start(bf16[128,4640]{0,1:T(8,128)(2,1)} %bitcast.16), channel_id=1, source_target_pairs={{0,4},{4,0},{1,5},{5,1},{2,6},{6,2},{3,7},{7,3},{8,12},{12,8},{9,1... | collective-permute-start | bytes 3563528 | tf_op jit(solution)/shard_map/ppermute | solution.py:314
  21.6 6.1 %collective-permute-start.1 = (bf16[8,2560]{1,0:T(8,128)(2,1)S(1)}, bf16[8,2560]{1,0:T(8,128)(2,1)S(1)}, u32[]{:S(2)}, u32[]{:S(2)}) collective-permute-start(bf16[8,2560]{1,0:T(8,128)(2,1)S(1)} %slice.12), channel_id=1, source_target_pairs={{4,8},{12,16},{20,24},{28,32},{36,40},{44,48},{52,56},{60,64},{68,... | collective-permute-start | bytes 122888 | tf_op jit(solution)/shard_map/ppermute | solution.py:317
  24.4 4.3 %collective-permute-start.2 = (bf16[8,2560]{1,0:T(8,128)(2,1)S(1)}, bf16[8,2560]{1,0:T(8,128)(2,1)S(1)}, u32[]{:S(2)}, u32[]{:S(2)}) collective-permute-start(bf16[8,2560]{1,0:T(8,128)(2,1)S(1)} %slice.12), channel_id=1, source_target_pairs={{4,12},{12,20},{20,28},{28,36},{36,44},{44,52},{52,60},{60,68},{68... | collective-permute-start | bytes 122888 | tf_op jit(solution)/shard_map/ppermute | solution.py:318
  28.7 1.8 %copy-start.1 = (f32[1,4,2560]{2,1,0:T(4,128)S(1)}, f32[1,4,2560]{2,1,0:T(4,128)}, u32[]{:S(2)}) copy-start(f32[1,4,2560]{2,1,0:T(4,128)} %param.8) | copy-start | bytes 122884
  28.8 1.8 %copy-start.2 = (f32[1,2560]{1,0:T(1,128)S(1)}, f32[1,2560]{1,0:T(1,128)}, u32[]{:S(2)}) copy-start(f32[1,2560]{1,0:T(1,128)} %bias.1) | copy-start | bytes 30724
  28.8 1.8 %copy-start.4 = (f32[1,32]{1,0:T(1,128)S(1)}, f32[1,32]{1,0:T(1,128)}, u32[]{:S(2)}) copy-start(f32[1,32]{1,0:T(1,128)} %step_bias.1) | copy-start | bytes 388
  28.8 1.8 %copy-start.5 = (f32[1,32]{1,0:T(1,128)S(1)}, f32[1,32]{1,0:T(1,128)}, u32[]{:S(2)}) copy-start(f32[1,32]{1,0:T(1,128)} %log_rates.1) | copy-start | bytes 388
  35.3 7.0 %collective-permute-start.3 = (bf16[272,256]{1,0:T(8,128)(2,1)S(1)}, bf16[272,256]{1,0:T(8,128)(2,1)S(1)}, u32[]{:S(2)}, u32[]{:S(2)}) collective-permute-start(bf16[272,256]{1,0:T(8,128)(2,1)S(1)} %get-tuple-element.26), channel_id=1, source_target_pairs={{0,8},{8,16},{16,24},{24,0},{1,9},{9,17},{17,25},{25,1},{2,10},{10... | collective-permute-start | bytes 417800 | tf_op jit(solution)/shard_map/ppermute | solution.py:345
  37.1 10.0 %collective-permute-start.4 = (bf16[272,256]{1,0:T(8,128)(2,1)S(1)}, bf16[272,256]{1,0:T(8,128)(2,1)S(1)}, u32[]{:S(2)}, u32[]{:S(2)}) collective-permute-start(bf16[272,256]{1,0:T(8,128)(2,1)S(1)} %get-tuple-element.27), channel_id=1, source_target_pairs={{0,16},{8,24},{16,0},{24,8},{1,17},{9,25},{17,1},{25,9},{2,18},{10... | collective-permute-start | bytes 417800 | tf_op jit(solution)/shard_map/ppermute | solution.py:345
  39.8 7.3 %collective-permute-start.5 = (bf16[272,256]{1,0:T(8,128)(2,1)S(1)}, bf16[272,256]{1,0:T(8,128)(2,1)S(1)}, u32[]{:S(2)}, u32[]{:S(2)}) collective-permute-start(bf16[272,256]{1,0:T(8,128)(2,1)S(1)} %get-tuple-element.28), channel_id=1, source_target_pairs={{0,24},{8,0},{16,8},{24,16},{1,25},{9,1},{17,9},{25,17},{2,26},{10... | collective-permute-start | bytes 417800 | tf_op jit(solution)/shard_map/ppermute | solution.py:345
  78.9 8.8 %collective-permute-start.6 = (bf16[256,256]{1,0:T(8,128)(2,1)S(1)}, bf16[256,256]{1,0:T(8,128)(2,1)S(1)}, u32[]{:S(2)}, u32[]{:S(2)}) collective-permute-start(bf16[256,256]{1,0:T(8,128)(2,1)S(1)} %get-tuple-element.30), channel_id=1, source_target_pairs={{0,8},{8,16},{16,24},{24,0},{1,9},{9,17},{17,25},{25,1},{2,10},{10... | collective-permute-start | bytes 393224 | tf_op jit(solution)/shard_map/ppermute | solution.py:345
  80.2 13.8 %collective-permute-start.7 = (bf16[256,256]{1,0:T(8,128)(2,1)S(1)}, bf16[256,256]{1,0:T(8,128)(2,1)S(1)}, u32[]{:S(2)}, u32[]{:S(2)}) collective-permute-start(bf16[256,256]{1,0:T(8,128)(2,1)S(1)} %get-tuple-element.31), channel_id=1, source_target_pairs={{0,16},{8,24},{16,0},{24,8},{1,17},{9,25},{17,1},{25,9},{2,18},{10... | collective-permute-start | bytes 393224 | tf_op jit(solution)/shard_map/ppermute | solution.py:345
  82.5 11.5 %collective-permute-start.8 = (bf16[256,256]{1,0:T(8,128)(2,1)S(1)}, bf16[256,256]{1,0:T(8,128)(2,1)S(1)}, u32[]{:S(2)}, u32[]{:S(2)}) collective-permute-start(bf16[256,256]{1,0:T(8,128)(2,1)S(1)} %get-tuple-element.32), channel_id=1, source_target_pairs={{0,24},{8,0},{16,8},{24,16},{1,25},{9,1},{17,9},{25,17},{2,26},{10... | collective-permute-start | bytes 393224 | tf_op jit(solution)/shard_map/ppermute | solution.py:345
  94.0 6.1 %copy-start.3 = (f32[1,2048]{1,0:T(1,128)S(1)}, f32[1,2048]{1,0:T(1,128)}, u32[]{:S(2)}) copy-start(f32[1,2048]{1,0:T(1,128)} %gain.1) | copy-start | bytes 24580
  95.6 4.5 %collective-permute-start.9 = (bf16[128,1024]{1,0:T(8,128)(2,1)S(1)}, bf16[128,1024]{1,0:T(8,128)(2,1)S(1)}, u32[]{:S(2)}, u32[]{:S(2)}) collective-permute-start(bf16[128,1024]{1,0:T(8,128)(2,1)S(1)} %get-tuple-element.34), channel_id=1, source_target_pairs={{0,4},{4,0},{1,5},{5,1},{2,6},{6,2},{3,7},{7,3},{8,12},{12,8},{9,1... | collective-permute-start | bytes 786440 | tf_op jit(solution)/shard_map/ppermute | solution.py:409
  101.7 15.1 %collective-permute-start.10 = (bf16[128,2048]{1,0:T(8,128)(2,1)S(1)}, bf16[128,2048]{1,0:T(8,128)(2,1)S(1)}, u32[]{:S(2)}, u32[]{:S(2)}) collective-permute-start(bf16[128,2048]{1,0:T(8,128)(2,1)S(1)} %norm.1.own), channel_id=1, source_target_pairs={{0,1},{1,2},{2,3},{3,0},{4,5},{5,6},{6,7},{7,4},{8,9},{9,10},{10,1... | collective-permute-start | bytes 1572872 | tf_op jit(solution)/shard_map/ppermute | solution.py:411
  102.8 14.1 %collective-permute-start.12 = (bf16[128,2048]{1,0:T(8,128)(2,1)S(1)}, bf16[128,2048]{1,0:T(8,128)(2,1)S(1)}, u32[]{:S(2)}, u32[]{:S(2)}) collective-permute-start(bf16[128,2048]{1,0:T(8,128)(2,1)S(1)} %norm.1.own), channel_id=1, source_target_pairs={{0,3},{1,0},{2,1},{3,2},{4,7},{5,4},{6,5},{7,6},{8,11},{9,8},{10,9... | collective-permute-start | bytes 1572872 | tf_op jit(solution)/shard_map/ppermute | solution.py:412
  116.8 8.4 %collective-permute-start.11 = (bf16[64,2048]{1,0:T(8,128)(2,1)S(1)}, bf16[64,2048]{1,0:T(8,128)(2,1)S(1)}, u32[]{:S(2)}, u32[]{:S(2)}) collective-permute-start(bf16[64,2048]{1,0:T(8,128)(2,1)S(1)} %slice.13), channel_id=1, source_target_pairs={{0,1},{1,2},{2,3},{3,0},{4,5},{5,6},{6,7},{7,4},{8,9},{9,10},{10,1... | collective-permute-start | bytes 786440 | tf_op jit(solution)/shard_map/ppermute | solution.py:413
  117.0 8.3 %collective-permute-start.13 = (bf16[64,2048]{1,0:T(8,128)(2,1)S(1)}, bf16[64,2048]{1,0:T(8,128)(2,1)S(1)}, u32[]{:S(2)}, u32[]{:S(2)}) collective-permute-start(bf16[64,2048]{1,0:T(8,128)(2,1)S(1)} %slice.14), channel_id=1, source_target_pairs={{0,3},{1,0},{2,1},{3,2},{4,7},{5,4},{6,5},{7,6},{8,11},{9,8},{10,9... | collective-permute-start | bytes 786440 | tf_op jit(solution)/shard_map/ppermute | solution.py:414
Sparse Core Ops, SparseCore 0:
  17.5 111.3 all-gather.1
